TPU v7x, 1024 devices: a whole 8x8x8 slice. The times are simulated.
1024 devices in a mesh: gx: 32 (over z, x_lo), gy: 4 (over x_hi, core), gz: 8 (over y).
Axes of the slice: x: 8 (x_hi: 2, x_lo: 4; x = x_hi * 4 + x_lo), y: 8, z: 8, core: 2. Of those that a mesh axis runs over, the one named last changes fastest.
Arguments:
- coefficients: bfloat16 [8, 256, 32, 64, 256], P(None, 'gx', 'gy', 'gz'), may hold values from -6 to 6
- fun_count: int32 [32, 4, 8], P('gx', 'gy', 'gz'), may hold values from 64 to 256, as said below
- tile_offset: int32 [32, 4, 8], P('gx', 'gy', 'gz'), may hold values from -1 to 1
- kernel: bfloat16 [32, 256, 256], P('gx'), may hold values from -0.0234375 to 0.0234375
Outputs:
- density: float32 [32, 4, 8, 4096], P('gx', 'gy', 'gz')
Inputs may be any that keep to these rules, and one draw needn't show every extreme that they name: `fun_count`: the slots below a domain's count hold its support functions; the other slots are empty. Some domain has all 256 slots live. `tile_offset`: the kernel tile of a domain is held by the first domain index that differs from its own by the offset, cyclically.
All inputs are finite; a program needn't handle non-finite values.
Results may differ from a plain program's by a relative error of at most 0.007.
Values may be sent and summed in bfloat16 or wider, within the bound.
No kernel may reach another device: no remote copies, remote signals or barrier semaphores. Data moves between devices by JAX's collectives and lax.ppermute only.
A program may use at most 32 MiB of HBM per device.

v0:
```python
import jax
import jax.numpy as jnp
from jax import lax
from jax.sharding import PartitionSpec as P

FILT = [0.48296291314453416, 0.8365163037378079, 0.2241438680420134, -0.12940952255126037]
WAVE = [(1.0 if t % 2 == 0 else -1.0) * FILT[3 - t] for t in range(4)]


def with_halo(shard, sides, width):
    for axis, dim in sides:
        count, length = (lax.axis_size(axis), shard.shape[dim])
        up = [(i, (i + 1) % count) for i in range(count - 1)]
        down = [(j, i) for i, j in up]
        last = lax.slice_in_dim(shard, length - width, length, axis=dim)
        initial = lax.slice_in_dim(shard, 0, width, axis=dim)
        before = lax.ppermute(last, axis, up)
        after = lax.ppermute(initial, axis, down)
        shard = jnp.concatenate([before, shard, after], axis=dim)
    return shard


def passed_along(value, axis, steps):
    count = lax.axis_size(axis)
    pairs = [(source, (source + steps) % count) for source in range(count)]
    return lax.ppermute(value, axis, pairs)


def band_table(coarse):
    fine_idx = jnp.arange(2 * coarse, dtype=jnp.int32)[:, None]
    coarse_idx = jnp.arange(coarse + 2, dtype=jnp.int32)[None, :]
    offset = fine_idx - 2 * coarse_idx + 3
    low = jnp.zeros(offset.shape, jnp.float32)
    high = jnp.zeros(offset.shape, jnp.float32)
    for tap in range(4):
        low = low + jnp.where(offset == tap, FILT[tap], 0.0).astype(jnp.float32)
        high = high + jnp.where(offset == tap, WAVE[tap], 0.0).astype(jnp.float32)
    return jnp.stack([low, high])


def body(coefficients, fun_count, tile_offset, kernel):
    high = lax.Precision.HIGHEST
    slots_all = coefficients.shape[4]
    coarse_x = coefficients.shape[1]
    coarse_y = coefficients.shape[2]
    coarse_z = coefficients.shape[3]
    live_count = fun_count.reshape(())
    slots = jnp.arange(slots_all, dtype=jnp.int32)
    live = jnp.where(
        (slots < live_count)[None, None, None, None, :], coefficients, jnp.zeros((), jnp.bfloat16)
    )
    extended = with_halo(live, (("gx", 1),), 1)
    data = extended.astype(jnp.float32)
    data = data.reshape((2, 4) + data.shape[1:])
    after_x = jnp.einsum("cnk,cpkyzf->pnyzf", band_table(coarse_x), data, precision=high).astype(
        jnp.bfloat16
    )
    table_y = band_table(coarse_y)
    table_z = band_table(coarse_z)
    extended = with_halo(after_x, (("gy", 2),), 1)
    data = extended.astype(jnp.float32)
    data = data.reshape((2, 2) + data.shape[1:])
    after_y = jnp.einsum("cnk,cpxkzf->pxnzf", table_y, data, precision=high).astype(jnp.bfloat16)
    extended = with_halo(after_y, (("gz", 3),), 1)
    data = extended.astype(jnp.float32)
    phi = jnp.einsum("cnk,cxykf->xynf", table_z, data, precision=high).astype(jnp.bfloat16)
    phi = phi.reshape(-1, slots_all)
    offset = tile_offset.reshape(())
    received = []
    for step_by in (1, -1):
        received.append(passed_along(kernel, "gx", step_by))
    tile = jnp.where(
        offset == -1, received[0][0], jnp.where(offset == 1, received[1][0], kernel[0])
    )
    psi = jnp.dot(phi, tile, preferred_element_type=jnp.float32)
    density = jnp.sum(phi.astype(jnp.float32) * psi, axis=1)
    return density.reshape(1, 1, 1, -1)


def solution(mesh):
    placed = (
        P(None, "gx", "gy", "gz", None),
        P("gx", "gy", "gz"),
        P("gx", "gy", "gz"),
        P("gx", None, None),
    )
    return jax.shard_map(
        body, mesh=mesh, in_specs=placed, out_specs=P("gx", "gy", "gz", None), check_vma=False
    )
```

profile of v0, /device:TPU:65, one launch (start us, length us, event | category | flops | bytes accessed | tf_op | source)
XLA Modules:
  0.0 81.6 jit_solution(10356591769268226703)
XLA Ops:
  0.7 1.7 %broadcast_select_fusion = bf16[8,8,8,8,256]{4,3,2,1,0:T(8,128)(2,1)S(1)} fusion(bf16[8,8,8,8,256]{4,3,2,1,0:T(8,128)(2,1)} %param.4, pred[256]{0:T(512)(128)(4,1)S(1)} %iota_compare_fusion), kind=kLoop, calls=%fused_computation.15 | loop fusion | flops 1048576 | bytes 4194560 | tf_op jit(solution)/shard_map/jit(_where)/select_n | solution.py:49
  2.5 3.1 %collective-permute-start = (bf16[8,1,8,8,256]{4,3,2,1,0:T(8,128)(2,1)S(1)}, bf16[8,1,8,8,256]{4,3,2,1,0:T(8,128)(2,1)S(1)}, u32[]{:S(2)}, u32[]{:S(2)}) collective-permute-start(bf16[8,1,8,8,256]{4,3,2,1,0:T(8,128)(2,1)S(1)} %get-tuple-element.9), channel_id=1, source_target_pairs={{0,32},{32,64},{64,96},{96,128},{128,160},{160,192},{192,224},{224... | collective-permute-start | bytes 786440 | tf_op jit(solution)/shard_map/ppermute | solution.py:17
  5.6 1.3 %collective-permute-start.1 = (bf16[8,1,8,8,256]{4,3,2,1,0:T(8,128)(2,1)S(1)}, bf16[8,1,8,8,256]{4,3,2,1,0:T(8,128)(2,1)S(1)}, u32[]{:S(2)}, u32[]{:S(2)}) collective-permute-start(bf16[8,1,8,8,256]{4,3,2,1,0:T(8,128)(2,1)S(1)} %get-tuple-element.10), channel_id=1, source_target_pairs={{32,0},{64,32},{96,64},{128,96},{160,128},{192,160},{224,192},{256... | collective-permute-start | bytes 786440 | tf_op jit(solution)/shard_map/ppermute | solution.py:18
  6.9 3.6 %collective-permute-done = bf16[8,1,8,8,256]{4,3,2,1,0:T(8,128)(2,1)S(1)} collective-permute-done((bf16[8,1,8,8,256]{4,3,2,1,0:T(8,128)(2,1)S(1)}, bf16[8,1,8,8,256]{4,3,2,1,0:T(8,128)(2,1)S(1)}, u32[]{:S(2)}, u32[]{:S(2)}) %collective-permute-start) | collective-permute-done | bytes 262176 | tf_op jit(solution)/shard_map/ppermute | solution.py:17
  10.5 9.5 %collective-permute-done.1 = bf16[8,1,8,8,256]{4,3,2,1,0:T(8,128)(2,1)S(1)} collective-permute-done((bf16[8,1,8,8,256]{4,3,2,1,0:T(8,128)(2,1)S(1)}, bf16[8,1,8,8,256]{4,3,2,1,0:T(8,128)(2,1)S(1)}, u32[]{:S(2)}, u32[]{:S(2)}) %collective-permute-start.1) | collective-permute-done | bytes 262176 | tf_op jit(solution)/shard_map/ppermute | solution.py:18
  20.0 0.3 pad_maximum_fusion
  20.3 3.6 %fusion.6 = bf16[4,16,8,8,256]{4,1,3,2,0:T(8,128)(2,1)S(1)} fusion(bf16[2,4,10,8,8,256]{5,4,3,2,1,0:T(8,128)(2,1)S(1)} %bitcast.43, f32[1,16,10]{2,1,0:T(8,128)S(1)} %get-tuple-element.12, f32[1,16,10]{2,1,0:T(8,128)S(1)} %get-tuple-element.11), kind=kOutput, calls=%fused_computation.13 | convolution fusion | flops 252707136 | bytes 4719872 | tf_op jit(solution)/shard_map/cnk,cpkyzf->pnyzf/dot_general | solution.py:55
  24.0 7.9 %collective-permute-start.2 = (bf16[4,16,1,8,256]{4,1,3,2,0:T(8,128)(2,1)S(1)}, bf16[4,16,1,8,256]{4,1,3,2,0:T(8,128)(2,1)S(1)}, u32[]{:S(2)}, u32[]{:S(2)}) collective-permute-start(bf16[4,16,1,8,256]{4,1,3,2,0:T(8,128)(2,1)S(1)} %get-tuple-element.7), channel_id=1, source_target_pairs={{0,8},{8,16},{16,24},{1,9},{9,17},{17,25},{2,10},{10,18},{18,26},{... | collective-permute-start | bytes 786440 | tf_op jit(solution)/shard_map/ppermute | solution.py:17
  31.9 1.9 %collective-permute-start.3 = (bf16[4,16,1,8,256]{4,1,3,2,0:T(8,128)(2,1)S(1)}, bf16[4,16,1,8,256]{4,1,3,2,0:T(8,128)(2,1)S(1)}, u32[]{:S(2)}, u32[]{:S(2)}) collective-permute-start(bf16[4,16,1,8,256]{4,1,3,2,0:T(8,128)(2,1)S(1)} %get-tuple-element.8), channel_id=1, source_target_pairs={{8,0},{16,8},{24,16},{9,1},{17,9},{25,17},{10,2},{18,10},{26,18},{... | collective-permute-start | bytes 786440 | tf_op jit(solution)/shard_map/ppermute | solution.py:18
  33.8 1.4 %collective-permute-done.2 = bf16[4,16,1,8,256]{4,1,3,2,0:T(8,128)(2,1)S(1)} collective-permute-done((bf16[4,16,1,8,256]{4,1,3,2,0:T(8,128)(2,1)S(1)}, bf16[4,16,1,8,256]{4,1,3,2,0:T(8,128)(2,1)S(1)}, u32[]{:S(2)}, u32[]{:S(2)}) %collective-permute-start.2) | collective-permute-done | bytes 262176 | tf_op jit(solution)/shard_map/ppermute | solution.py:17
  35.2 11.1 %collective-permute-done.3 = bf16[4,16,1,8,256]{4,1,3,2,0:T(8,128)(2,1)S(1)} collective-permute-done((bf16[4,16,1,8,256]{4,1,3,2,0:T(8,128)(2,1)S(1)}, bf16[4,16,1,8,256]{4,1,3,2,0:T(8,128)(2,1)S(1)}, u32[]{:S(2)}, u32[]{:S(2)}) %collective-permute-start.3) | collective-permute-done | bytes 262176 | tf_op jit(solution)/shard_map/ppermute | solution.py:18
  46.3 0.3 pad_maximum_fusion.1
  46.6 0.0 copy-start
  46.6 6.5 %fusion.7 = bf16[2,16,16,8,256]{4,2,3,1,0:T(8,128)(2,1)S(1)} fusion(bf16[2,2,16,10,8,256]{5,2,4,3,1,0:T(8,128)(2,1)S(1)} %bitcast.44, f32[1,16,10]{2,1,0:T(8,128)S(1)} %get-tuple-element.12, f32[1,16,10]{2,1,0:T(8,128)S(1)} %get-tuple-element.11), kind=kOutput, calls=%fused_computation.14 | convolution fusion | flops 252707136 | bytes 4719872 | tf_op jit(solution)/shard_map/cnk,cpxkzf->pxnzf/dot_general | solution.py:63
  53.3 2.4 %collective-permute-start.4 = (bf16[2,16,16,1,256]{4,2,3,1,0:T(8,128)(2,1)S(1)}, bf16[2,16,16,1,256]{4,2,3,1,0:T(8,128)(2,1)S(1)}, u32[]{:S(2)}, u32[]{:S(2)}) collective-permute-start(bf16[2,16,16,1,256]{4,2,3,1,0:T(8,128)(2,1)S(1)} %get-tuple-element.5), channel_id=1, source_target_pairs={{0,1},{1,2},{2,3},{3,4},{4,5},{5,6},{6,7},{8,9},{9,10},{10,11},{11... | collective-permute-start | bytes 786440 | tf_op jit(solution)/shard_map/ppermute | solution.py:17
  55.7 4.1 %collective-permute-start.5 = (bf16[2,16,16,1,256]{4,2,3,1,0:T(8,128)(2,1)S(1)}, bf16[2,16,16,1,256]{4,2,3,1,0:T(8,128)(2,1)S(1)}, u32[]{:S(2)}, u32[]{:S(2)}) collective-permute-start(bf16[2,16,16,1,256]{4,2,3,1,0:T(8,128)(2,1)S(1)} %get-tuple-element.6), channel_id=1, source_target_pairs={{1,0},{2,1},{3,2},{4,3},{5,4},{6,5},{7,6},{9,8},{10,9},{11,10},{12... | collective-permute-start | bytes 786440 | tf_op jit(solution)/shard_map/ppermute | solution.py:18
  59.8 0.0 copy-done
  59.8 2.2 %collective-permute-start.6 = (bf16[1,256,256]{2,1,0:T(8,128)(2,1)S(1)}, bf16[1,256,256]{2,1,0:T(8,128)(2,1)S(1)}, u32[]{:S(2)}, u32[]{:S(2)}) collective-permute-start(bf16[1,256,256]{2,1,0:T(8,128)(2,1)S(1)} %copy-done), channel_id=1, source_target_pairs={{0,32},{32,64},{64,96},{96,128},{128,160},{160,192},{192,224},{224... | collective-permute-start | bytes 393224 | tf_op jit(solution)/shard_map/ppermute | solution.py:26
  62.0 10.2 %collective-permute-start.7 = (bf16[1,256,256]{2,1,0:T(8,128)(2,1)S(1)}, bf16[1,256,256]{2,1,0:T(8,128)(2,1)S(1)}, u32[]{:S(2)}, u32[]{:S(2)}) collective-permute-start(bf16[1,256,256]{2,1,0:T(8,128)(2,1)S(1)} %copy-done), channel_id=1, source_target_pairs={{0,992},{32,0},{64,32},{96,64},{128,96},{160,128},{192,160},{224,1... | collective-permute-start | bytes 393224 | tf_op jit(solution)/shard_map/ppermute | solution.py:26
  72.8 0.0 collective-permute-done.4
  72.8 0.0 collective-permute-done.5
  72.8 0.3 pad_maximum_fusion.2
  73.2 2.5 %bitcast_convert_fusion = bf16[16,16,256,16]{2,3,1,0:T(8,128)(2,1)S(1)} fusion(bf16[2,16,16,10,256]{4,2,3,1,0:T(8,128)(2,1)S(1)} %pad_maximum_fusion.2, f32[1,16,10]{2,1,0:T(8,128)S(1)} %get-tuple-element.12, f32[1,16,10]{2,1,0:T(8,128)S(1)} %get-tuple-element.11), kind=kOutput, calls=%fused_computation.1 | convolution fusion | flops 252707136 | bytes 4719872 | tf_op jit(solution)/shard_map/cnk,cxykf->xynf/dot_general | solution.py:66
  75.7 3.0 %copy.11 = bf16[4096,256]{0,1:T(8,128)(2,1)} copy(bf16[4096,256]{1,0:T(8,128)(2,1)S(1)} %bitcast.45) | data formatting | bytes 4194304 | tf_op jit(solution)/shard_map/reshape | solution.py:67
  78.6 0.0 collective-permute-done.6
  78.7 0.0 collective-permute-done.7
  78.7 3.0 %fusion.14 = f32[4096]{0:T(1024)} fusion(bf16[4096,256]{1,0:T(8,128)(2,1)S(1)} %bitcast.46, bf16[4096,256]{0,1:T(8,128)(2,1)} %copy.11, bf16[1,256,256]{2,1,0:T(8,128)(2,1)S(1)} %collective-permute-done.6, bf16[1,256,256]{2,1,0:T(8,128)(2,1)S(1)} %collective-permute-done.7, bf16[1,256,256]{2,1,0:T(8,128)(2,1)S(1)} %copy-done, pred[]{:T(512)} %bitcast.19, ...), kind=kOutput, calls=%fused_computation.16 | convolution fusion | flops 540143616 | bytes 4603906 | tf_op jit(solution)/shard_map/dot_general | solution.py:75
  (6 shorter events, 0.1 us)
Async XLA Ops:
  2.5 8.1 %collective-permute-start = (bf16[8,1,8,8,256]{4,3,2,1,0:T(8,128)(2,1)S(1)}, bf16[8,1,8,8,256]{4,3,2,1,0:T(8,128)(2,1)S(1)}, u32[]{:S(2)}, u32[]{:S(2)}) collective-permute-start(bf16[8,1,8,8,256]{4,3,2,1,0:T(8,128)(2,1)S(1)} %get-tuple-element.9), channel_id=1, source_target_pairs={{0,32},{32,64},{64,96},{96,128},{128,160},{160,192},{192,224},{224... | collective-permute-start | bytes 786440 | tf_op jit(solution)/shard_map/ppermute | solution.py:17
  5.6 14.4 %collective-permute-start.1 = (bf16[8,1,8,8,256]{4,3,2,1,0:T(8,128)(2,1)S(1)}, bf16[8,1,8,8,256]{4,3,2,1,0:T(8,128)(2,1)S(1)}, u32[]{:S(2)}, u32[]{:S(2)}) collective-permute-start(bf16[8,1,8,8,256]{4,3,2,1,0:T(8,128)(2,1)S(1)} %get-tuple-element.10), channel_id=1, source_target_pairs={{32,0},{64,32},{96,64},{128,96},{160,128},{192,160},{224,192},{256... | collective-permute-start | bytes 786440 | tf_op jit(solution)/shard_map/ppermute | solution.py:18
  24.0 11.2 %collective-permute-start.2 = (bf16[4,16,1,8,256]{4,1,3,2,0:T(8,128)(2,1)S(1)}, bf16[4,16,1,8,256]{4,1,3,2,0:T(8,128)(2,1)S(1)}, u32[]{:S(2)}, u32[]{:S(2)}) collective-permute-start(bf16[4,16,1,8,256]{4,1,3,2,0:T(8,128)(2,1)S(1)} %get-tuple-element.7), channel_id=1, source_target_pairs={{0,8},{8,16},{16,24},{1,9},{9,17},{17,25},{2,10},{10,18},{18,26},{... | collective-permute-start | bytes 786440 | tf_op jit(solution)/shard_map/ppermute | solution.py:17
  31.9 14.4 %collective-permute-start.3 = (bf16[4,16,1,8,256]{4,1,3,2,0:T(8,128)(2,1)S(1)}, bf16[4,16,1,8,256]{4,1,3,2,0:T(8,128)(2,1)S(1)}, u32[]{:S(2)}, u32[]{:S(2)}) collective-permute-start(bf16[4,16,1,8,256]{4,1,3,2,0:T(8,128)(2,1)S(1)} %get-tuple-element.8), channel_id=1, source_target_pairs={{8,0},{16,8},{24,16},{9,1},{17,9},{25,17},{10,2},{18,10},{26,18},{... | collective-permute-start | bytes 786440 | tf_op jit(solution)/shard_map/ppermute | solution.py:18
  46.6 13.1 %copy-start = (bf16[1,256,256]{2,1,0:T(8,128)(2,1)S(1)}, bf16[1,256,256]{2,1,0:T(8,128)(2,1)}, u32[]{:S(2)}) copy-start(bf16[1,256,256]{2,1,0:T(8,128)(2,1)} %param.7) | copy-start | bytes 393220
  53.3 19.6 %collective-permute-start.4 = (bf16[2,16,16,1,256]{4,2,3,1,0:T(8,128)(2,1)S(1)}, bf16[2,16,16,1,256]{4,2,3,1,0:T(8,128)(2,1)S(1)}, u32[]{:S(2)}, u32[]{:S(2)}) collective-permute-start(bf16[2,16,16,1,256]{4,2,3,1,0:T(8,128)(2,1)S(1)} %get-tuple-element.5), channel_id=1, source_target_pairs={{0,1},{1,2},{2,3},{3,4},{4,5},{5,6},{6,7},{8,9},{9,10},{10,11},{11... | collective-permute-start | bytes 786440 | tf_op jit(solution)/shard_map/ppermute | solution.py:17
  55.7 17.1 %collective-permute-start.5 = (bf16[2,16,16,1,256]{4,2,3,1,0:T(8,128)(2,1)S(1)}, bf16[2,16,16,1,256]{4,2,3,1,0:T(8,128)(2,1)S(1)}, u32[]{:S(2)}, u32[]{:S(2)}) collective-permute-start(bf16[2,16,16,1,256]{4,2,3,1,0:T(8,128)(2,1)S(1)} %get-tuple-element.6), channel_id=1, source_target_pairs={{1,0},{2,1},{3,2},{4,3},{5,4},{6,5},{7,6},{9,8},{10,9},{11,10},{12... | collective-permute-start | bytes 786440 | tf_op jit(solution)/shard_map/ppermute | solution.py:18
  59.8 18.9 %collective-permute-start.6 = (bf16[1,256,256]{2,1,0:T(8,128)(2,1)S(1)}, bf16[1,256,256]{2,1,0:T(8,128)(2,1)S(1)}, u32[]{:S(2)}, u32[]{:S(2)}) collective-permute-start(bf16[1,256,256]{2,1,0:T(8,128)(2,1)S(1)} %copy-done), channel_id=1, source_target_pairs={{0,32},{32,64},{64,96},{96,128},{128,160},{160,192},{192,224},{224... | collective-permute-start | bytes 393224 | tf_op jit(solution)/shard_map/ppermute | solution.py:26
  62.0 16.7 %collective-permute-start.7 = (bf16[1,256,256]{2,1,0:T(8,128)(2,1)S(1)}, bf16[1,256,256]{2,1,0:T(8,128)(2,1)S(1)}, u32[]{:S(2)}, u32[]{:S(2)}) collective-permute-start(bf16[1,256,256]{2,1,0:T(8,128)(2,1)S(1)} %copy-done), channel_id=1, source_target_pairs={{0,992},{32,0},{64,32},{96,64},{128,96},{160,128},{192,160},{224,1... | collective-permute-start | bytes 393224 | tf_op jit(solution)/shard_map/ppermute | solution.py:26
where the time goes:
time: 82 us; the launch traced here: 81.6 us
  starting transfers between devices  33.1 us (40%)
  waiting for transfers between devices  25.6 us (31%)
  matrix products  15.6 us (19%)
  local copies, waits for them, and re-layouts  3.09 us (4%)
  other arithmetic  2.72 us (3%)
  between operations  1.49 us (2%)
    ppermute x3, waiting for transfers between devices, with_halo(): after = lax.ppermute(initial, axis, down)  20.6 us
    ppermute x3, starting transfers between devices, with_halo(): before = lax.ppermute(last, axis, up)  13.5 us
    ppermute x2, starting transfers between devices, passed_along(): return lax.ppermute(value, axis, pairs)  12.4 us
    ppermute x3, starting transfers between devices, with_halo(): after = lax.ppermute(initial, axis, down)  7.29 us
    dot_general x1, matrix products, body(): jnp.einsum('cnk,cpxkzf->pxnzf', table_y, data, precision=high)  6.55 us
    ppermute x3, waiting for transfers between devices, with_halo(): before = lax.ppermute(last, axis, up)  5 us
    dot_general x1, matrix products, body(): jnp.einsum('cnk,cpkyzf->pnyzf', band_table(coarse_x), data, precision=high)  3.59 us
    dot_general x1, matrix products, body(): psi = jnp.dot(phi, tile, preferred_element_type=jnp.float32)  2.97 us
  transfers between devices with their start and end apart: 8, of which 4 were waited for; matrix products, arithmetic and copies ran while one was open for 7% of the time, Pallas kernels for 0%

commit v1 on v0

v1 whole, which is shorter than its diff:
```python
import functools

import jax
import jax.numpy as jnp
import ml_dtypes
import numpy as np
from jax import lax
from jax.experimental import pallas as pl
from jax.experimental.pallas import tpu as pltpu
from jax.sharding import PartitionSpec as P

FILT = [0.48296291314453416, 0.8365163037378079, 0.2241438680420134, -0.12940952255126037]
WAVE = [(1.0 if t % 2 == 0 else -1.0) * FILT[3 - t] for t in range(4)]
AXES = ("gx", "gy", "gz")
F32, BF16 = jnp.float32, jnp.bfloat16


def band_table(coarse):
    table = np.zeros((2, 2 * coarse, coarse))
    for fine in range(2 * coarse):
        for point in range(coarse):
            tap = fine - 2 * point + 1
            if 0 <= tap <= 3:
                table[0, fine, point] = FILT[tap]
                table[1, fine, point] = WAVE[tap]
    return table


def make_tables(cy, cz):
    ty, tz = band_table(cy), band_table(cz)
    fy, fz = 2 * cy, 2 * cz
    inner = np.einsum("cnk,dml->nmcdkl", ty, tz).reshape(fy * fz, 4 * cy * cz)
    ends = {}
    for name, plane, tap in (("first", 0, 0), ("last", cz - 1, 3)):
        pick = np.zeros((2, cz))
        pick[0, plane], pick[1, plane] = FILT[tap], WAVE[tap]
        own = np.einsum("cnk,dl->ncdkl", ty, pick).reshape(fy, 4 * cy * cz)
        before = np.zeros((fy, 2 * cz))
        before[0] = pick.reshape(-1)
        after = np.zeros((fy, 2 * cz))
        after[fy - 1] = pick.reshape(-1)
        ends[name] = (own, before, after)
    halo_y = {}
    for name, row in (("before", 0), ("after", fy - 1)):
        block = np.zeros((fy, fz, 2 * cz))
        block[row] = np.transpose(tz, (1, 0, 2)).reshape(fz, 2 * cz)
        halo_y[name] = block.reshape(fy * fz, 2 * cz)
    halo_z = {}
    for name, column in (("before", 0), ("after", fz - 1)):
        block = np.zeros((fy, fz, fy))
        for row in range(fy):
            block[row, column, row] = 1.0
        halo_z[name] = block.reshape(fy * fz, fy)
    text, mzh, th = [], [], []
    for pz in range(2):
        order = ("last", "first") if pz == 0 else ("first", "last")
        text.append(np.concatenate([inner] + [ends[o][0] for o in order]))
    for py in range(2):
        for pz in range(2):
            order = ("last", "first") if pz == 0 else ("first", "last")
            sides_y = ("after", "before") if py == 0 else ("before", "after")
            sides_z = ("after", "before") if pz == 0 else ("before", "after")
            which = {"before": 1, "after": 2}
            mzh.append(np.concatenate([np.concatenate([ends[o][which[s]] for s in sides_y], axis=1) for o in order]))
            th.append(np.concatenate([halo_y[s] for s in sides_y] + [halo_z[s] for s in sides_z], axis=1))
    cast = lambda parts: np.stack(parts).astype(np.float32).astype(ml_dtypes.bfloat16)
    return cast(text), cast(mzh), cast(th)


def swap_pairs(shape, axis, near):
    out = []
    for place in np.ndindex(*shape):
        other = list(place)
        other[axis] = place[axis] ^ 1 if near else ((place[axis] - 1) ^ 1) + 1
        if 0 <= other[axis] < shape[axis]:
            out.append((int(np.ravel_multi_index(place, shape)), int(np.ravel_multi_index(other, shape))))
    return out


def tile_pairs(shape):
    nx, ny, nz = shape
    index = lambda x, y, z: int(np.ravel_multi_index((x % nx, y, z), shape))
    out = []
    for x, y, z in np.ndindex(*shape):
        step = 1 if y % 2 == 0 else -1
        if x == 0 and ny == 4:
            continue
        out.append((index(x, y, z), index(x + step, y, z)))
    if ny == 4:
        for z in range(nz):
            out.append((index(0, 0, z), index(1, 0, z)))
            out.append((index(0, 1, z), index(1, 2, z)))
        senders = [index(0, y, z) for z in range(nz) for y in (3, 2)]
        takers = [index(nx - 1, y, z) for z in range(nz) for y in (1, 3)]
        out += list(zip(senders, takers))
    return out


def parity(axis):
    return lax.rem(lax.axis_index(axis), 2)


def lane_mask(count_ref, rows, lanes):
    return lax.broadcasted_iota(jnp.int32, (rows, lanes), 1) < count_ref[0]


def faces_kernel(count_ref, c_ref, near_ref, far_ref):
    last_k, rows = c_ref.shape[1] - 1, c_ref.shape[2]
    even = parity("gx") == 0
    mask = lane_mask(count_ref, rows, c_ref.shape[3])
    for b in range(4):
        first = FILT[0] * c_ref[b, 0].astype(F32) + WAVE[0] * c_ref[4 + b, 0].astype(F32)
        last = FILT[3] * c_ref[b, last_k].astype(F32) + WAVE[3] * c_ref[4 + b, last_k].astype(F32)
        first, last = jnp.where(mask, first, 0.0), jnp.where(mask, last, 0.0)
        near_ref[b * rows : (b + 1) * rows] = jnp.where(even, last, first).astype(BF16)
        far_ref[b * rows : (b + 1) * rows] = jnp.where(even, first, last).astype(BF16)


def inner_kernel(count_ref, c_ref, text_ref, x_ref, p_ref, z_ref):
    rows = c_ref.shape[2]
    mask = lane_mask(count_ref, rows, c_ref.shape[3])
    pz = parity("gz")
    cells = p_ref.shape[1]
    for m in range(1, c_ref.shape[1]):
        odd, even = [], []
        for b in range(4):
            s0, w0 = c_ref[b, m - 1].astype(F32), c_ref[4 + b, m - 1].astype(F32)
            s1, w1 = c_ref[b, m].astype(F32), c_ref[4 + b, m].astype(F32)
            o = FILT[2] * s0 + WAVE[2] * w0 + FILT[0] * s1 + WAVE[0] * w1
            e = FILT[3] * s0 + WAVE[3] * w0 + FILT[1] * s1 + WAVE[1] * w1
            odd.append(jnp.where(mask, o, 0.0).astype(BF16))
            even.append(jnp.where(mask, e, 0.0).astype(BF16))
        for i, parts in ((2 * m - 2, odd), (2 * m - 1, even)):
            x = jnp.concatenate(parts, axis=0)
            x_ref[i] = x
            r = jnp.dot(text_ref[pz], x, preferred_element_type=F32)
            p_ref[i] = r[:cells]
            z_ref[i] = r[cells:]


def edge_kernel(count_ref, c_ref, near_ref, far_ref, x_ref, edge_ref, ynear_ref, yfar_ref, *, cy, cz):
    last_k, rows = c_ref.shape[1] - 1, c_ref.shape[2]
    mask = lane_mask(count_ref, rows, c_ref.shape[3])
    even = parity("gx") == 0
    for b in range(4):
        near, far = near_ref[b * rows : (b + 1) * rows].astype(F32), far_ref[b * rows : (b + 1) * rows].astype(F32)
        before, after = jnp.where(even, far, near), jnp.where(even, near, far)
        s0, w0 = c_ref[b, 0].astype(F32), c_ref[4 + b, 0].astype(F32)
        s1, w1 = c_ref[b, last_k].astype(F32), c_ref[4 + b, last_k].astype(F32)
        lo = jnp.where(mask, FILT[1] * s0 + WAVE[1] * w0, 0.0) + before
        hi = jnp.where(mask, FILT[2] * s1 + WAVE[2] * w1, 0.0) + after
        edge_ref[0, b * rows : (b + 1) * rows] = lo.astype(BF16)
        edge_ref[1, b * rows : (b + 1) * rows] = hi.astype(BF16)
    even_y = parity("gy") == 0
    fine = x_ref.shape[0] + 2
    for n in range(fine):
        ref, i = (edge_ref, 0) if n == 0 else (edge_ref, 1) if n == fine - 1 else (x_ref, n - 1)
        near_rows, far_rows = [], []
        for zb in range(2):
            low, high = zb * rows, (2 + zb) * rows
            end = (cy - 1) * cz
            first = FILT[0] * ref[i, low : low + cz].astype(F32) + WAVE[0] * ref[i, high : high + cz].astype(F32)
            last = FILT[3] * ref[i, low + end : low + end + cz].astype(F32) + WAVE[3] * ref[i, high + end : high + end + cz].astype(F32)
            near_rows.append(jnp.where(even_y, last, first))
            far_rows.append(jnp.where(even_y, first, last))
        ynear_ref[n * 2 * cz : (n + 1) * 2 * cz] = jnp.concatenate(near_rows, axis=0).astype(BF16)
        yfar_ref[n * 2 * cz : (n + 1) * 2 * cz] = jnp.concatenate(far_rows, axis=0).astype(BF16)


def edge_cells_kernel(edge_ref, text_ref, p_ref, z_ref):
    pz = parity("gz")
    cells = p_ref.shape[1]
    for i in range(2):
        r = jnp.dot(text_ref[pz], edge_ref[i], preferred_element_type=F32)
        p_ref[i] = r[:cells]
        z_ref[i] = r[cells:]


def zfaces_kernel(ynear_ref, yfar_ref, z_ref, ze_ref, mzh_ref, near_ref, far_ref):
    case = 2 * parity("gy") + parity("gz")
    fine = z_ref.shape[0] + 2
    step = ynear_ref.shape[0] // fine
    half = z_ref.shape[1] // 2
    for n in range(fine):
        own = ze_ref[0] if n == 0 else ze_ref[1] if n == fine - 1 else z_ref[n - 1]
        rows = slice(n * step, (n + 1) * step)
        halo = jnp.concatenate([ynear_ref[rows], yfar_ref[rows]], axis=0)
        r = own + jnp.dot(mzh_ref[case], halo, preferred_element_type=F32)
        near_ref[n * half : (n + 1) * half] = r[:half].astype(BF16)
        far_ref[n * half : (n + 1) * half] = r[half:].astype(BF16)


def density_kernel(offset_ref, own_ref, tile1_ref, tile2_ref, p_ref, pe_ref, th_ref, *rest):
    halos, out_ref, k_ref = rest[:4], rest[4], rest[5]
    case = 2 * parity("gy") + parity("gz")
    even = parity("gy") == 0
    offset = offset_ref[0]
    first, second = tile1_ref[...], tile2_ref[...]
    before, after = jnp.where(even, first, second), jnp.where(even, second, first)
    k_ref[...] = jnp.where(offset == -1, before, jnp.where(offset == 1, after, own_ref[...]))
    fine = p_ref.shape[0] + 2
    lanes = k_ref.shape[1] // 2
    ones = jnp.ones((8, lanes), BF16)
    step = halos[0].shape[0] // fine
    for n in range(fine):
        own = pe_ref[0] if n == 0 else pe_ref[1] if n == fine - 1 else p_ref[n - 1]
        rows = slice(n * step, (n + 1) * step)
        halo = jnp.concatenate([h[rows] for h in halos], axis=0)
        phi = (own + jnp.dot(th_ref[case], halo, preferred_element_type=F32)).astype(BF16)
        psi = jnp.dot(phi, k_ref[...], preferred_element_type=F32)
        prod = phi.astype(F32) * psi
        prod = prod[:, :lanes] + prod[:, lanes:]
        high = prod.astype(BF16)
        low = (prod - high.astype(F32)).astype(BF16)
        dims = (((1,), (1,)), ((), ()))
        sums = lax.dot_general(ones, high, dims, preferred_element_type=F32)
        sums = sums + lax.dot_general(ones, low, dims, preferred_element_type=F32)
        cells = sums.shape[1]
        for j in range(cells // 128):
            row = n * (cells // 128) + j
            out_ref[row : row + 1] = sums[0:1, j * 128 : (j + 1) * 128]


def call(body, name, outs, args, scalars=0, scratch=(), flops=1e6, in_hbm=()):
    specs = [pl.BlockSpec(memory_space=pltpu.SMEM if i < scalars else pltpu.VMEM) for i in range(len(args))]
    args = [a if i < scalars else pltpu.with_memory_space_constraint(a, pltpu.VMEM) for i, a in enumerate(args)]
    size = sum(int(np.prod(o.shape)) * o.dtype.itemsize for o in outs)
    return pl.pallas_call(
        body,
        out_shape=tuple(outs),
        in_specs=specs,
        out_specs=tuple(pl.BlockSpec(memory_space=pltpu.VMEM) for _ in outs),
        scratch_shapes=list(scratch),
        name=name,
        compiler_params=pltpu.CompilerParams(vmem_limit_bytes=16 << 20),
        cost_estimate=pl.CostEstimate(flops=int(flops), bytes_accessed=size, transcendentals=0),
    )(*args)


def body(coefficients, fun_count, tile_offset, kernel, *, shape):
    bands, cx, cy, cz, slots = coefficients.shape
    text, mzh, th = make_tables(cy, cz)
    rows, cells, fx = cy * cz, 4 * cy * cz, 2 * cx
    near = [swap_pairs(shape, axis, True) for axis in range(3)]
    far = [swap_pairs(shape, axis, False) for axis in range(3)]
    send = lambda value, pairs: lax.ppermute(value, AXES, pairs)
    vmem = lambda shape, dtype: pltpu.VMEM(shape, dtype)
    count = fun_count.reshape(1)
    c = coefficients.reshape(bands, cx, rows, slots)
    face = vmem((4 * rows, slots), BF16)

    xnear, xfar = call(faces_kernel, "x_faces", [face] * 2, [count, c], 1)
    xnear, xfar = send(xnear, near[0]), send(xfar, far[0])
    own = kernel.reshape(kernel.shape[1:])
    tile1 = send(own, tile_pairs(shape))
    x, p, z = call(
        inner_kernel, "inner_cells",
        [vmem((fx - 2, 4 * rows, slots), BF16), vmem((fx - 2, cells, slots), F32), vmem((fx - 2, 4 * cy, slots), F32)],
        [count, c, text], 1, flops=2e9,
    )
    yshape = vmem((fx * 2 * cz, slots), BF16)
    edge, ynear, yfar = call(
        functools.partial(edge_kernel, cy=cy, cz=cz), "x_edges_y_faces",
        [vmem((2, 4 * rows, slots), BF16), yshape, yshape], [count, c, xnear, xfar, x], 1,
    )
    yfar, ynear = send(yfar, far[1]), send(ynear, near[1])
    tile2 = send(tile1, near[1])
    pe, ze = call(
        edge_cells_kernel, "edge_cells", [vmem((2, cells, slots), F32), vmem((2, 4 * cy, slots), F32)], [edge, text], flops=3e8
    )
    zshape = vmem((fx * 2 * cy, slots), BF16)
    znear, zfar = call(zfaces_kernel, "z_faces", [zshape, zshape], [ynear, yfar, z, ze, mzh])
    znear, zfar = send(znear, near[2]), send(zfar, far[2])
    (out,) = call(
        density_kernel, "density", [jax.ShapeDtypeStruct((fx * cells // 128, 128), F32)],
        [tile_offset.reshape(1), own, tile1, tile2, p, pe, th, ynear, yfar, znear, zfar], 1,
        scratch=[pltpu.VMEM((slots, slots), BF16)],
    )
    return out.reshape(1, 1, 1, -1)


def solution(mesh):
    placed = (
        P(None, "gx", "gy", "gz", None),
        P("gx", "gy", "gz"),
        P("gx", "gy", "gz"),
        P("gx", None, None),
    )
    shape = tuple(mesh.shape[a] for a in AXES)
    return jax.shard_map(
        functools.partial(body, shape=shape), mesh=mesh, in_specs=placed, out_specs=P("gx", "gy", "gz", None), check_vma=False
    )
```

time: 82 us -> 53.7 us (0.65)
  waiting for transfers between devices: 25.6 us -> 5.69 us
  matrix products: 15.6 us -> 0 us
  Pallas kernels: 0 us -> 7.5 us
  starting transfers between devices: 33.1 us -> 36.6 us
  other arithmetic: 2.72 us -> 0 us
  local copies, waits for them, and re-layouts: 3.09 us -> 1.61 us
    ppermute x8, waiting for transfers between devices: 25.6 us -> 5.69 us  [body(): send = lambda value, pairs: lax.ppermute(value, AXES, pairs)]
    dot_general x4 -> x0, matrix products: 15.6 us -> none  [the longest x1 6.55 us: body(): jnp.einsum('cnk,cpxkzf->pxnzf', table_y, data, precision=high)]
    pallas_call x0 -> x6, Pallas kernels: none -> 7.5 us  [call(): pl.pallas_call(body, out_shape=tuple(outs), in_specs=specs, out_specs=tup...]
    ppermute x8, starting transfers between devices: 33.1 us -> 36.6 us  [body(): send = lambda value, pairs: lax.ppermute(value, AXES, pairs)]
    reshape x1 -> x0, local copies, waits for them, and re-layouts: 2.96 us -> none  [body(): phi = phi.reshape(-1, slots_all)]
    select_n x1 -> x0, other arithmetic: 1.73 us -> none  [body(): jnp.where((slots < live_count)[None, None, None, None, :], coefficients,...]
    unnamed x2 -> x10, local copies, waits for them, and re-layouts: 0.01 us -> 1.61 us
    concatenate x3 -> x0, other arithmetic: 0.96 us -> none  [with_halo(): shard = jnp.concatenate([before, shard, after], axis=dim)]
  transfers between devices with their start and end apart: 8 -> 8, of which waited for: 4 -> 3; matrix products, arithmetic and copies ran while one was open for 7% -> 0% of each run, Pallas kernels for 0% -> 5%
where the time goes in v1:
time: 53.7 us; the launch traced here: 52.8 us
  starting transfers between devices  36.6 us (68%)
  Pallas kernels  7.5 us (14%)
  waiting for transfers between devices  5.69 us (11%)
  local copies, waits for them, and re-layouts  1.61 us (3%)
  between operations  1.47 us (3%)
    ppermute x8, starting transfers between devices, body(): send = lambda value, pairs: lax.ppermute(value, AXES, pairs)  36.6 us
    pallas_call x6, Pallas kernels, call(): pl.pallas_call(body, out_shape=tuple(outs), in_specs=specs, out_specs=tup...  7.5 us
    ppermute x8, waiting for transfers between devices, body(): send = lambda value, pairs: lax.ppermute(value, AXES, pairs)  5.69 us
    unnamed x10, local copies, waits for them, and re-layouts  1.61 us
  transfers between devices with their start and end apart: 8, of which 3 were waited for; matrix products, arithmetic and copies ran while one was open for 0% of the time, Pallas kernels for 5%

profile of v1, /device:TPU:65, one launch (start us, length us, event | category | flops | bytes accessed | tf_op | source)
XLA Modules:
  0.0 52.8 jit_solution(5506715700027618770)
XLA Ops:
  0.7 0.0 copy-start
  0.7 1.6 %copy-done = bf16[8,8,8,8,256]{4,3,2,1,0:T(8,128)(2,1)S(1)} copy-done((bf16[8,8,8,8,256]{4,3,2,1,0:T(8,128)(2,1)S(1)}, bf16[8,8,8,8,256]{4,3,2,1,0:T(8,128)(2,1)}, u32[]{:S(2)}) %copy-start) | copy-done | bytes 2097176
  2.2 0.0 copy-start.2
  2.2 0.0 copy-start.4
  2.2 0.1 x_faces.1
  2.4 3.3 %collective-permute-start.2 = (bf16[256,256]{1,0:T(8,128)(2,1)S(1)}, bf16[256,256]{1,0:T(8,128)(2,1)S(1)}, u32[]{:S(2)}, u32[]{:S(2)}) collective-permute-start(bf16[256,256]{1,0:T(8,128)(2,1)S(1)} %get-tuple-element.18), channel_id=1, source_target_pairs={{0,32},{1,33},{2,34},{3,35},{4,36},{5,37},{6,38},{7,39},{8,40},{9,... | collective-permute-start | bytes 393224 | tf_op jit(solution)/shard_map/ppermute | solution.py:246
  5.6 0.7 %collective-permute-start.3 = (bf16[256,256]{1,0:T(8,128)(2,1)S(1)}, bf16[256,256]{1,0:T(8,128)(2,1)S(1)}, u32[]{:S(2)}, u32[]{:S(2)}) collective-permute-start(bf16[256,256]{1,0:T(8,128)(2,1)S(1)} %get-tuple-element.19), channel_id=1, source_target_pairs={{32,64},{33,65},{34,66},{35,67},{36,68},{37,69},{38,70},{39,71},{4... | collective-permute-start | bytes 393224 | tf_op jit(solution)/shard_map/ppermute | solution.py:246
  6.3 0.0 copy-done.2
  6.3 8.3 %collective-permute-start = (bf16[256,256]{1,0:T(8,128)(2,1)S(1)}, bf16[256,256]{1,0:T(8,128)(2,1)S(1)}, u32[]{:S(2)}, u32[]{:S(2)}) collective-permute-start(bf16[256,256]{1,0:T(8,128)(2,1)S(1)} %bitcast.12), channel_id=1, source_target_pairs={{32,64},{33,65},{34,66},{35,67},{36,68},{37,69},{38,70},{39,71},{4... | collective-permute-start | bytes 393224 | tf_op jit(solution)/shard_map/ppermute | solution.py:246
  14.6 0.0 copy-done.4
  14.6 1.7 %inner_cells.1 = (bf16[14,256,256]{2,1,0:T(8,128)(2,1)S(1)}, f32[14,256,256]{2,1,0:T(8,128)S(1)}, f32[14,32,256]{2,1,0:T(8,128)S(1)}) custom-call(s32[1]{0:T(128)} %bitcast.5.count_ref, bf16[8,8,64,256]{3,2,1,0:T(8,128)(2,1)S(1)} %bitcast.10, bf16[2,288,256]{2,1,0:T(8,128)(2,1)S(1)} %copy-done.4), custom_call_target="tpu_custom_call" | custom-call | flops 2000000000 | bytes 5963776 | tf_op jit(solution)/shard_map/inner_cells/pallas_call | solution.py:228
  16.3 0.0 collective-permute-done.2.near_ref
  16.3 0.0 collective-permute-done.3.far_ref
  16.3 0.0 copy-start.3
  16.3 0.0 copy-start.1
  16.4 0.3 x_edges_y_faces.1
  16.7 1.9 %collective-permute-start.4 = (bf16[256,256]{1,0:T(8,128)(2,1)S(1)}, bf16[256,256]{1,0:T(8,128)(2,1)S(1)}, u32[]{:S(2)}, u32[]{:S(2)}) collective-permute-start(bf16[256,256]{1,0:T(8,128)(2,1)S(1)} %get-tuple-element.23), channel_id=1, source_target_pairs={{0,8},{1,9},{2,10},{3,11},{4,12},{5,13},{6,14},{7,15},{8,0},{9,1},... | collective-permute-start | bytes 393224 | tf_op jit(solution)/shard_map/ppermute | solution.py:246
  18.6 16.2 %collective-permute-start.5 = (bf16[256,256]{1,0:T(8,128)(2,1)S(1)}, bf16[256,256]{1,0:T(8,128)(2,1)S(1)}, u32[]{:S(2)}, u32[]{:S(2)}) collective-permute-start(bf16[256,256]{1,0:T(8,128)(2,1)S(1)} %get-tuple-element.24), channel_id=1, source_target_pairs={{8,16},{9,17},{10,18},{11,19},{12,20},{13,21},{14,22},{15,23},{16,... | collective-permute-start | bytes 393224 | tf_op jit(solution)/shard_map/ppermute | solution.py:246
  34.8 0.0 collective-permute-done.tile1_ref
  34.8 1.9 %collective-permute-start.1 = (bf16[256,256]{1,0:T(8,128)(2,1)S(1)}, bf16[256,256]{1,0:T(8,128)(2,1)S(1)}, u32[]{:S(2)}, u32[]{:S(2)}) collective-permute-start(bf16[256,256]{1,0:T(8,128)(2,1)S(1)} %collective-permute-done.tile1_ref), channel_id=1, source_target_pairs={{0,8},{1,9},{2,10},{3,11},{4,12},{5,13},{6,14},{7,15},{8,0},{9,1},... | collective-permute-start | bytes 393224 | tf_op jit(solution)/shard_map/ppermute | solution.py:246
  36.7 0.2 edge_cells.1
  36.9 0.0 collective-permute-done.4.ynear_ref.rest_0_
  37.0 0.5 collective-permute-done.5.yfar_ref.rest_1_
  37.4 0.0 copy-done.3
  37.4 0.2 z_faces.1
  37.6 2.4 %collective-permute-start.6 = (bf16[256,256]{1,0:T(8,128)(2,1)S(1)}, bf16[256,256]{1,0:T(8,128)(2,1)S(1)}, u32[]{:S(2)}, u32[]{:S(2)}) collective-permute-start(bf16[256,256]{1,0:T(8,128)(2,1)S(1)} %get-tuple-element.27), channel_id=1, source_target_pairs={{0,1},{1,0},{2,3},{3,2},{4,5},{5,4},{6,7},{7,6},{8,9},{9,8},{10,11... | collective-permute-start | bytes 393224 | tf_op jit(solution)/shard_map/ppermute | solution.py:246
  40.1 1.9 %collective-permute-start.7 = (bf16[256,256]{1,0:T(8,128)(2,1)S(1)}, bf16[256,256]{1,0:T(8,128)(2,1)S(1)}, u32[]{:S(2)}, u32[]{:S(2)}) collective-permute-start(bf16[256,256]{1,0:T(8,128)(2,1)S(1)} %get-tuple-element.28), channel_id=1, source_target_pairs={{1,2},{2,1},{3,4},{4,3},{5,6},{6,5},{9,10},{10,9},{11,12},{12,11},... | collective-permute-start | bytes 393224 | tf_op jit(solution)/shard_map/ppermute | solution.py:246
  42.6 0.0 collective-permute-done.1.tile2_ref
  42.6 1.9 %collective-permute-done.6.rest_2_ = bf16[256,256]{1,0:T(8,128)(2,1)S(1)} collective-permute-done((bf16[256,256]{1,0:T(8,128)(2,1)S(1)}, bf16[256,256]{1,0:T(8,128)(2,1)S(1)}, u32[]{:S(2)}, u32[]{:S(2)}) %collective-permute-start.6) | collective-permute-done | bytes 131104 | tf_op jit(solution)/shard_map/ppermute | solution.py:246
  44.5 3.4 %collective-permute-done.7.rest_3_ = bf16[256,256]{1,0:T(8,128)(2,1)S(1)} collective-permute-done((bf16[256,256]{1,0:T(8,128)(2,1)S(1)}, bf16[256,256]{1,0:T(8,128)(2,1)S(1)}, u32[]{:S(2)}, u32[]{:S(2)}) %collective-permute-start.7) | collective-permute-done | bytes 131104 | tf_op jit(solution)/shard_map/ppermute | solution.py:246
  47.9 0.0 copy-done.1
  47.9 5.0 %density.1 = f32[32,128]{1,0:T(8,128)} custom-call(s32[1]{0:T(128)} %bitcast.8.offset_ref, bf16[256,256]{1,0:T(8,128)(2,1)S(1)} %bitcast.13, bf16[256,256]{1,0:T(8,128)(2,1)S(1)} %collective-permute-done.tile1_ref, bf16[256,256]{1,0:T(8,128)(2,1)S(1)} %collective-permute-done.1.tile2_ref, f32[14,256,256]{2,1,0:T(8,128)S(1)} %get-tuple-element.17.p_ref, ...), custom_call_target="tpu_custom_call" | custom-call | flops 1000000 | bytes 16384 | tf_op jit(solution)/shard_map/density/pallas_call | solution.py:228
Async XLA Ops:
  0.7 1.6 %copy-start = (bf16[8,8,8,8,256]{4,3,2,1,0:T(8,128)(2,1)S(1)}, bf16[8,8,8,8,256]{4,3,2,1,0:T(8,128)(2,1)}, u32[]{:S(2)}) copy-start(bf16[8,8,8,8,256]{4,3,2,1,0:T(8,128)(2,1)} %param.7) | copy-start | bytes 6291460
  2.2 4.1 %copy-start.2 = (bf16[1,256,256]{2,1,0:T(8,128)(2,1)S(1)}, bf16[1,256,256]{2,1,0:T(8,128)(2,1)}, u32[]{:S(2)}) copy-start(bf16[1,256,256]{2,1,0:T(8,128)(2,1)} %param.10) | copy-start | bytes 393220
  2.2 12.4 %copy-start.4 = (bf16[2,288,256]{2,1,0:T(8,128)(2,1)S(1)}, bf16[2,288,256]{2,1,0:T(8,128)(2,1)}, u32[]{:S(2)}) copy-start(bf16[2,288,256]{2,1,0:T(8,128)(2,1)} %constant.6.clone.text_ref) | copy-start | bytes 884740
  2.4 13.9 %collective-permute-start.2 = (bf16[256,256]{1,0:T(8,128)(2,1)S(1)}, bf16[256,256]{1,0:T(8,128)(2,1)S(1)}, u32[]{:S(2)}, u32[]{:S(2)}) collective-permute-start(bf16[256,256]{1,0:T(8,128)(2,1)S(1)} %get-tuple-element.18), channel_id=1, source_target_pairs={{0,32},{1,33},{2,34},{3,35},{4,36},{5,37},{6,38},{7,39},{8,40},{9,... | collective-permute-start | bytes 393224 | tf_op jit(solution)/shard_map/ppermute | solution.py:246
  5.6 10.7 %collective-permute-start.3 = (bf16[256,256]{1,0:T(8,128)(2,1)S(1)}, bf16[256,256]{1,0:T(8,128)(2,1)S(1)}, u32[]{:S(2)}, u32[]{:S(2)}) collective-permute-start(bf16[256,256]{1,0:T(8,128)(2,1)S(1)} %get-tuple-element.19), channel_id=1, source_target_pairs={{32,64},{33,65},{34,66},{35,67},{36,68},{37,69},{38,70},{39,71},{4... | collective-permute-start | bytes 393224 | tf_op jit(solution)/shard_map/ppermute | solution.py:246
  6.3 28.4 %collective-permute-start = (bf16[256,256]{1,0:T(8,128)(2,1)S(1)}, bf16[256,256]{1,0:T(8,128)(2,1)S(1)}, u32[]{:S(2)}, u32[]{:S(2)}) collective-permute-start(bf16[256,256]{1,0:T(8,128)(2,1)S(1)} %bitcast.12), channel_id=1, source_target_pairs={{32,64},{33,65},{34,66},{35,67},{36,68},{37,69},{38,70},{39,71},{4... | collective-permute-start | bytes 393224 | tf_op jit(solution)/shard_map/ppermute | solution.py:246
  16.3 21.1 %copy-start.3 = (bf16[4,32,32]{2,1,0:T(8,128)(2,1)S(1)}, bf16[4,32,32]{2,1,0:T(8,128)(2,1)}, u32[]{:S(2)}) copy-start(bf16[4,32,32]{2,1,0:T(8,128)(2,1)} %constant.7.clone.mzh_ref) | copy-start | bytes 24580
  16.3 31.5 %copy-start.1 = (bf16[4,256,64]{2,1,0:T(8,128)(2,1)S(1)}, bf16[4,256,64]{2,1,0:T(8,128)(2,1)}, u32[]{:S(2)}) copy-start(bf16[4,256,64]{2,1,0:T(8,128)(2,1)} %constant.8.clone.th_ref) | copy-start | bytes 393220
  16.7 20.3 %collective-permute-start.4 = (bf16[256,256]{1,0:T(8,128)(2,1)S(1)}, bf16[256,256]{1,0:T(8,128)(2,1)S(1)}, u32[]{:S(2)}, u32[]{:S(2)}) collective-permute-start(bf16[256,256]{1,0:T(8,128)(2,1)S(1)} %get-tuple-element.23), channel_id=1, source_target_pairs={{0,8},{1,9},{2,10},{3,11},{4,12},{5,13},{6,14},{7,15},{8,0},{9,1},... | collective-permute-start | bytes 393224 | tf_op jit(solution)/shard_map/ppermute | solution.py:246
  18.6 18.8 %collective-permute-start.5 = (bf16[256,256]{1,0:T(8,128)(2,1)S(1)}, bf16[256,256]{1,0:T(8,128)(2,1)S(1)}, u32[]{:S(2)}, u32[]{:S(2)}) collective-permute-start(bf16[256,256]{1,0:T(8,128)(2,1)S(1)} %get-tuple-element.24), channel_id=1, source_target_pairs={{8,16},{9,17},{10,18},{11,19},{12,20},{13,21},{14,22},{15,23},{16,... | collective-permute-start | bytes 393224 | tf_op jit(solution)/shard_map/ppermute | solution.py:246
  34.8 7.9 %collective-permute-start.1 = (bf16[256,256]{1,0:T(8,128)(2,1)S(1)}, bf16[256,256]{1,0:T(8,128)(2,1)S(1)}, u32[]{:S(2)}, u32[]{:S(2)}) collective-permute-start(bf16[256,256]{1,0:T(8,128)(2,1)S(1)} %collective-permute-done.tile1_ref), channel_id=1, source_target_pairs={{0,8},{1,9},{2,10},{3,11},{4,12},{5,13},{6,14},{7,15},{8,0},{9,1},... | collective-permute-start | bytes 393224 | tf_op jit(solution)/shard_map/ppermute | solution.py:246
  37.6 6.9 %collective-permute-start.6 = (bf16[256,256]{1,0:T(8,128)(2,1)S(1)}, bf16[256,256]{1,0:T(8,128)(2,1)S(1)}, u32[]{:S(2)}, u32[]{:S(2)}) collective-permute-start(bf16[256,256]{1,0:T(8,128)(2,1)S(1)} %get-tuple-element.27), channel_id=1, source_target_pairs={{0,1},{1,0},{2,3},{3,2},{4,5},{5,4},{6,7},{7,6},{8,9},{9,8},{10,11... | collective-permute-start | bytes 393224 | tf_op jit(solution)/shard_map/ppermute | solution.py:246
  40.1 7.8 %collective-permute-start.7 = (bf16[256,256]{1,0:T(8,128)(2,1)S(1)}, bf16[256,256]{1,0:T(8,128)(2,1)S(1)}, u32[]{:S(2)}, u32[]{:S(2)}) collective-permute-start(bf16[256,256]{1,0:T(8,128)(2,1)S(1)} %get-tuple-element.28), channel_id=1, source_target_pairs={{1,2},{2,1},{3,4},{4,3},{5,6},{6,5},{9,10},{10,9},{11,12},{12,11},... | collective-permute-start | bytes 393224 | tf_op jit(solution)/shard_map/ppermute | solution.py:246

commit v2 on v1

v2 whole, which is shorter than its diff:
```python
import functools

import jax
import jax.numpy as jnp
import ml_dtypes
import numpy as np
from jax import lax
from jax.experimental import pallas as pl
from jax.experimental.pallas import tpu as pltpu
from jax.sharding import PartitionSpec as P


FILT = [0.48296291314453416, 0.8365163037378079, 0.2241438680420134, -0.12940952255126037]
WAVE = [(1.0 if t % 2 == 0 else -1.0) * FILT[3 - t] for t in range(4)]
AXES = ("gx", "gy", "gz")
F32, BF16 = jnp.float32, jnp.bfloat16


def band_table(coarse):
    table = np.zeros((2, 2 * coarse, coarse))
    for fine in range(2 * coarse):
        for point in range(coarse):
            tap = fine - 2 * point + 1
            if 0 <= tap <= 3:
                table[0, fine, point] = FILT[tap]
                table[1, fine, point] = WAVE[tap]
    return table


def make_tables(cy, cz):
    ty, tz = band_table(cy), band_table(cz)
    fy, fz = 2 * cy, 2 * cz
    inner = np.einsum("cnk,dml->nmcdkl", ty, tz).reshape(fy, fz, 4 * cy * cz)
    zside = np.concatenate([inner[:, 0], inner[:, fz - 1]])
    inner = inner.reshape(fy * fz, 4 * cy * cz)
    ends = {}
    for name, plane, tap in (("first", 0, 0), ("last", cz - 1, 3)):
        pick = np.zeros((2, cz))
        pick[0, plane], pick[1, plane] = FILT[tap], WAVE[tap]
        own = np.einsum("cnk,dl->ncdkl", ty, pick).reshape(fy, 4 * cy * cz)
        before = np.zeros((fy, 2 * cz))
        before[0] = pick.reshape(-1)
        after = np.zeros((fy, 2 * cz))
        after[fy - 1] = pick.reshape(-1)
        ends[name] = (own, before, after)
    along = np.transpose(tz, (1, 0, 2)).reshape(fz, 2 * cz)
    adds = {}
    for name, row in (("before", 0), ("after", fy - 1)):
        rows = np.zeros((2, fz, 2 * cz))
        rows[0 if name == "before" else 1] = along
        sides = np.zeros((2, fy, 2 * cz))
        sides[0, row], sides[1, row] = along[0], along[fz - 1]
        adds[name] = np.concatenate([rows.reshape(2 * fz, -1), sides.reshape(2 * fy, -1)])
    text, mzh, add = [], [], []
    which = {"before": 1, "after": 2}
    for pz in range(2):
        order = ("last", "first") if pz == 0 else ("first", "last")
        text.append(np.concatenate([inner] + [ends[o][0] for o in order] + [zside]))
    for py in range(2):
        sides = ("after", "before") if py == 0 else ("before", "after")
        add.append(np.concatenate([adds[s] for s in sides], axis=1))
        for pz in range(2):
            order = ("last", "first") if pz == 0 else ("first", "last")
            mzh.append(np.concatenate([np.concatenate([ends[o][which[s]] for s in sides], axis=1) for o in order]))
    cast = lambda parts: np.stack(parts).astype(np.float32).astype(ml_dtypes.bfloat16)
    return cast(text), cast(mzh), cast(add)


def swap_pairs(shape, axis, near):
    out = []
    for place in np.ndindex(*shape):
        other = list(place)
        other[axis] = place[axis] ^ 1 if near else ((place[axis] - 1) ^ 1) + 1
        if 0 <= other[axis] < shape[axis]:
            out.append((int(np.ravel_multi_index(place, shape)), int(np.ravel_multi_index(other, shape))))
    return out


def tile_pairs(shape):
    nx, ny, _ = shape
    index = lambda x, y, z: int(np.ravel_multi_index((x % nx, y % ny, z), shape))
    out = []
    for x, y, z in np.ndindex(*shape):
        source = x - 1 if y % 2 == 0 else x + 1
        if source < nx:
            crosses = (source % nx) // 4 != x // 4
            out.append((index(source, y + 2 if crosses else y, z), index(x, y, z)))
    return out


def wrap_pairs(shape):
    nx, ny, nz = shape
    index = lambda x, y, z: int(np.ravel_multi_index((x, y, z), shape))
    return [(index(0, ny - y, z), index(nx - 1, y if y == 1 else ny - 1, z)) if y == 1 else (index(0, ny - 2, z), index(nx - 1, ny - 1, z)) for z in range(nz) for y in (1, 2)]


def last_pairs(shape):
    nx, ny, nz = shape
    index = lambda y, z: int(np.ravel_multi_index((nx - 1, y, z), shape))
    return [(index(y, z), index(y ^ 1, z)) for y in range(ny) for z in range(nz)]


def parity(axis):
    return lax.rem(lax.axis_index(axis), 2)


def lane_mask(count_ref, rows, lanes):
    return lax.broadcasted_iota(jnp.int32, (rows, lanes), 1) < count_ref[0]


def faces_kernel(count_ref, c_hbm, near_ref, far_ref, planes_ref, sem):
    last_k, rows = c_hbm.shape[1] - 1, c_hbm.shape[2]
    copies = [pltpu.make_async_copy(c_hbm.at[:, k], planes_ref.at[i], sem.at[i]) for i, k in enumerate((0, last_k))]
    for copy in copies:
        copy.start()
    even = parity("gx") == 0
    mask = lane_mask(count_ref, rows, c_hbm.shape[3])
    for copy in copies:
        copy.wait()
    for b in range(4):
        first = FILT[0] * planes_ref[0, b].astype(F32) + WAVE[0] * planes_ref[0, 4 + b].astype(F32)
        last = FILT[3] * planes_ref[1, b].astype(F32) + WAVE[3] * planes_ref[1, 4 + b].astype(F32)
        first, last = jnp.where(mask, first, 0.0), jnp.where(mask, last, 0.0)
        near_ref[b * rows : (b + 1) * rows] = jnp.where(even, last, first).astype(BF16)
        far_ref[b * rows : (b + 1) * rows] = jnp.where(even, first, last).astype(BF16)


def split_cells(r, i, mid_ref, yside_ref, z_ref, zside_ref):
    fz, sent = yside_ref.shape[1] // 2, z_ref.shape[1]
    cells = mid_ref.shape[1] + 2 * fz
    mid_ref[i] = r[fz : cells - fz].astype(BF16)
    yside_ref[i] = jnp.concatenate([r[:fz], r[cells - fz : cells]], axis=0)
    z_ref[i] = r[cells : cells + sent]
    zside_ref[i] = r[cells + sent :]


def inner_kernel(count_ref, c_hbm, text_ref, x_ref, mid_ref, yside_ref, z_ref, zside_ref, c_ref, sem):
    planes, rows = c_hbm.shape[1], c_hbm.shape[2]
    copies = [pltpu.make_async_copy(c_hbm.at[:, k], c_ref.at[k], sem.at[k]) for k in range(planes)]
    for copy in copies:
        copy.start()
    mask = lane_mask(count_ref, rows, c_hbm.shape[3])
    pz = parity("gz")
    copies[0].wait()
    for m in range(1, planes):
        copies[m].wait()
        odd, even = [], []
        for b in range(4):
            s0, w0 = c_ref[m - 1, b].astype(F32), c_ref[m - 1, 4 + b].astype(F32)
            s1, w1 = c_ref[m, b].astype(F32), c_ref[m, 4 + b].astype(F32)
            o = FILT[2] * s0 + WAVE[2] * w0 + FILT[0] * s1 + WAVE[0] * w1
            e = FILT[3] * s0 + WAVE[3] * w0 + FILT[1] * s1 + WAVE[1] * w1
            odd.append(jnp.where(mask, o, 0.0).astype(BF16))
            even.append(jnp.where(mask, e, 0.0).astype(BF16))
        for i, parts in ((2 * m - 2, odd), (2 * m - 1, even)):
            x = jnp.concatenate(parts, axis=0)
            x_ref[i] = x
            split_cells(jnp.dot(text_ref[pz], x, preferred_element_type=F32), i, mid_ref, yside_ref, z_ref, zside_ref)


def edge_kernel(count_ref, planes_ref, near_ref, far_ref, x_ref, edge_ref, ynear_ref, yfar_ref, *, cy, cz):
    rows = planes_ref.shape[2]
    mask = lane_mask(count_ref, rows, planes_ref.shape[3])
    even = parity("gx") == 0
    for b in range(4):
        near, far = near_ref[b * rows : (b + 1) * rows].astype(F32), far_ref[b * rows : (b + 1) * rows].astype(F32)
        before, after = jnp.where(even, far, near), jnp.where(even, near, far)
        s0, w0 = planes_ref[0, b].astype(F32), planes_ref[0, 4 + b].astype(F32)
        s1, w1 = planes_ref[1, b].astype(F32), planes_ref[1, 4 + b].astype(F32)
        lo = jnp.where(mask, FILT[1] * s0 + WAVE[1] * w0, 0.0) + before
        hi = jnp.where(mask, FILT[2] * s1 + WAVE[2] * w1, 0.0) + after
        edge_ref[0, b * rows : (b + 1) * rows] = lo.astype(BF16)
        edge_ref[1, b * rows : (b + 1) * rows] = hi.astype(BF16)
    even_y = parity("gy") == 0
    fine = x_ref.shape[0] + 2
    for n in range(fine):
        ref, i = (edge_ref, 0) if n == 0 else (edge_ref, 1) if n == fine - 1 else (x_ref, n - 1)
        near_rows, far_rows = [], []
        for zb in range(2):
            low, high = zb * rows, (2 + zb) * rows
            end = (cy - 1) * cz
            first = FILT[0] * ref[i, low : low + cz].astype(F32) + WAVE[0] * ref[i, high : high + cz].astype(F32)
            last = FILT[3] * ref[i, low + end : low + end + cz].astype(F32) + WAVE[3] * ref[i, high + end : high + end + cz].astype(F32)
            near_rows.append(jnp.where(even_y, last, first))
            far_rows.append(jnp.where(even_y, first, last))
        ynear_ref[n * 2 * cz : (n + 1) * 2 * cz] = jnp.concatenate(near_rows, axis=0).astype(BF16)
        yfar_ref[n * 2 * cz : (n + 1) * 2 * cz] = jnp.concatenate(far_rows, axis=0).astype(BF16)


def edge_cells_kernel(edge_ref, text_ref, *out_refs):
    pz = parity("gz")
    for i in range(2):
        split_cells(jnp.dot(text_ref[pz], edge_ref[i], preferred_element_type=F32), i, *out_refs)


def at(n, fine, inner_ref, edge_ref):
    return edge_ref[0] if n == 0 else edge_ref[1] if n == fine - 1 else inner_ref[n - 1]


def zfaces_kernel(ynear_ref, yfar_ref, z_ref, ze_ref, mzh_ref, near_ref, far_ref):
    case = 2 * parity("gy") + parity("gz")
    fine = z_ref.shape[0] + 2
    step = ynear_ref.shape[0] // fine
    half = z_ref.shape[1] // 2
    for n in range(fine):
        rows = slice(n * step, (n + 1) * step)
        halo = jnp.concatenate([ynear_ref[rows], yfar_ref[rows]], axis=0)
        r = at(n, fine, z_ref, ze_ref) + jnp.dot(mzh_ref[case], halo, preferred_element_type=F32)
        near_ref[n * half : (n + 1) * half] = r[:half].astype(BF16)
        far_ref[n * half : (n + 1) * half] = r[half:].astype(BF16)


def slot_sums(phi, k, wide):
    psi = jnp.dot(phi, k, preferred_element_type=F32)
    prod = phi.astype(F32) * psi
    half = prod.shape[1] // 2
    prod = prod[:, :half] + prod[:, half:]
    high = prod.astype(BF16)
    low = (prod - high.astype(F32)).astype(BF16)
    return jnp.dot(jnp.concatenate([high, low], axis=1), jnp.ones((2 * half, wide), BF16), preferred_element_type=F32)


def row_of(sums):
    lanes = sums.shape[1]
    diag = lax.broadcasted_iota(jnp.int32, (lanes, lanes), 0) == lax.broadcasted_iota(jnp.int32, (lanes, lanes), 1)
    parts = [jnp.where(diag, sums[i : i + lanes], 0.0) for i in range(0, sums.shape[0], lanes)]
    return jnp.concatenate([jnp.sum(part, axis=0, keepdims=True) for part in parts], axis=1)


def density_kernel(offset_ref, own_ref, tile1_ref, tile2_ref, ynear_ref, yfar_ref, add_ref, *rest):
    mid_ref, yside_ref, zside_ref, mide_ref, ysidee_ref, zsidee_ref, phi_ref, side_ref, d_ref, k_ref, own_out_ref = rest
    own_out_ref[...] = own_ref[...]
    even = parity("gy") == 0
    offset = offset_ref[0]
    first, second = tile1_ref[...], tile2_ref[...]
    before, after = jnp.where(even, first, second), jnp.where(even, second, first)
    k_ref[...] = jnp.where(offset == -1, before, jnp.where(offset == 1, after, own_ref[...]))
    fine = phi_ref.shape[0]
    step = ynear_ref.shape[0] // fine
    fz = yside_ref.shape[1] // 2
    for n in range(fine):
        rows = slice(n * step, (n + 1) * step)
        halo = jnp.concatenate([ynear_ref[rows], yfar_ref[rows]], axis=0)
        more = jnp.dot(add_ref[parity("gy")], halo, preferred_element_type=F32)
        ends = (at(n, fine, yside_ref, ysidee_ref) + more[: 2 * fz]).astype(BF16)
        side_ref[n] = at(n, fine, zside_ref, zsidee_ref) + more[2 * fz :]
        phi = jnp.concatenate([ends[:fz], at(n, fine, mid_ref, mide_ref), ends[fz:]], axis=0)
        phi_ref[n] = phi

    @pl.when(~in_last_domain())
    def _():
        for n in range(fine):
            d_ref[n : n + 1] = row_of(slot_sums(phi_ref[n], k_ref[...], 128))


def in_last_domain():
    return lax.axis_index("gx") == lax.axis_size("gx") - 1


def finish_kernel(offset_ref, wrap1_ref, wrap2_ref, near_ref, far_ref, phi_ref, side_ref, d_ref, k_ref, out_ref, tile_ref, dens_ref):
    fine, cells = d_ref.shape
    tile_ref[...] = k_ref[...]
    dens_ref[...] = d_ref[...]

    @pl.when(in_last_domain())
    def _():
        wrapped = jnp.where(parity("gy") == 0, wrap2_ref[...], wrap1_ref[...])
        tile_ref[...] = jnp.where(offset_ref[0] == 1, wrapped, k_ref[...])

        @pl.loop(0, fine)
        def _(n):
            dens_ref[pl.ds(n, 1)] = row_of(slot_sums(phi_ref[n], tile_ref[...], 128))

    even = parity("gz") == 0
    fy = near_ref.shape[0] // fine
    fz = cells // fy
    shape = (2 * fy, cells)
    row, lane = lax.broadcasted_iota(jnp.int32, shape, 0), lax.broadcasted_iota(jnp.int32, shape, 1)
    mine = lane == jnp.where(row < fy, row * fz, (row - fy) * fz + fz - 1)
    lane = lax.broadcasted_iota(jnp.int32, (1, cells), 1) % fz
    side = (lane == 0) | (lane == fz - 1)
    some = fine // 4
    for part in range(4):
        phi = []
        for n in range(part * some, (part + 1) * some):
            near, far = near_ref[n * fy : (n + 1) * fy].astype(F32), far_ref[n * fy : (n + 1) * fy].astype(F32)
            before, after = jnp.where(even, far, near), jnp.where(even, near, far)
            phi.append((side_ref[n] + jnp.concatenate([before, after], axis=0)).astype(BF16))
        sums = slot_sums(jnp.concatenate(phi, axis=0), tile_ref[...], cells)
        for i in range(some):
            n = part * some + i
            new = jnp.sum(jnp.where(mine, sums[i * 2 * fy : (i + 1) * 2 * fy], 0.0), axis=0, keepdims=True)
            new = jnp.where(side, new, dens_ref[n : n + 1])
            for j in range(cells // 128):
                out_ref[n * (cells // 128) + j : n * (cells // 128) + j + 1] = new[:, j * 128 : (j + 1) * 128]


def call(body, outs, args, scalars=0, scratch=(), flops=1e6, hbm=()):
    space = lambda i: pltpu.SMEM if i < scalars else pltpu.HBM if i in hbm else pltpu.VMEM
    specs = [pl.BlockSpec(memory_space=space(i)) for i in range(len(args))]
    args = [a if i < scalars else pltpu.with_memory_space_constraint(a, space(i)) for i, a in enumerate(args)]
    size = sum(int(np.prod(o.shape)) * o.dtype.itemsize for o in outs)
    return pl.pallas_call(
        body,
        out_shape=tuple(outs),
        in_specs=specs,
        out_specs=tuple(pl.BlockSpec(memory_space=pltpu.VMEM) for _ in outs),
        scratch_shapes=list(scratch),
        compiler_params=pltpu.CompilerParams(vmem_limit_bytes=16 << 20),
        cost_estimate=pl.CostEstimate(flops=int(flops), bytes_accessed=size, transcendentals=0),
    )(*args)


def send(value, pairs):
    return lax.ppermute(value, AXES, pairs)


def body(coefficients, fun_count, tile_offset, kernel, *, shape):
    return steps(coefficients, fun_count, tile_offset, kernel, shape)


def steps(coefficients, fun_count, tile_offset, kernel, shape):
    bands, cx, cy, cz, slots = coefficients.shape
    text, mzh, add = make_tables(cy, cz)
    rows, cells, fx = cy * cz, 4 * cy * cz, 2 * cx
    near = [swap_pairs(shape, axis, True) for axis in range(3)]
    far = [swap_pairs(shape, axis, False) for axis in range(3)]
    vmem = pltpu.VMEM
    count = fun_count.reshape(1)
    offset = tile_offset.reshape(1)
    c = coefficients.reshape(bands, cx, rows, slots)
    own = kernel.reshape(kernel.shape[1:])
    face = vmem((4 * rows, slots), BF16)

    xnear, xfar, planes = call(
        faces_kernel, [face, face, vmem((2, bands, rows, slots), BF16)], [count, c], 1,
        scratch=[pltpu.SemaphoreType.DMA((2,))], hbm=(1,),
    )
    xfar = send(xfar, far[0])
    xnear = send(xnear, near[0])
    tile1 = send(own, tile_pairs(shape))

    def cell_outs(n):
        return [
            vmem((n, cells - 4 * cz, slots), BF16), vmem((n, 4 * cz, slots), F32),
            vmem((n, 4 * cy, slots), F32), vmem((n, 4 * cy, slots), F32),
        ]

    x, mid, yside, z, zside = call(
        inner_kernel, [vmem((fx - 2, 4 * rows, slots), BF16)] + cell_outs(fx - 2), [count, c, text], 1,
        scratch=[vmem((cx, bands, rows, slots), BF16), pltpu.SemaphoreType.DMA((cx,))], flops=2e9, hbm=(1,),
    )
    yshape = vmem((fx * 2 * cz, slots), BF16)
    edge, ynear, yfar = call(
        functools.partial(edge_kernel, cy=cy, cz=cz),
        [vmem((2, 4 * rows, slots), BF16), yshape, yshape], [count, planes, xnear, xfar, x], 1,
    )
    yfar = send(yfar, far[1])
    ynear = send(ynear, near[1])
    mide, ysidee, ze, zsidee = call(edge_cells_kernel, cell_outs(2), [edge, text], flops=3e8)
    zshape = vmem((fx * 2 * cy, slots), BF16)
    znear, zfar = call(zfaces_kernel, [zshape, zshape], [ynear, yfar, z, ze, mzh])
    znear = send(znear, near[2])
    zfar = send(zfar, far[2])
    tile2 = send(tile1, near[1])
    square = vmem((slots, slots), BF16)
    phi, side, d, tile, own_late = call(
        density_kernel,
        [vmem((fx, cells, slots), BF16), vmem((fx, 4 * cy, slots), F32), vmem((fx, cells), F32), square, square],
        [offset, own, tile1, tile2, ynear, yfar, add, mid, yside, zside, mide, ysidee, zsidee], 1, flops=2e9,
    )
    wrap1 = send(own_late, wrap_pairs(shape))
    wrap2 = send(wrap1, last_pairs(shape))
    (out,) = call(
        finish_kernel, [jax.ShapeDtypeStruct((fx * cells // 128, 128), F32)],
        [offset, wrap1, wrap2, znear, zfar, phi, side, d, tile], 1,
        scratch=[vmem((slots, slots), BF16), vmem((fx, cells), F32)],
    )
    return out.reshape(1, 1, 1, -1)


def solution(mesh):
    placed = (
        P(None, "gx", "gy", "gz", None),
        P("gx", "gy", "gz"),
        P("gx", "gy", "gz"),
        P("gx", None, None),
    )
    shape = tuple(mesh.shape[a] for a in AXES)
    return jax.shard_map(
        functools.partial(body, shape=shape), mesh=mesh, in_specs=placed, out_specs=P("gx", "gy", "gz", None), check_vma=False
    )
```

time: 53.7 us -> 56.1 us (1.045)
  the two profiles are of different devices: /device:TPU:65 before, /device:TPU:73 now
where the time goes in v2:
time: 56.1 us; the launch traced here: 55.7 us
  starting transfers between devices  41 us (73%)
  Pallas kernels  8.83 us (16%)
  waiting for transfers between devices  4.33 us (8%)
  between operations  1.52 us (3%)
    ppermute x10, starting transfers between devices, send(): return lax.ppermute(value, AXES, pairs)  41 us
    pallas_call x7, Pallas kernels, call(): pl.pallas_call(body, out_shape=tuple(outs), in_specs=specs, out_specs=tup...  8.83 us
    ppermute x10, waiting for transfers between devices, send(): return lax.ppermute(value, AXES, pairs)  4.33 us
  transfers between devices with their start and end apart: 10, of which 2 were waited for; matrix products, arithmetic and copies ran while one was open for 0% of the time, Pallas kernels for 11%

profile of v2, /device:TPU:73, one launch (start us, length us, event | category | flops | bytes accessed | tf_op | source)
XLA Modules:
  0.0 55.7 jit_solution(2763122025614989546)
XLA Ops:
  0.0 0.0 copy-start.2
  0.0 1.4 %collective-permute-start = (bf16[256,256]{1,0:T(8,128)(2,1)}, bf16[256,256]{1,0:T(8,128)(2,1)S(1)}, u32[]{:S(2)}, u32[]{:S(2)}) collective-permute-start(bf16[256,256]{1,0:T(8,128)(2,1)} %bitcast.10), channel_id=1, source_target_pairs={{1008,0},{1009,1},{1010,2},{1011,3},{1012,4},{1013,5},{1014,6},{10... | collective-permute-start | bytes 393224 | tf_op jit(solution)/shard_map/ppermute | solution.py:315
  2.1 1.2 %shard_map.73 = (bf16[256,256]{1,0:T(8,128)(2,1)S(1)}, bf16[256,256]{1,0:T(8,128)(2,1)S(1)}, bf16[2,8,64,256]{3,2,1,0:T(8,128)(2,1)S(1)}) custom-call(s32[1]{0:T(128)} %bitcast.5.count_ref, bf16[8,8,64,256]{3,2,1,0:T(8,128)(2,1)} %bitcast.12), custom_call_target="tpu_custom_call" | custom-call | flops 1000000 | bytes 786432 | tf_op jit(solution)/shard_map/pallas_call | solution.py:303
  3.3 4.0 %collective-permute-start.2 = (bf16[256,256]{1,0:T(8,128)(2,1)S(1)}, bf16[256,256]{1,0:T(8,128)(2,1)S(1)}, u32[]{:S(2)}, u32[]{:S(2)}) collective-permute-start(bf16[256,256]{1,0:T(8,128)(2,1)S(1)} %get-tuple-element.28), channel_id=1, source_target_pairs={{0,32},{1,33},{2,34},{3,35},{4,36},{5,37},{6,38},{7,39},{8,40},{9,... | collective-permute-start | bytes 393224 | tf_op jit(solution)/shard_map/ppermute | solution.py:315
  7.3 0.7 %collective-permute-start.3 = (bf16[256,256]{1,0:T(8,128)(2,1)S(1)}, bf16[256,256]{1,0:T(8,128)(2,1)S(1)}, u32[]{:S(2)}, u32[]{:S(2)}) collective-permute-start(bf16[256,256]{1,0:T(8,128)(2,1)S(1)} %get-tuple-element.29), channel_id=1, source_target_pairs={{32,64},{33,65},{34,66},{35,67},{36,68},{37,69},{38,70},{39,71},{4... | collective-permute-start | bytes 393224 | tf_op jit(solution)/shard_map/ppermute | solution.py:315
  7.9 0.0 copy-done.2
  7.9 3.9 %shard_map.74 = (bf16[14,256,256]{2,1,0:T(8,128)(2,1)S(1)}, bf16[14,224,256]{2,1,0:T(8,128)(2,1)S(1)}, f32[14,32,256]{2,1,0:T(8,128)S(1)}, f32[14,32,256]{2,1,0:T(8,128)S(1)}, f32[14,32,256]{2,1,0:T(8,128)S(1)}) custom-call(s32[1]{0:T(128)} %bitcast.6.count_ref, bf16[8,8,64,256]{3,2,1,0:T(8,128)(2,1)} %bitcast.13, bf16[2,320,256]{2,1,0:T(8,128)(2,1)S(1)} %copy-done.2), custom_call_target="tpu_custom_call" | custom-call | flops 2000000000 | bytes 4816896 | tf_op jit(solution)/shard_map/pallas_call | solution.py:303
  11.9 0.0 copy-start.1
  11.9 0.0 copy-start.3
  11.9 0.0 collective-permute-done.2.near_ref
  11.9 0.0 collective-permute-done.3.far_ref
  11.9 0.3 shard_map.75
  12.2 2.3 %collective-permute-start.4 = (bf16[256,256]{1,0:T(8,128)(2,1)S(1)}, bf16[256,256]{1,0:T(8,128)(2,1)S(1)}, u32[]{:S(2)}, u32[]{:S(2)}) collective-permute-start(bf16[256,256]{1,0:T(8,128)(2,1)S(1)} %get-tuple-element.31), channel_id=1, source_target_pairs={{0,8},{1,9},{2,10},{3,11},{4,12},{5,13},{6,14},{7,15},{8,0},{9,1},... | collective-permute-start | bytes 393224 | tf_op jit(solution)/shard_map/ppermute | solution.py:315
  14.5 0.0 collective-permute-done.tile1_ref
  14.5 8.6 %collective-permute-start.1 = (bf16[256,256]{1,0:T(8,128)(2,1)S(1)}, bf16[256,256]{1,0:T(8,128)(2,1)S(1)}, u32[]{:S(2)}, u32[]{:S(2)}) collective-permute-start(bf16[256,256]{1,0:T(8,128)(2,1)S(1)} %collective-permute-done.tile1_ref), channel_id=1, source_target_pairs={{0,8},{1,9},{2,10},{3,11},{4,12},{5,13},{6,14},{7,15},{8,0},{9,1},... | collective-permute-start | bytes 393224 | tf_op jit(solution)/shard_map/ppermute | solution.py:315
  23.1 0.7 %collective-permute-start.5 = (bf16[256,256]{1,0:T(8,128)(2,1)S(1)}, bf16[256,256]{1,0:T(8,128)(2,1)S(1)}, u32[]{:S(2)}, u32[]{:S(2)}) collective-permute-start(bf16[256,256]{1,0:T(8,128)(2,1)S(1)} %get-tuple-element.32), channel_id=1, source_target_pairs={{8,16},{9,17},{10,18},{11,19},{12,20},{13,21},{14,22},{15,23},{16,... | collective-permute-start | bytes 393224 | tf_op jit(solution)/shard_map/ppermute | solution.py:315
  24.5 0.2 shard_map.76
  24.7 0.0 collective-permute-done.1.tile2_ref
  24.7 0.0 collective-permute-done.4.ynear_ref
  24.7 0.0 collective-permute-done.5.yfar_ref
  24.8 0.0 copy-done.1
  24.8 0.0 copy-done.3
  24.8 0.0 copy-start
  24.8 1.9 %shard_map.77 = (bf16[16,256,256]{2,1,0:T(8,128)(2,1)S(1)}, f32[16,32,256]{2,1,0:T(8,128)S(1)}, f32[16,256]{1,0:T(8,128)S(1)}, bf16[256,256]{1,0:T(8,128)(2,1)S(1)}, bf16[256,256]{1,0:T(8,128)(2,1)S(1)}) custom-call(s32[1]{0:T(128)} %bitcast.8.offset_ref, bf16[256,256]{1,0:T(8,128)(2,1)S(1)} %bitcast.11, ...), custom_call_target="tpu_custom_call" | custom-call | flops 2000000000 | bytes 2899968 | tf_op jit(solution)/shard_map/pallas_call | solution.py:303
  26.7 18.3 %collective-permute-start.6 = (bf16[256,256]{1,0:T(8,128)(2,1)S(1)}, bf16[256,256]{1,0:T(8,128)(2,1)S(1)}, u32[]{:S(2)}, u32[]{:S(2)}) collective-permute-start(bf16[256,256]{1,0:T(8,128)(2,1)S(1)} %get-tuple-element.40), channel_id=1, source_target_pairs={{24,1000},{16,1016},{25,1001},{17,1017},{26,1002},{18,1018},{27,10... | collective-permute-start | bytes 393224 | tf_op jit(solution)/shard_map/ppermute | solution.py:315
  45.1 0.0 copy-done
  45.1 0.2 shard_map.78
  45.3 2.4 %collective-permute-start.8 = (bf16[256,256]{1,0:T(8,128)(2,1)S(1)}, bf16[256,256]{1,0:T(8,128)(2,1)S(1)}, u32[]{:S(2)}, u32[]{:S(2)}) collective-permute-start(bf16[256,256]{1,0:T(8,128)(2,1)S(1)} %get-tuple-element.43), channel_id=1, source_target_pairs={{0,1},{1,0},{2,3},{3,2},{4,5},{5,4},{6,7},{7,6},{8,9},{9,8},{10,11... | collective-permute-start | bytes 393224 | tf_op jit(solution)/shard_map/ppermute | solution.py:315
  47.7 1.9 %collective-permute-start.9 = (bf16[256,256]{1,0:T(8,128)(2,1)S(1)}, bf16[256,256]{1,0:T(8,128)(2,1)S(1)}, u32[]{:S(2)}, u32[]{:S(2)}) collective-permute-start(bf16[256,256]{1,0:T(8,128)(2,1)S(1)} %get-tuple-element.44), channel_id=1, source_target_pairs={{1,2},{2,1},{3,4},{4,3},{5,6},{6,5},{9,10},{10,9},{11,12},{12,11},... | collective-permute-start | bytes 393224 | tf_op jit(solution)/shard_map/ppermute | solution.py:315
  49.7 0.0 collective-permute-done.6.wrap1_ref
  49.7 0.7 %collective-permute-start.7 = (bf16[256,256]{1,0:T(8,128)(2,1)S(1)}, bf16[256,256]{1,0:T(8,128)(2,1)S(1)}, u32[]{:S(2)}, u32[]{:S(2)}) collective-permute-start(bf16[256,256]{1,0:T(8,128)(2,1)S(1)} %collective-permute-done.6.wrap1_ref), channel_id=1, source_target_pairs={{992,1000},{993,1001},{994,1002},{995,1003},{996,1004},{997,1005},... | collective-permute-start | bytes 393224 | tf_op jit(solution)/shard_map/ppermute | solution.py:315
  50.3 0.7 %collective-permute-done.8.near_ref = bf16[256,256]{1,0:T(8,128)(2,1)S(1)} collective-permute-done((bf16[256,256]{1,0:T(8,128)(2,1)S(1)}, bf16[256,256]{1,0:T(8,128)(2,1)S(1)}, u32[]{:S(2)}, u32[]{:S(2)}) %collective-permute-start.8) | collective-permute-done | bytes 131104 | tf_op jit(solution)/shard_map/ppermute | solution.py:315
  51.0 3.6 %collective-permute-done.9.far_ref = bf16[256,256]{1,0:T(8,128)(2,1)S(1)} collective-permute-done((bf16[256,256]{1,0:T(8,128)(2,1)S(1)}, bf16[256,256]{1,0:T(8,128)(2,1)S(1)}, u32[]{:S(2)}, u32[]{:S(2)}) %collective-permute-start.9) | collective-permute-done | bytes 131104 | tf_op jit(solution)/shard_map/ppermute | solution.py:315
  54.7 0.0 collective-permute-done.7.wrap2_ref
  54.7 1.0 %shard_map.79 = f32[32,128]{1,0:T(8,128)} custom-call(s32[1]{0:T(128)} %bitcast.9.offset_ref, bf16[256,256]{1,0:T(8,128)(2,1)S(1)} %collective-permute-done.6.wrap1_ref, bf16[256,256]{1,0:T(8,128)(2,1)S(1)} %collective-permute-done.7.wrap2_ref, bf16[256,256]{1,0:T(8,128)(2,1)S(1)} %collective-permute-done.8.near_ref, ...), custom_call_target="tpu_custom_call" | custom-call | flops 1000000 | bytes 16384 | tf_op jit(solution)/shard_map/pallas_call | solution.py:303
Async XLA Ops:
  0.0 7.9 %copy-start.2 = (bf16[2,320,256]{2,1,0:T(8,128)(2,1)S(1)}, bf16[2,320,256]{2,1,0:T(8,128)(2,1)}, u32[]{:S(2)}) copy-start(bf16[2,320,256]{2,1,0:T(8,128)(2,1)} %constant.6.clone.text_ref) | copy-start | bytes 983044
  0.0 14.5 %collective-permute-start = (bf16[256,256]{1,0:T(8,128)(2,1)}, bf16[256,256]{1,0:T(8,128)(2,1)S(1)}, u32[]{:S(2)}, u32[]{:S(2)}) collective-permute-start(bf16[256,256]{1,0:T(8,128)(2,1)} %bitcast.10), channel_id=1, source_target_pairs={{1008,0},{1009,1},{1010,2},{1011,3},{1012,4},{1013,5},{1014,6},{10... | collective-permute-start | bytes 393224 | tf_op jit(solution)/shard_map/ppermute | solution.py:315
  3.3 8.6 %collective-permute-start.2 = (bf16[256,256]{1,0:T(8,128)(2,1)S(1)}, bf16[256,256]{1,0:T(8,128)(2,1)S(1)}, u32[]{:S(2)}, u32[]{:S(2)}) collective-permute-start(bf16[256,256]{1,0:T(8,128)(2,1)S(1)} %get-tuple-element.28), channel_id=1, source_target_pairs={{0,32},{1,33},{2,34},{3,35},{4,36},{5,37},{6,38},{7,39},{8,40},{9,... | collective-permute-start | bytes 393224 | tf_op jit(solution)/shard_map/ppermute | solution.py:315
  7.3 4.6 %collective-permute-start.3 = (bf16[256,256]{1,0:T(8,128)(2,1)S(1)}, bf16[256,256]{1,0:T(8,128)(2,1)S(1)}, u32[]{:S(2)}, u32[]{:S(2)}) collective-permute-start(bf16[256,256]{1,0:T(8,128)(2,1)S(1)} %get-tuple-element.29), channel_id=1, source_target_pairs={{32,64},{33,65},{34,66},{35,67},{36,68},{37,69},{38,70},{39,71},{4... | collective-permute-start | bytes 393224 | tf_op jit(solution)/shard_map/ppermute | solution.py:315
  11.9 12.9 %copy-start.1 = (bf16[1,256,256]{2,1,0:T(8,128)(2,1)S(1)}, bf16[1,256,256]{2,1,0:T(8,128)(2,1)}, u32[]{:S(2)}) copy-start(bf16[1,256,256]{2,1,0:T(8,128)(2,1)} %param.10) | copy-start | bytes 393220
  11.9 12.9 %copy-start.3 = (bf16[2,64,32]{2,1,0:T(8,128)(2,1)S(1)}, bf16[2,64,32]{2,1,0:T(8,128)(2,1)}, u32[]{:S(2)}) copy-start(bf16[2,64,32]{2,1,0:T(8,128)(2,1)} %constant.8.clone.add_ref) | copy-start | bytes 24580
  12.2 12.5 %collective-permute-start.4 = (bf16[256,256]{1,0:T(8,128)(2,1)S(1)}, bf16[256,256]{1,0:T(8,128)(2,1)S(1)}, u32[]{:S(2)}, u32[]{:S(2)}) collective-permute-start(bf16[256,256]{1,0:T(8,128)(2,1)S(1)} %get-tuple-element.31), channel_id=1, source_target_pairs={{0,8},{1,9},{2,10},{3,11},{4,12},{5,13},{6,14},{7,15},{8,0},{9,1},... | collective-permute-start | bytes 393224 | tf_op jit(solution)/shard_map/ppermute | solution.py:315
  14.5 10.2 %collective-permute-start.1 = (bf16[256,256]{1,0:T(8,128)(2,1)S(1)}, bf16[256,256]{1,0:T(8,128)(2,1)S(1)}, u32[]{:S(2)}, u32[]{:S(2)}) collective-permute-start(bf16[256,256]{1,0:T(8,128)(2,1)S(1)} %collective-permute-done.tile1_ref), channel_id=1, source_target_pairs={{0,8},{1,9},{2,10},{3,11},{4,12},{5,13},{6,14},{7,15},{8,0},{9,1},... | collective-permute-start | bytes 393224 | tf_op jit(solution)/shard_map/ppermute | solution.py:315
  23.1 1.6 %collective-permute-start.5 = (bf16[256,256]{1,0:T(8,128)(2,1)S(1)}, bf16[256,256]{1,0:T(8,128)(2,1)S(1)}, u32[]{:S(2)}, u32[]{:S(2)}) collective-permute-start(bf16[256,256]{1,0:T(8,128)(2,1)S(1)} %get-tuple-element.32), channel_id=1, source_target_pairs={{8,16},{9,17},{10,18},{11,19},{12,20},{13,21},{14,22},{15,23},{16,... | collective-permute-start | bytes 393224 | tf_op jit(solution)/shard_map/ppermute | solution.py:315
  24.8 20.3 %copy-start = (bf16[4,32,32]{2,1,0:T(8,128)(2,1)S(1)}, bf16[4,32,32]{2,1,0:T(8,128)(2,1)}, u32[]{:S(2)}) copy-start(bf16[4,32,32]{2,1,0:T(8,128)(2,1)} %constant.7.clone.mzh_ref) | copy-start | bytes 24580
  26.7 22.9 %collective-permute-start.6 = (bf16[256,256]{1,0:T(8,128)(2,1)S(1)}, bf16[256,256]{1,0:T(8,128)(2,1)S(1)}, u32[]{:S(2)}, u32[]{:S(2)}) collective-permute-start(bf16[256,256]{1,0:T(8,128)(2,1)S(1)} %get-tuple-element.40), channel_id=1, source_target_pairs={{24,1000},{16,1016},{25,1001},{17,1017},{26,1002},{18,1018},{27,10... | collective-permute-start | bytes 393224 | tf_op jit(solution)/shard_map/ppermute | solution.py:315
  45.3 5.7 %collective-permute-start.8 = (bf16[256,256]{1,0:T(8,128)(2,1)S(1)}, bf16[256,256]{1,0:T(8,128)(2,1)S(1)}, u32[]{:S(2)}, u32[]{:S(2)}) collective-permute-start(bf16[256,256]{1,0:T(8,128)(2,1)S(1)} %get-tuple-element.43), channel_id=1, source_target_pairs={{0,1},{1,0},{2,3},{3,2},{4,5},{5,4},{6,7},{7,6},{8,9},{9,8},{10,11... | collective-permute-start | bytes 393224 | tf_op jit(solution)/shard_map/ppermute | solution.py:315
  47.7 6.9 %collective-permute-start.9 = (bf16[256,256]{1,0:T(8,128)(2,1)S(1)}, bf16[256,256]{1,0:T(8,128)(2,1)S(1)}, u32[]{:S(2)}, u32[]{:S(2)}) collective-permute-start(bf16[256,256]{1,0:T(8,128)(2,1)S(1)} %get-tuple-element.44), channel_id=1, source_target_pairs={{1,2},{2,1},{3,4},{4,3},{5,6},{6,5},{9,10},{10,9},{11,12},{12,11},... | collective-permute-start | bytes 393224 | tf_op jit(solution)/shard_map/ppermute | solution.py:315
  49.7 5.0 %collective-permute-start.7 = (bf16[256,256]{1,0:T(8,128)(2,1)S(1)}, bf16[256,256]{1,0:T(8,128)(2,1)S(1)}, u32[]{:S(2)}, u32[]{:S(2)}) collective-permute-start(bf16[256,256]{1,0:T(8,128)(2,1)S(1)} %collective-permute-done.6.wrap1_ref), channel_id=1, source_target_pairs={{992,1000},{993,1001},{994,1002},{995,1003},{996,1004},{997,1005},... | collective-permute-start | bytes 393224 | tf_op jit(solution)/shard_map/ppermute | solution.py:315

commit v3 on v2

--- a/solution.py
+++ b/solution.py
@@ -91,13 +91,13 @@
 def wrap_pairs(shape):
     nx, ny, nz = shape
     index = lambda x, y, z: int(np.ravel_multi_index((x, y, z), shape))
-    return [(index(0, ny - y, z), index(nx - 1, y if y == 1 else ny - 1, z)) if y == 1 else (index(0, ny - 2, z), index(nx - 1, ny - 1, z)) for z in range(nz) for y in (1, 2)]
+    return [(index(0, ny - 2 + y, z), index(nx - 1, y, z)) for y in range(2) for z in range(nz)]
 
 
 def last_pairs(shape):
     nx, ny, nz = shape
     index = lambda y, z: int(np.ravel_multi_index((nx - 1, y, z), shape))
-    return [(index(y, z), index(y ^ 1, z)) for y in range(ny) for z in range(nz)]
+    return [(index(y, z), index(y + ny - 2, z)) for y in range(2) for z in range(nz)]
 
 
 def parity(axis):
@@ -108,11 +108,13 @@
     return lax.broadcasted_iota(jnp.int32, (rows, lanes), 1) < count_ref[0]
 
 
-def faces_kernel(count_ref, c_hbm, near_ref, far_ref, planes_ref, sem):
+def faces_kernel(count_ref, c_hbm, text_hbm, near_ref, far_ref, planes_ref, text_ref, sem):
     last_k, rows = c_hbm.shape[1] - 1, c_hbm.shape[2]
     copies = [pltpu.make_async_copy(c_hbm.at[:, k], planes_ref.at[i], sem.at[i]) for i, k in enumerate((0, last_k))]
+    table = pltpu.make_async_copy(text_hbm.at[parity("gz")], text_ref, sem.at[2])
     for copy in copies:
         copy.start()
+    table.start()
     even = parity("gx") == 0
     mask = lane_mask(count_ref, rows, c_hbm.shape[3])
     for copy in copies:
@@ -123,6 +125,7 @@
         first, last = jnp.where(mask, first, 0.0), jnp.where(mask, last, 0.0)
         near_ref[b * rows : (b + 1) * rows] = jnp.where(even, last, first).astype(BF16)
         far_ref[b * rows : (b + 1) * rows] = jnp.where(even, first, last).astype(BF16)
+    table.wait()
 
 
 def split_cells(r, i, mid_ref, yside_ref, z_ref, zside_ref):
@@ -134,20 +137,14 @@
     zside_ref[i] = r[cells + sent :]
 
 
-def inner_kernel(count_ref, c_hbm, text_ref, x_ref, mid_ref, yside_ref, z_ref, zside_ref, c_ref, sem):
-    planes, rows = c_hbm.shape[1], c_hbm.shape[2]
-    copies = [pltpu.make_async_copy(c_hbm.at[:, k], c_ref.at[k], sem.at[k]) for k in range(planes)]
-    for copy in copies:
-        copy.start()
-    mask = lane_mask(count_ref, rows, c_hbm.shape[3])
-    pz = parity("gz")
-    copies[0].wait()
+def inner_kernel(count_ref, c_ref, text_ref, x_ref, mid_ref, yside_ref, z_ref, zside_ref):
+    planes, rows = c_ref.shape[1], c_ref.shape[2]
+    mask = lane_mask(count_ref, rows, c_ref.shape[3])
     for m in range(1, planes):
-        copies[m].wait()
         odd, even = [], []
         for b in range(4):
-            s0, w0 = c_ref[m - 1, b].astype(F32), c_ref[m - 1, 4 + b].astype(F32)
-            s1, w1 = c_ref[m, b].astype(F32), c_ref[m, 4 + b].astype(F32)
+            s0, w0 = c_ref[b, m - 1].astype(F32), c_ref[4 + b, m - 1].astype(F32)
+            s1, w1 = c_ref[b, m].astype(F32), c_ref[4 + b, m].astype(F32)
             o = FILT[2] * s0 + WAVE[2] * w0 + FILT[0] * s1 + WAVE[0] * w1
             e = FILT[3] * s0 + WAVE[3] * w0 + FILT[1] * s1 + WAVE[1] * w1
             odd.append(jnp.where(mask, o, 0.0).astype(BF16))
@@ -155,7 +152,7 @@
         for i, parts in ((2 * m - 2, odd), (2 * m - 1, even)):
             x = jnp.concatenate(parts, axis=0)
             x_ref[i] = x
-            split_cells(jnp.dot(text_ref[pz], x, preferred_element_type=F32), i, mid_ref, yside_ref, z_ref, zside_ref)
+            split_cells(jnp.dot(text_ref[...], x, preferred_element_type=F32), i, mid_ref, yside_ref, z_ref, zside_ref)
 
 
 def edge_kernel(count_ref, planes_ref, near_ref, far_ref, x_ref, edge_ref, ynear_ref, yfar_ref, *, cy, cz):
@@ -188,9 +185,8 @@
 
 
 def edge_cells_kernel(edge_ref, text_ref, *out_refs):
-    pz = parity("gz")
     for i in range(2):
-        split_cells(jnp.dot(text_ref[pz], edge_ref[i], preferred_element_type=F32), i, *out_refs)
+        split_cells(jnp.dot(text_ref[...], edge_ref[i], preferred_element_type=F32), i, *out_refs)
 
 
 def at(n, fine, inner_ref, edge_ref):
@@ -227,15 +223,16 @@
     return jnp.concatenate([jnp.sum(part, axis=0, keepdims=True) for part in parts], axis=1)
 
 
-def density_kernel(offset_ref, own_ref, tile1_ref, tile2_ref, ynear_ref, yfar_ref, add_ref, *rest):
-    mid_ref, yside_ref, zside_ref, mide_ref, ysidee_ref, zsidee_ref, phi_ref, side_ref, d_ref, k_ref, own_out_ref = rest
-    own_out_ref[...] = own_ref[...]
+def density_kernel(offset_ref, own_ref, tile1_ref, tile2_ref, wrap1_ref, wrap2_ref, ynear_ref, yfar_ref, add_ref, *rest):
+    mid_ref, yside_ref, zside_ref, mide_ref, ysidee_ref, zsidee_ref, side_ref, d_ref, k_ref = rest
     even = parity("gy") == 0
     offset = offset_ref[0]
     first, second = tile1_ref[...], tile2_ref[...]
     before, after = jnp.where(even, first, second), jnp.where(even, second, first)
+    wrapped = jnp.where(lax.axis_index("gy") < 2, wrap1_ref[...], wrap2_ref[...])
+    after = jnp.where(lax.axis_index("gx") == lax.axis_size("gx") - 1, wrapped, after)
     k_ref[...] = jnp.where(offset == -1, before, jnp.where(offset == 1, after, own_ref[...]))
-    fine = phi_ref.shape[0]
+    fine = d_ref.shape[0]
     step = ynear_ref.shape[0] // fine
     fz = yside_ref.shape[1] // 2
     for n in range(fine):
@@ -245,32 +242,11 @@
         ends = (at(n, fine, yside_ref, ysidee_ref) + more[: 2 * fz]).astype(BF16)
         side_ref[n] = at(n, fine, zside_ref, zsidee_ref) + more[2 * fz :]
         phi = jnp.concatenate([ends[:fz], at(n, fine, mid_ref, mide_ref), ends[fz:]], axis=0)
-        phi_ref[n] = phi
-
-    @pl.when(~in_last_domain())
-    def _():
-        for n in range(fine):
-            d_ref[n : n + 1] = row_of(slot_sums(phi_ref[n], k_ref[...], 128))
-
-
-def in_last_domain():
-    return lax.axis_index("gx") == lax.axis_size("gx") - 1
-
-
-def finish_kernel(offset_ref, wrap1_ref, wrap2_ref, near_ref, far_ref, phi_ref, side_ref, d_ref, k_ref, out_ref, tile_ref, dens_ref):
+        d_ref[n : n + 1] = row_of(slot_sums(phi, k_ref[...], 128))
+
+
+def finish_kernel(near_ref, far_ref, side_ref, d_ref, tile_ref, out_ref):
     fine, cells = d_ref.shape
-    tile_ref[...] = k_ref[...]
-    dens_ref[...] = d_ref[...]
-
-    @pl.when(in_last_domain())
-    def _():
-        wrapped = jnp.where(parity("gy") == 0, wrap2_ref[...], wrap1_ref[...])
-        tile_ref[...] = jnp.where(offset_ref[0] == 1, wrapped, k_ref[...])
-
-        @pl.loop(0, fine)
-        def _(n):
-            dens_ref[pl.ds(n, 1)] = row_of(slot_sums(phi_ref[n], tile_ref[...], 128))
-
     even = parity("gz") == 0
     fy = near_ref.shape[0] // fine
     fz = cells // fy
@@ -290,7 +266,7 @@
         for i in range(some):
             n = part * some + i
             new = jnp.sum(jnp.where(mine, sums[i * 2 * fy : (i + 1) * 2 * fy], 0.0), axis=0, keepdims=True)
-            new = jnp.where(side, new, dens_ref[n : n + 1])
+            new = jnp.where(side, new, d_ref[n : n + 1])
             for j in range(cells // 128):
                 out_ref[n * (cells // 128) + j : n * (cells // 128) + j + 1] = new[:, j * 128 : (j + 1) * 128]
 
@@ -332,9 +308,9 @@
     own = kernel.reshape(kernel.shape[1:])
     face = vmem((4 * rows, slots), BF16)
 
-    xnear, xfar, planes = call(
-        faces_kernel, [face, face, vmem((2, bands, rows, slots), BF16)], [count, c], 1,
-        scratch=[pltpu.SemaphoreType.DMA((2,))], hbm=(1,),
+    xnear, xfar, planes, text = call(
+        faces_kernel, [face, face, vmem((2, bands, rows, slots), BF16), vmem(text.shape[1:], BF16)], [count, c, text], 1,
+        scratch=[pltpu.SemaphoreType.DMA((3,))], hbm=(1, 2),
     )
     xfar = send(xfar, far[0])
     xnear = send(xnear, near[0])
@@ -348,7 +324,7 @@
 
     x, mid, yside, z, zside = call(
         inner_kernel, [vmem((fx - 2, 4 * rows, slots), BF16)] + cell_outs(fx - 2), [count, c, text], 1,
-        scratch=[vmem((cx, bands, rows, slots), BF16), pltpu.SemaphoreType.DMA((cx,))], flops=2e9, hbm=(1,),
+        flops=2e9,
     )
     yshape = vmem((fx * 2 * cz, slots), BF16)
     edge, ynear, yfar = call(
@@ -357,25 +333,19 @@
     )
     yfar = send(yfar, far[1])
     ynear = send(ynear, near[1])
+    wrap1 = send(own, wrap_pairs(shape))
     mide, ysidee, ze, zsidee = call(edge_cells_kernel, cell_outs(2), [edge, text], flops=3e8)
     zshape = vmem((fx * 2 * cy, slots), BF16)
     znear, zfar = call(zfaces_kernel, [zshape, zshape], [ynear, yfar, z, ze, mzh])
     znear = send(znear, near[2])
     zfar = send(zfar, far[2])
     tile2 = send(tile1, near[1])
-    square = vmem((slots, slots), BF16)
-    phi, side, d, tile, own_late = call(
-        density_kernel,
-        [vmem((fx, cells, slots), BF16), vmem((fx, 4 * cy, slots), F32), vmem((fx, cells), F32), square, square],
-        [offset, own, tile1, tile2, ynear, yfar, add, mid, yside, zside, mide, ysidee, zsidee], 1, flops=2e9,
-    )
-    wrap1 = send(own_late, wrap_pairs(shape))
     wrap2 = send(wrap1, last_pairs(shape))
-    (out,) = call(
-        finish_kernel, [jax.ShapeDtypeStruct((fx * cells // 128, 128), F32)],
-        [offset, wrap1, wrap2, znear, zfar, phi, side, d, tile], 1,
-        scratch=[vmem((slots, slots), BF16), vmem((fx, cells), F32)],
-    )
+    side, d, tile = call(
+        density_kernel, [vmem((fx, 4 * cy, slots), F32), vmem((fx, cells), F32), vmem((slots, slots), BF16)],
+        [offset, own, tile1, tile2, wrap1, wrap2, ynear, yfar, add, mid, yside, zside, mide, ysidee, zsidee], 1, flops=2e9,
+    )
+    (out,) = call(finish_kernel, [jax.ShapeDtypeStruct((fx * cells // 128, 128), F32)], [znear, zfar, side, d, tile])
     return out.reshape(1, 1, 1, -1)
 
 

time: 56.1 us -> 57.9 us (1.032)
  the two profiles are of different devices: /device:TPU:73 before, /device:TPU:58 now
where the time goes in v3:
time: 57.9 us; the launch traced here: 57.5 us
  starting transfers between devices  38.5 us (66%)
  waiting for transfers between devices  9.26 us (16%)
  Pallas kernels  8.23 us (14%)
  between operations  1.5 us (3%)
    ppermute x10, starting transfers between devices, send(): return lax.ppermute(value, AXES, pairs)  38.5 us
    ppermute x10, waiting for transfers between devices, send(): return lax.ppermute(value, AXES, pairs)  9.26 us
    pallas_call x7, Pallas kernels, call(): pl.pallas_call(body, out_shape=tuple(outs), in_specs=specs, out_specs=tup...  8.23 us
  transfers between devices with their start and end apart: 10, of which 2 were waited for; matrix products, arithmetic and copies ran while one was open for 0% of the time, Pallas kernels for 13%

profile of v3, /device:TPU:58, one launch (start us, length us, event | category | flops | bytes accessed | tf_op | source)
XLA Modules:
  0.0 57.5 jit_solution(9313373871132090644)
XLA Ops:
  0.0 0.0 copy-start
  0.0 2.6 %collective-permute-start.6 = (bf16[256,256]{1,0:T(8,128)(2,1)}, bf16[256,256]{1,0:T(8,128)(2,1)S(1)}, u32[]{:S(2)}, u32[]{:S(2)}) collective-permute-start(bf16[256,256]{1,0:T(8,128)(2,1)} %bitcast.11), channel_id=1, source_target_pairs={{1008,0},{1009,1},{1010,2},{1011,3},{1012,4},{1013,5},{1014,6},{10... | collective-permute-start | bytes 393224 | tf_op jit(solution)/shard_map/ppermute | solution.py:291
  2.6 0.7 %collective-permute-start.8 = (bf16[256,256]{1,0:T(8,128)(2,1)}, bf16[256,256]{1,0:T(8,128)(2,1)S(1)}, u32[]{:S(2)}, u32[]{:S(2)}) collective-permute-start(bf16[256,256]{1,0:T(8,128)(2,1)} %bitcast.12), channel_id=1, source_target_pairs={{16,992},{17,993},{18,994},{19,995},{20,996},{21,997},{22,998},{23... | collective-permute-start | bytes 393224 | tf_op jit(solution)/shard_map/ppermute | solution.py:291
  4.0 1.2 %shard_map.73 = (bf16[256,256]{1,0:T(8,128)(2,1)S(1)}, bf16[256,256]{1,0:T(8,128)(2,1)S(1)}, bf16[2,8,64,256]{3,2,1,0:T(8,128)(2,1)S(1)}, bf16[320,256]{1,0:T(8,128)(2,1)S(1)}) custom-call(s32[1]{0:T(128)} %bitcast.5.count_ref, bf16[8,8,64,256]{3,2,1,0:T(8,128)(2,1)} %bitcast.9, bf16[2,320,256]{2,1,0:T(8,128)(2,1)} %constant.6.clone.text_hbm), custom_call_target="tpu_custom_call" | custom-call | flops 1000000 | bytes 950272 | tf_op jit(solution)/shard_map/pallas_call | solution.py:279
  5.2 19.4 %collective-permute-start = (bf16[256,256]{1,0:T(8,128)(2,1)S(1)}, bf16[256,256]{1,0:T(8,128)(2,1)S(1)}, u32[]{:S(2)}, u32[]{:S(2)}) collective-permute-start(bf16[256,256]{1,0:T(8,128)(2,1)S(1)} %get-tuple-element.27), channel_id=1, source_target_pairs={{0,32},{1,33},{2,34},{3,35},{4,36},{5,37},{6,38},{7,39},{8,40},{9,... | collective-permute-start | bytes 393224 | tf_op jit(solution)/shard_map/ppermute | solution.py:291
  24.5 1.9 %collective-permute-start.1 = (bf16[256,256]{1,0:T(8,128)(2,1)S(1)}, bf16[256,256]{1,0:T(8,128)(2,1)S(1)}, u32[]{:S(2)}, u32[]{:S(2)}) collective-permute-start(bf16[256,256]{1,0:T(8,128)(2,1)S(1)} %get-tuple-element.28), channel_id=1, source_target_pairs={{32,64},{33,65},{34,66},{35,67},{36,68},{37,69},{38,70},{39,71},{4... | collective-permute-start | bytes 393224 | tf_op jit(solution)/shard_map/ppermute | solution.py:291
  26.5 0.0 copy-done
  26.5 1.8 %shard_map.74 = (bf16[14,256,256]{2,1,0:T(8,128)(2,1)S(1)}, bf16[14,224,256]{2,1,0:T(8,128)(2,1)S(1)}, f32[14,32,256]{2,1,0:T(8,128)S(1)}, f32[14,32,256]{2,1,0:T(8,128)S(1)}, f32[14,32,256]{2,1,0:T(8,128)S(1)}) custom-call(s32[1]{0:T(128)} %bitcast.6.count_ref, bf16[8,8,64,256]{3,2,1,0:T(8,128)(2,1)S(1)} %bitcast.10, ...), custom_call_target="tpu_custom_call" | custom-call | flops 2000000000 | bytes 4816896 | tf_op jit(solution)/shard_map/pallas_call | solution.py:279
  28.3 0.0 collective-permute-done.near_ref
  28.3 4.5 %collective-permute-done.1.far_ref = bf16[256,256]{1,0:T(8,128)(2,1)S(1)} collective-permute-done((bf16[256,256]{1,0:T(8,128)(2,1)S(1)}, bf16[256,256]{1,0:T(8,128)(2,1)S(1)}, u32[]{:S(2)}, u32[]{:S(2)}) %collective-permute-start.1) | collective-permute-done | bytes 131104 | tf_op jit(solution)/shard_map/ppermute | solution.py:291
  32.8 0.0 copy-start.1
  32.8 0.0 copy-start.2
  32.8 0.0 copy-start.3
  32.8 0.3 shard_map.75
  33.1 1.9 %collective-permute-start.2 = (bf16[256,256]{1,0:T(8,128)(2,1)S(1)}, bf16[256,256]{1,0:T(8,128)(2,1)S(1)}, u32[]{:S(2)}, u32[]{:S(2)}) collective-permute-start(bf16[256,256]{1,0:T(8,128)(2,1)S(1)} %get-tuple-element.31), channel_id=1, source_target_pairs={{0,8},{1,9},{2,10},{3,11},{4,12},{5,13},{6,14},{7,15},{8,0},{9,1},... | collective-permute-start | bytes 393224 | tf_op jit(solution)/shard_map/ppermute | solution.py:291
  35.0 1.9 %collective-permute-start.3 = (bf16[256,256]{1,0:T(8,128)(2,1)S(1)}, bf16[256,256]{1,0:T(8,128)(2,1)S(1)}, u32[]{:S(2)}, u32[]{:S(2)}) collective-permute-start(bf16[256,256]{1,0:T(8,128)(2,1)S(1)} %get-tuple-element.32), channel_id=1, source_target_pairs={{8,16},{9,17},{10,18},{11,19},{12,20},{13,21},{14,22},{15,23},{16,... | collective-permute-start | bytes 393224 | tf_op jit(solution)/shard_map/ppermute | solution.py:291
  37.0 0.0 collective-permute-done.6.tile1_ref
  37.0 1.9 %collective-permute-start.7 = (bf16[256,256]{1,0:T(8,128)(2,1)S(1)}, bf16[256,256]{1,0:T(8,128)(2,1)S(1)}, u32[]{:S(2)}, u32[]{:S(2)}) collective-permute-start(bf16[256,256]{1,0:T(8,128)(2,1)S(1)} %collective-permute-done.6.tile1_ref), channel_id=1, source_target_pairs={{0,8},{1,9},{2,10},{3,11},{4,12},{5,13},{6,14},{7,15},{8,0},{9,1},... | collective-permute-start | bytes 393224 | tf_op jit(solution)/shard_map/ppermute | solution.py:291
  38.9 0.0 collective-permute-done.8.wrap1_ref
  38.9 0.7 %collective-permute-start.9 = (bf16[256,256]{1,0:T(8,128)(2,1)S(1)}, bf16[256,256]{1,0:T(8,128)(2,1)S(1)}, u32[]{:S(2)}, u32[]{:S(2)}) collective-permute-start(bf16[256,256]{1,0:T(8,128)(2,1)S(1)} %collective-permute-done.8.wrap1_ref), channel_id=1, source_target_pairs={{992,1008},{993,1009},{994,1010},{995,1011},{996,1012},{997,1013},... | collective-permute-start | bytes 393224 | tf_op jit(solution)/shard_map/ppermute | solution.py:291
  40.3 0.2 shard_map.76
  40.5 0.0 collective-permute-done.2.ynear_ref
  40.5 4.7 %collective-permute-done.3.yfar_ref = bf16[256,256]{1,0:T(8,128)(2,1)S(1)} collective-permute-done((bf16[256,256]{1,0:T(8,128)(2,1)S(1)}, bf16[256,256]{1,0:T(8,128)(2,1)S(1)}, u32[]{:S(2)}, u32[]{:S(2)}) %collective-permute-start.3) | collective-permute-done | bytes 131104 | tf_op jit(solution)/shard_map/ppermute | solution.py:291
  45.2 0.0 copy-done.1
  45.2 0.2 shard_map.77
  45.5 2.2 %collective-permute-start.4 = (bf16[256,256]{1,0:T(8,128)(2,1)S(1)}, bf16[256,256]{1,0:T(8,128)(2,1)S(1)}, u32[]{:S(2)}, u32[]{:S(2)}) collective-permute-start(bf16[256,256]{1,0:T(8,128)(2,1)S(1)} %get-tuple-element.36), channel_id=1, source_target_pairs={{0,1},{1,0},{2,3},{3,2},{4,5},{5,4},{6,7},{7,6},{8,9},{9,8},{10,11... | collective-permute-start | bytes 393224 | tf_op jit(solution)/shard_map/ppermute | solution.py:291
  47.7 5.3 %collective-permute-start.5 = (bf16[256,256]{1,0:T(8,128)(2,1)S(1)}, bf16[256,256]{1,0:T(8,128)(2,1)S(1)}, u32[]{:S(2)}, u32[]{:S(2)}) collective-permute-start(bf16[256,256]{1,0:T(8,128)(2,1)S(1)} %get-tuple-element.37), channel_id=1, source_target_pairs={{1,2},{2,1},{3,4},{4,3},{5,6},{6,5},{9,10},{10,9},{11,12},{12,11},... | collective-permute-start | bytes 393224 | tf_op jit(solution)/shard_map/ppermute | solution.py:291
  53.0 0.0 collective-permute-done.7.tile2_ref
  53.0 0.0 collective-permute-done.9.wrap2_ref
  53.0 0.0 copy-done.2
  53.0 0.0 copy-done.3
  53.0 3.5 %shard_map.78 = (f32[16,32,256]{2,1,0:T(8,128)S(1)}, f32[16,256]{1,0:T(8,128)S(1)}, bf16[256,256]{1,0:T(8,128)(2,1)S(1)}) custom-call(s32[1]{0:T(128)} %bitcast.8.offset_ref, bf16[256,256]{1,0:T(8,128)(2,1)S(1)} %bitcast.13, bf16[256,256]{1,0:T(8,128)(2,1)S(1)} %collective-permute-done.6.tile1_ref, bf16[256,256]{1,0:T(8,128)(2,1)S(1)} %collective-permute-done.7.tile2_ref, ...), custom_call_target="tpu_custom_call" | custom-call | flops 2000000000 | bytes 671744 | tf_op jit(solution)/shard_map/pallas_call | solution.py:279
  56.5 0.0 collective-permute-done.4.near_ref
  56.5 0.0 collective-permute-done.5.far_ref
  56.5 1.0 %shard_map.79 = f32[32,128]{1,0:T(8,128)} custom-call(bf16[256,256]{1,0:T(8,128)(2,1)S(1)} %collective-permute-done.4.near_ref, bf16[256,256]{1,0:T(8,128)(2,1)S(1)} %collective-permute-done.5.far_ref, f32[16,32,256]{2,1,0:T(8,128)S(1)} %get-tuple-element.44.side_ref, f32[16,256]{1,0:T(8,128)S(1)} %get-tuple-element.45.d_ref, ...), custom_call_target="tpu_custom_call" | custom-call | flops 1000000 | bytes 16384 | tf_op jit(solution)/shard_map/pallas_call | solution.py:279
Async XLA Ops:
  0.0 26.5 %copy-start = (bf16[8,8,8,8,256]{4,3,2,1,0:T(8,128)(2,1)S(1)}, bf16[8,8,8,8,256]{4,3,2,1,0:T(8,128)(2,1)}, u32[]{:S(2)}) copy-start(bf16[8,8,8,8,256]{4,3,2,1,0:T(8,128)(2,1)} %param.7) | copy-start | bytes 6291460
  0.0 37.0 %collective-permute-start.6 = (bf16[256,256]{1,0:T(8,128)(2,1)}, bf16[256,256]{1,0:T(8,128)(2,1)S(1)}, u32[]{:S(2)}, u32[]{:S(2)}) collective-permute-start(bf16[256,256]{1,0:T(8,128)(2,1)} %bitcast.11), channel_id=1, source_target_pairs={{1008,0},{1009,1},{1010,2},{1011,3},{1012,4},{1013,5},{1014,6},{10... | collective-permute-start | bytes 393224 | tf_op jit(solution)/shard_map/ppermute | solution.py:291
  2.6 36.3 %collective-permute-start.8 = (bf16[256,256]{1,0:T(8,128)(2,1)}, bf16[256,256]{1,0:T(8,128)(2,1)S(1)}, u32[]{:S(2)}, u32[]{:S(2)}) collective-permute-start(bf16[256,256]{1,0:T(8,128)(2,1)} %bitcast.12), channel_id=1, source_target_pairs={{16,992},{17,993},{18,994},{19,995},{20,996},{21,997},{22,998},{23... | collective-permute-start | bytes 393224 | tf_op jit(solution)/shard_map/ppermute | solution.py:291
  5.2 23.1 %collective-permute-start = (bf16[256,256]{1,0:T(8,128)(2,1)S(1)}, bf16[256,256]{1,0:T(8,128)(2,1)S(1)}, u32[]{:S(2)}, u32[]{:S(2)}) collective-permute-start(bf16[256,256]{1,0:T(8,128)(2,1)S(1)} %get-tuple-element.27), channel_id=1, source_target_pairs={{0,32},{1,33},{2,34},{3,35},{4,36},{5,37},{6,38},{7,39},{8,40},{9,... | collective-permute-start | bytes 393224 | tf_op jit(solution)/shard_map/ppermute | solution.py:291
  24.5 8.3 %collective-permute-start.1 = (bf16[256,256]{1,0:T(8,128)(2,1)S(1)}, bf16[256,256]{1,0:T(8,128)(2,1)S(1)}, u32[]{:S(2)}, u32[]{:S(2)}) collective-permute-start(bf16[256,256]{1,0:T(8,128)(2,1)S(1)} %get-tuple-element.28), channel_id=1, source_target_pairs={{32,64},{33,65},{34,66},{35,67},{36,68},{37,69},{38,70},{39,71},{4... | collective-permute-start | bytes 393224 | tf_op jit(solution)/shard_map/ppermute | solution.py:291
  32.8 12.4 %copy-start.1 = (bf16[4,32,32]{2,1,0:T(8,128)(2,1)S(1)}, bf16[4,32,32]{2,1,0:T(8,128)(2,1)}, u32[]{:S(2)}) copy-start(bf16[4,32,32]{2,1,0:T(8,128)(2,1)} %constant.7.clone.mzh_ref) | copy-start | bytes 24580
  32.8 20.2 %copy-start.2 = (bf16[1,256,256]{2,1,0:T(8,128)(2,1)S(1)}, bf16[1,256,256]{2,1,0:T(8,128)(2,1)}, u32[]{:S(2)}) copy-start(bf16[1,256,256]{2,1,0:T(8,128)(2,1)} %param.10) | copy-start | bytes 393220
  32.8 20.2 %copy-start.3 = (bf16[2,64,32]{2,1,0:T(8,128)(2,1)S(1)}, bf16[2,64,32]{2,1,0:T(8,128)(2,1)}, u32[]{:S(2)}) copy-start(bf16[2,64,32]{2,1,0:T(8,128)(2,1)} %constant.8.clone.add_ref) | copy-start | bytes 24580
  33.1 7.4 %collective-permute-start.2 = (bf16[256,256]{1,0:T(8,128)(2,1)S(1)}, bf16[256,256]{1,0:T(8,128)(2,1)S(1)}, u32[]{:S(2)}, u32[]{:S(2)}) collective-permute-start(bf16[256,256]{1,0:T(8,128)(2,1)S(1)} %get-tuple-element.31), channel_id=1, source_target_pairs={{0,8},{1,9},{2,10},{3,11},{4,12},{5,13},{6,14},{7,15},{8,0},{9,1},... | collective-permute-start | bytes 393224 | tf_op jit(solution)/shard_map/ppermute | solution.py:291
  35.0 10.2 %collective-permute-start.3 = (bf16[256,256]{1,0:T(8,128)(2,1)S(1)}, bf16[256,256]{1,0:T(8,128)(2,1)S(1)}, u32[]{:S(2)}, u32[]{:S(2)}) collective-permute-start(bf16[256,256]{1,0:T(8,128)(2,1)S(1)} %get-tuple-element.32), channel_id=1, source_target_pairs={{8,16},{9,17},{10,18},{11,19},{12,20},{13,21},{14,22},{15,23},{16,... | collective-permute-start | bytes 393224 | tf_op jit(solution)/shard_map/ppermute | solution.py:291
  37.0 16.0 %collective-permute-start.7 = (bf16[256,256]{1,0:T(8,128)(2,1)S(1)}, bf16[256,256]{1,0:T(8,128)(2,1)S(1)}, u32[]{:S(2)}, u32[]{:S(2)}) collective-permute-start(bf16[256,256]{1,0:T(8,128)(2,1)S(1)} %collective-permute-done.6.tile1_ref), channel_id=1, source_target_pairs={{0,8},{1,9},{2,10},{3,11},{4,12},{5,13},{6,14},{7,15},{8,0},{9,1},... | collective-permute-start | bytes 393224 | tf_op jit(solution)/shard_map/ppermute | solution.py:291
  38.9 14.1 %collective-permute-start.9 = (bf16[256,256]{1,0:T(8,128)(2,1)S(1)}, bf16[256,256]{1,0:T(8,128)(2,1)S(1)}, u32[]{:S(2)}, u32[]{:S(2)}) collective-permute-start(bf16[256,256]{1,0:T(8,128)(2,1)S(1)} %collective-permute-done.8.wrap1_ref), channel_id=1, source_target_pairs={{992,1008},{993,1009},{994,1010},{995,1011},{996,1012},{997,1013},... | collective-permute-start | bytes 393224 | tf_op jit(solution)/shard_map/ppermute | solution.py:291
  45.5 11.0 %collective-permute-start.4 = (bf16[256,256]{1,0:T(8,128)(2,1)S(1)}, bf16[256,256]{1,0:T(8,128)(2,1)S(1)}, u32[]{:S(2)}, u32[]{:S(2)}) collective-permute-start(bf16[256,256]{1,0:T(8,128)(2,1)S(1)} %get-tuple-element.36), channel_id=1, source_target_pairs={{0,1},{1,0},{2,3},{3,2},{4,5},{5,4},{6,7},{7,6},{8,9},{9,8},{10,11... | collective-permute-start | bytes 393224 | tf_op jit(solution)/shard_map/ppermute | solution.py:291
  47.7 8.8 %collective-permute-start.5 = (bf16[256,256]{1,0:T(8,128)(2,1)S(1)}, bf16[256,256]{1,0:T(8,128)(2,1)S(1)}, u32[]{:S(2)}, u32[]{:S(2)}) collective-permute-start(bf16[256,256]{1,0:T(8,128)(2,1)S(1)} %get-tuple-element.37), channel_id=1, source_target_pairs={{1,2},{2,1},{3,4},{4,3},{5,6},{6,5},{9,10},{10,9},{11,12},{12,11},... | collective-permute-start | bytes 393224 | tf_op jit(solution)/shard_map/ppermute | solution.py:291

commit v4 on v3

--- a/solution.py
+++ b/solution.py
@@ -78,26 +78,30 @@
 
 def tile_pairs(shape):
     nx, ny, _ = shape
-    index = lambda x, y, z: int(np.ravel_multi_index((x % nx, y % ny, z), shape))
     out = []
     for x, y, z in np.ndindex(*shape):
         source = x - 1 if y % 2 == 0 else x + 1
-        if source < nx:
-            crosses = (source % nx) // 4 != x // 4
-            out.append((index(source, y + 2 if crosses else y, z), index(x, y, z)))
+        if 0 <= source < nx:
+            place = (source, (y + ny // 2) % ny if source // 4 != x // 4 else y, z)
+            out.append((at_place(shape, *place), at_place(shape, x, y, z)))
     return out
 
 
-def wrap_pairs(shape):
+def at_place(shape, x, y, z):
+    return int(np.ravel_multi_index((x, y, z), shape))
+
+
+def round_pairs(shape):
     nx, ny, nz = shape
-    index = lambda x, y, z: int(np.ravel_multi_index((x, y, z), shape))
-    return [(index(0, ny - 2 + y, z), index(nx - 1, y, z)) for y in range(2) for z in range(nz)]
-
-
-def last_pairs(shape):
-    nx, ny, nz = shape
-    index = lambda y, z: int(np.ravel_multi_index((nx - 1, y, z), shape))
-    return [(index(y, z), index(y + ny - 2, z)) for y in range(2) for z in range(nz)]
+    up, down1, down2 = [], [], []
+    stops = ((3, 15, 1, 1), (2, 12, 3, 3))
+    for z in range(nz):
+        for y in (0, 2):
+            up.append((at_place(shape, nx - 1, (y + 2) % ny, z), at_place(shape, 0, y, z)))
+        for y, stop_x, stop_y, last_y in stops:
+            down1.append((at_place(shape, 0, y, z), at_place(shape, stop_x, stop_y, z)))
+            down2.append((at_place(shape, stop_x, stop_y, z), at_place(shape, nx - 1, last_y, z)))
+    return up, down1, down2
 
 
 def parity(axis):
@@ -223,14 +227,12 @@
     return jnp.concatenate([jnp.sum(part, axis=0, keepdims=True) for part in parts], axis=1)
 
 
-def density_kernel(offset_ref, own_ref, tile1_ref, tile2_ref, wrap1_ref, wrap2_ref, ynear_ref, yfar_ref, add_ref, *rest):
-    mid_ref, yside_ref, zside_ref, mide_ref, ysidee_ref, zsidee_ref, side_ref, d_ref, k_ref = rest
+def density_kernel(offset_ref, own_ref, tile1_ref, tile2_ref, ynear_ref, yfar_ref, add_ref, *rest):
+    mid_ref, yside_ref, zside_ref, mide_ref, ysidee_ref, zsidee_ref, side_ref, d_ref, k_ref, phi_ref = rest
     even = parity("gy") == 0
     offset = offset_ref[0]
     first, second = tile1_ref[...], tile2_ref[...]
     before, after = jnp.where(even, first, second), jnp.where(even, second, first)
-    wrapped = jnp.where(lax.axis_index("gy") < 2, wrap1_ref[...], wrap2_ref[...])
-    after = jnp.where(lax.axis_index("gx") == lax.axis_size("gx") - 1, wrapped, after)
     k_ref[...] = jnp.where(offset == -1, before, jnp.where(offset == 1, after, own_ref[...]))
     fine = d_ref.shape[0]
     step = ynear_ref.shape[0] // fine
@@ -241,8 +243,9 @@
         more = jnp.dot(add_ref[parity("gy")], halo, preferred_element_type=F32)
         ends = (at(n, fine, yside_ref, ysidee_ref) + more[: 2 * fz]).astype(BF16)
         side_ref[n] = at(n, fine, zside_ref, zsidee_ref) + more[2 * fz :]
-        phi = jnp.concatenate([ends[:fz], at(n, fine, mid_ref, mide_ref), ends[fz:]], axis=0)
-        d_ref[n : n + 1] = row_of(slot_sums(phi, k_ref[...], 128))
+        phi_ref[n] = jnp.concatenate([ends[:fz], at(n, fine, mid_ref, mide_ref), ends[fz:]], axis=0)
+    for n in range(fine):
+        d_ref[n : n + 1] = row_of(slot_sums(phi_ref[n], k_ref[...], 128))
 
 
 def finish_kernel(near_ref, far_ref, side_ref, d_ref, tile_ref, out_ref):
@@ -314,7 +317,9 @@
     )
     xfar = send(xfar, far[0])
     xnear = send(xnear, near[0])
-    tile1 = send(own, tile_pairs(shape))
+    up_pairs, down1_pairs, down2_pairs = round_pairs(shape)
+    up = send(own, up_pairs)
+    down = send(own, down1_pairs)
 
     def cell_outs(n):
         return [
@@ -333,17 +338,19 @@
     )
     yfar = send(yfar, far[1])
     ynear = send(ynear, near[1])
-    wrap1 = send(own, wrap_pairs(shape))
+    down = send(down, down2_pairs)
+    tile1 = send(own, tile_pairs(shape))
     mide, ysidee, ze, zsidee = call(edge_cells_kernel, cell_outs(2), [edge, text], flops=3e8)
     zshape = vmem((fx * 2 * cy, slots), BF16)
     znear, zfar = call(zfaces_kernel, [zshape, zshape], [ynear, yfar, z, ze, mzh])
     znear = send(znear, near[2])
     zfar = send(zfar, far[2])
+    tile1 = tile1 + up + down
     tile2 = send(tile1, near[1])
-    wrap2 = send(wrap1, last_pairs(shape))
     side, d, tile = call(
         density_kernel, [vmem((fx, 4 * cy, slots), F32), vmem((fx, cells), F32), vmem((slots, slots), BF16)],
-        [offset, own, tile1, tile2, wrap1, wrap2, ynear, yfar, add, mid, yside, zside, mide, ysidee, zsidee], 1, flops=2e9,
+        [offset, own, tile1, tile2, ynear, yfar, add, mid, yside, zside, mide, ysidee, zsidee], 1, flops=2e9,
+        scratch=[vmem((fx, cells, slots), BF16)],
     )
     (out,) = call(finish_kernel, [jax.ShapeDtypeStruct((fx * cells // 128, 128), F32)], [znear, zfar, side, d, tile])
     return out.reshape(1, 1, 1, -1)

time: 57.9 us -> 51.2 us (0.88)
  the two profiles are of different devices: /device:TPU:58 before, /device:TPU:76 now
where the time goes in v4:
time: 51.2 us; the launch traced here: 50.8 us
  starting transfers between devices  30.7 us (60%)
  waiting for transfers between devices  12.2 us (24%)
  Pallas kernels  6.41 us (13%)
  between operations  1.52 us (3%)
    ppermute x11, starting transfers between devices, send(): return lax.ppermute(value, AXES, pairs)  30.7 us
    ppermute x11, waiting for transfers between devices, send(): return lax.ppermute(value, AXES, pairs)  12.2 us
    pallas_call x7, Pallas kernels, call(): pl.pallas_call(body, out_shape=tuple(outs), in_specs=specs, out_specs=tup...  6.41 us
  transfers between devices with their start and end apart: 11, of which 4 were waited for; matrix products, arithmetic and copies ran while one was open for 0% of the time, Pallas kernels for 11%

profile of v4, /device:TPU:76, one launch (start us, length us, event | category | flops | bytes accessed | tf_op | source)
XLA Modules:
  0.0 50.8 jit_solution(4435244999633376517)
XLA Ops:
  0.0 0.0 copy-start
  0.0 0.8 %collective-permute-start.8 = (bf16[256,256]{1,0:T(8,128)(2,1)}, bf16[256,256]{1,0:T(8,128)(2,1)S(1)}, u32[]{:S(2)}, u32[]{:S(2)}) collective-permute-start(bf16[256,256]{1,0:T(8,128)(2,1)} %bitcast.11), channel_id=1, source_target_pairs={{24,488},{16,408},{25,489},{17,409},{26,490},{18,410},{27,491},{19... | collective-permute-start | bytes 393224 | tf_op jit(solution)/shard_map/ppermute | solution.py:294
  0.8 2.5 %collective-permute-start.6 = (bf16[256,256]{1,0:T(8,128)(2,1)}, bf16[256,256]{1,0:T(8,128)(2,1)S(1)}, u32[]{:S(2)}, u32[]{:S(2)}) collective-permute-start(bf16[256,256]{1,0:T(8,128)(2,1)} %bitcast.12), channel_id=1, source_target_pairs={{40,8},{41,9},{42,10},{43,11},{44,12},{45,13},{46,14},{47,15},{56,... | collective-permute-start | bytes 393224 | tf_op jit(solution)/shard_map/ppermute | solution.py:294
  3.3 0.7 %collective-permute-start.7 = (bf16[256,256]{1,0:T(8,128)(2,1)}, bf16[256,256]{1,0:T(8,128)(2,1)S(1)}, u32[]{:S(2)}, u32[]{:S(2)}) collective-permute-start(bf16[256,256]{1,0:T(8,128)(2,1)} %bitcast.13), channel_id=1, source_target_pairs={{1008,0},{992,16},{1009,1},{993,17},{1010,2},{994,18},{1011,3},{99... | collective-permute-start | bytes 393224 | tf_op jit(solution)/shard_map/ppermute | solution.py:294
  4.6 1.2 %shard_map.73 = (bf16[256,256]{1,0:T(8,128)(2,1)S(1)}, bf16[256,256]{1,0:T(8,128)(2,1)S(1)}, bf16[2,8,64,256]{3,2,1,0:T(8,128)(2,1)S(1)}, bf16[320,256]{1,0:T(8,128)(2,1)S(1)}) custom-call(s32[1]{0:T(128)} %bitcast.5.count_ref, bf16[8,8,64,256]{3,2,1,0:T(8,128)(2,1)} %bitcast.9, bf16[2,320,256]{2,1,0:T(8,128)(2,1)} %constant.6.clone.text_hbm), custom_call_target="tpu_custom_call" | custom-call | flops 1000000 | bytes 950272 | tf_op jit(solution)/shard_map/pallas_call | solution.py:282
  5.8 5.0 %collective-permute-start = (bf16[256,256]{1,0:T(8,128)(2,1)S(1)}, bf16[256,256]{1,0:T(8,128)(2,1)S(1)}, u32[]{:S(2)}, u32[]{:S(2)}) collective-permute-start(bf16[256,256]{1,0:T(8,128)(2,1)S(1)} %get-tuple-element.27), channel_id=1, source_target_pairs={{0,32},{1,33},{2,34},{3,35},{4,36},{5,37},{6,38},{7,39},{8,40},{9,... | collective-permute-start | bytes 393224 | tf_op jit(solution)/shard_map/ppermute | solution.py:294
  10.8 10.5 %collective-permute-start.1 = (bf16[256,256]{1,0:T(8,128)(2,1)S(1)}, bf16[256,256]{1,0:T(8,128)(2,1)S(1)}, u32[]{:S(2)}, u32[]{:S(2)}) collective-permute-start(bf16[256,256]{1,0:T(8,128)(2,1)S(1)} %get-tuple-element.28), channel_id=1, source_target_pairs={{32,64},{33,65},{34,66},{35,67},{36,68},{37,69},{38,70},{39,71},{4... | collective-permute-start | bytes 393224 | tf_op jit(solution)/shard_map/ppermute | solution.py:294
  21.4 0.0 collective-permute-done.8
  21.4 0.7 %collective-permute-start.9 = (bf16[256,256]{1,0:T(8,128)(2,1)S(1)}, bf16[256,256]{1,0:T(8,128)(2,1)S(1)}, u32[]{:S(2)}, u32[]{:S(2)}) collective-permute-start(bf16[256,256]{1,0:T(8,128)(2,1)S(1)} %collective-permute-done.8), channel_id=1, source_target_pairs={{488,1000},{408,1016},{489,1001},{409,1017},{490,1002},{410,1018},... | collective-permute-start | bytes 393224 | tf_op jit(solution)/shard_map/ppermute | solution.py:294
  22.0 0.0 copy-done
  22.0 1.8 %shard_map.74 = (bf16[14,256,256]{2,1,0:T(8,128)(2,1)S(1)}, bf16[14,224,256]{2,1,0:T(8,128)(2,1)S(1)}, f32[14,32,256]{2,1,0:T(8,128)S(1)}, f32[14,32,256]{2,1,0:T(8,128)S(1)}, f32[14,32,256]{2,1,0:T(8,128)S(1)}) custom-call(s32[1]{0:T(128)} %bitcast.6.count_ref, bf16[8,8,64,256]{3,2,1,0:T(8,128)(2,1)S(1)} %bitcast.10, ...), custom_call_target="tpu_custom_call" | custom-call | flops 2000000000 | bytes 4816896 | tf_op jit(solution)/shard_map/pallas_call | solution.py:282
  23.9 0.0 collective-permute-done.near_ref
  23.9 0.9 %collective-permute-done.1.far_ref = bf16[256,256]{1,0:T(8,128)(2,1)S(1)} collective-permute-done((bf16[256,256]{1,0:T(8,128)(2,1)S(1)}, bf16[256,256]{1,0:T(8,128)(2,1)S(1)}, u32[]{:S(2)}, u32[]{:S(2)}) %collective-permute-start.1) | collective-permute-done | bytes 131104 | tf_op jit(solution)/shard_map/ppermute | solution.py:294
  24.8 0.0 copy-start.1
  24.8 0.3 shard_map.75
  25.1 0.0 copy-start.2
  25.1 0.0 copy-start.3
  25.1 2.1 %collective-permute-start.2 = (bf16[256,256]{1,0:T(8,128)(2,1)S(1)}, bf16[256,256]{1,0:T(8,128)(2,1)S(1)}, u32[]{:S(2)}, u32[]{:S(2)}) collective-permute-start(bf16[256,256]{1,0:T(8,128)(2,1)S(1)} %get-tuple-element.31), channel_id=1, source_target_pairs={{0,8},{1,9},{2,10},{3,11},{4,12},{5,13},{6,14},{7,15},{8,0},{9,1},... | collective-permute-start | bytes 393224 | tf_op jit(solution)/shard_map/ppermute | solution.py:294
  27.2 1.9 %collective-permute-start.3 = (bf16[256,256]{1,0:T(8,128)(2,1)S(1)}, bf16[256,256]{1,0:T(8,128)(2,1)S(1)}, u32[]{:S(2)}, u32[]{:S(2)}) collective-permute-start(bf16[256,256]{1,0:T(8,128)(2,1)S(1)} %get-tuple-element.32), channel_id=1, source_target_pairs={{8,16},{9,17},{10,18},{11,19},{12,20},{13,21},{14,22},{15,23},{16,... | collective-permute-start | bytes 393224 | tf_op jit(solution)/shard_map/ppermute | solution.py:294
  29.1 0.0 collective-permute-done.6
  29.1 0.0 collective-permute-done.7
  29.1 0.0 collective-permute-done.9
  29.2 1.9 %collective-permute-start.10 = (bf16[256,256]{1,0:T(8,128)(2,1)S(1)}, bf16[256,256]{1,0:T(8,128)(2,1)S(1)}, u32[]{:S(2)}, u32[]{:S(2)}) collective-permute-start(bf16[256,256]{1,0:T(8,128)(2,1)S(1)} %add_add_fusion.tile1_ref), channel_id=1, source_target_pairs={{0,8},{1,9},{2,10},{3,11},{4,12},{5,13},{6,14},{7,15},{8,0},{9,1},... | collective-permute-start | bytes 393224 | tf_op jit(solution)/shard_map/ppermute | solution.py:294
  31.8 0.2 shard_map.76
  32.0 0.0 collective-permute-done.2.ynear_ref
  32.0 6.8 %collective-permute-done.3.yfar_ref = bf16[256,256]{1,0:T(8,128)(2,1)S(1)} collective-permute-done((bf16[256,256]{1,0:T(8,128)(2,1)S(1)}, bf16[256,256]{1,0:T(8,128)(2,1)S(1)}, u32[]{:S(2)}, u32[]{:S(2)}) %collective-permute-start.3) | collective-permute-done | bytes 131104 | tf_op jit(solution)/shard_map/ppermute | solution.py:294
  38.8 0.0 copy-done.1
  38.8 0.2 shard_map.77
  39.0 2.7 %collective-permute-start.4 = (bf16[256,256]{1,0:T(8,128)(2,1)S(1)}, bf16[256,256]{1,0:T(8,128)(2,1)S(1)}, u32[]{:S(2)}, u32[]{:S(2)}) collective-permute-start(bf16[256,256]{1,0:T(8,128)(2,1)S(1)} %get-tuple-element.36), channel_id=1, source_target_pairs={{0,1},{1,0},{2,3},{3,2},{4,5},{5,4},{6,7},{7,6},{8,9},{9,8},{10,11... | collective-permute-start | bytes 393224 | tf_op jit(solution)/shard_map/ppermute | solution.py:294
  41.7 1.9 %collective-permute-start.5 = (bf16[256,256]{1,0:T(8,128)(2,1)S(1)}, bf16[256,256]{1,0:T(8,128)(2,1)S(1)}, u32[]{:S(2)}, u32[]{:S(2)}) collective-permute-start(bf16[256,256]{1,0:T(8,128)(2,1)S(1)} %get-tuple-element.37), channel_id=1, source_target_pairs={{1,2},{2,1},{3,4},{4,3},{5,6},{6,5},{9,10},{10,9},{11,12},{12,11},... | collective-permute-start | bytes 393224 | tf_op jit(solution)/shard_map/ppermute | solution.py:294
  43.6 0.0 collective-permute-done.10.tile2_ref
  43.7 0.0 copy-done.2
  43.7 0.0 copy-done.3
  43.7 1.6 %shard_map.78 = (f32[16,32,256]{2,1,0:T(8,128)S(1)}, f32[16,256]{1,0:T(8,128)S(1)}, bf16[256,256]{1,0:T(8,128)(2,1)S(1)}) custom-call(s32[1]{0:T(128)} %bitcast.8.offset_ref, bf16[256,256]{1,0:T(8,128)(2,1)S(1)} %bitcast.14, bf16[256,256]{1,0:T(8,128)(2,1)S(1)} %add_add_fusion.tile1_ref, bf16[256,256]{1,0:T(8,128)(2,1)S(1)} %collective-permute-done.10.tile2_ref, ...), custom_call_target="tpu_custom_call" | custom-call | flops 2000000000 | bytes 671744 | tf_op jit(solution)/shard_map/pallas_call | solution.py:282
  45.3 0.5 %collective-permute-done.4.near_ref = bf16[256,256]{1,0:T(8,128)(2,1)S(1)} collective-permute-done((bf16[256,256]{1,0:T(8,128)(2,1)S(1)}, bf16[256,256]{1,0:T(8,128)(2,1)S(1)}, u32[]{:S(2)}, u32[]{:S(2)}) %collective-permute-start.4) | collective-permute-done | bytes 131104 | tf_op jit(solution)/shard_map/ppermute | solution.py:294
  45.9 3.9 %collective-permute-done.5.far_ref = bf16[256,256]{1,0:T(8,128)(2,1)S(1)} collective-permute-done((bf16[256,256]{1,0:T(8,128)(2,1)S(1)}, bf16[256,256]{1,0:T(8,128)(2,1)S(1)}, u32[]{:S(2)}, u32[]{:S(2)}) %collective-permute-start.5) | collective-permute-done | bytes 131104 | tf_op jit(solution)/shard_map/ppermute | solution.py:294
  49.8 1.0 %shard_map.79 = f32[32,128]{1,0:T(8,128)} custom-call(bf16[256,256]{1,0:T(8,128)(2,1)S(1)} %collective-permute-done.4.near_ref, bf16[256,256]{1,0:T(8,128)(2,1)S(1)} %collective-permute-done.5.far_ref, f32[16,32,256]{2,1,0:T(8,128)S(1)} %get-tuple-element.44.side_ref, f32[16,256]{1,0:T(8,128)S(1)} %get-tuple-element.45.d_ref, ...), custom_call_target="tpu_custom_call" | custom-call | flops 1000000 | bytes 16384 | tf_op jit(solution)/shard_map/pallas_call | solution.py:282
  (1 shorter events, 0.0 us)
Async XLA Ops:
  0.0 22.0 %copy-start = (bf16[8,8,8,8,256]{4,3,2,1,0:T(8,128)(2,1)S(1)}, bf16[8,8,8,8,256]{4,3,2,1,0:T(8,128)(2,1)}, u32[]{:S(2)}) copy-start(bf16[8,8,8,8,256]{4,3,2,1,0:T(8,128)(2,1)} %param.7) | copy-start | bytes 6291460
  0.0 21.4 %collective-permute-start.8 = (bf16[256,256]{1,0:T(8,128)(2,1)}, bf16[256,256]{1,0:T(8,128)(2,1)S(1)}, u32[]{:S(2)}, u32[]{:S(2)}) collective-permute-start(bf16[256,256]{1,0:T(8,128)(2,1)} %bitcast.11), channel_id=1, source_target_pairs={{24,488},{16,408},{25,489},{17,409},{26,490},{18,410},{27,491},{19... | collective-permute-start | bytes 393224 | tf_op jit(solution)/shard_map/ppermute | solution.py:294
  0.8 28.3 %collective-permute-start.6 = (bf16[256,256]{1,0:T(8,128)(2,1)}, bf16[256,256]{1,0:T(8,128)(2,1)S(1)}, u32[]{:S(2)}, u32[]{:S(2)}) collective-permute-start(bf16[256,256]{1,0:T(8,128)(2,1)} %bitcast.12), channel_id=1, source_target_pairs={{40,8},{41,9},{42,10},{43,11},{44,12},{45,13},{46,14},{47,15},{56,... | collective-permute-start | bytes 393224 | tf_op jit(solution)/shard_map/ppermute | solution.py:294
  3.3 25.8 %collective-permute-start.7 = (bf16[256,256]{1,0:T(8,128)(2,1)}, bf16[256,256]{1,0:T(8,128)(2,1)S(1)}, u32[]{:S(2)}, u32[]{:S(2)}) collective-permute-start(bf16[256,256]{1,0:T(8,128)(2,1)} %bitcast.13), channel_id=1, source_target_pairs={{1008,0},{992,16},{1009,1},{993,17},{1010,2},{994,18},{1011,3},{99... | collective-permute-start | bytes 393224 | tf_op jit(solution)/shard_map/ppermute | solution.py:294
  5.8 18.0 %collective-permute-start = (bf16[256,256]{1,0:T(8,128)(2,1)S(1)}, bf16[256,256]{1,0:T(8,128)(2,1)S(1)}, u32[]{:S(2)}, u32[]{:S(2)}) collective-permute-start(bf16[256,256]{1,0:T(8,128)(2,1)S(1)} %get-tuple-element.27), channel_id=1, source_target_pairs={{0,32},{1,33},{2,34},{3,35},{4,36},{5,37},{6,38},{7,39},{8,40},{9,... | collective-permute-start | bytes 393224 | tf_op jit(solution)/shard_map/ppermute | solution.py:294
  10.8 14.0 %collective-permute-start.1 = (bf16[256,256]{1,0:T(8,128)(2,1)S(1)}, bf16[256,256]{1,0:T(8,128)(2,1)S(1)}, u32[]{:S(2)}, u32[]{:S(2)}) collective-permute-start(bf16[256,256]{1,0:T(8,128)(2,1)S(1)} %get-tuple-element.28), channel_id=1, source_target_pairs={{32,64},{33,65},{34,66},{35,67},{36,68},{37,69},{38,70},{39,71},{4... | collective-permute-start | bytes 393224 | tf_op jit(solution)/shard_map/ppermute | solution.py:294
  21.4 7.8 %collective-permute-start.9 = (bf16[256,256]{1,0:T(8,128)(2,1)S(1)}, bf16[256,256]{1,0:T(8,128)(2,1)S(1)}, u32[]{:S(2)}, u32[]{:S(2)}) collective-permute-start(bf16[256,256]{1,0:T(8,128)(2,1)S(1)} %collective-permute-done.8), channel_id=1, source_target_pairs={{488,1000},{408,1016},{489,1001},{409,1017},{490,1002},{410,1018},... | collective-permute-start | bytes 393224 | tf_op jit(solution)/shard_map/ppermute | solution.py:294
  24.8 14.0 %copy-start.1 = (bf16[4,32,32]{2,1,0:T(8,128)(2,1)S(1)}, bf16[4,32,32]{2,1,0:T(8,128)(2,1)}, u32[]{:S(2)}) copy-start(bf16[4,32,32]{2,1,0:T(8,128)(2,1)} %constant.7.clone.mzh_ref) | copy-start | bytes 24580
  25.1 18.6 %copy-start.2 = (bf16[1,256,256]{2,1,0:T(8,128)(2,1)S(1)}, bf16[1,256,256]{2,1,0:T(8,128)(2,1)}, u32[]{:S(2)}) copy-start(bf16[1,256,256]{2,1,0:T(8,128)(2,1)} %param.10) | copy-start | bytes 393220
  25.1 18.6 %copy-start.3 = (bf16[2,64,32]{2,1,0:T(8,128)(2,1)S(1)}, bf16[2,64,32]{2,1,0:T(8,128)(2,1)}, u32[]{:S(2)}) copy-start(bf16[2,64,32]{2,1,0:T(8,128)(2,1)} %constant.8.clone.add_ref) | copy-start | bytes 24580
  25.1 6.9 %collective-permute-start.2 = (bf16[256,256]{1,0:T(8,128)(2,1)S(1)}, bf16[256,256]{1,0:T(8,128)(2,1)S(1)}, u32[]{:S(2)}, u32[]{:S(2)}) collective-permute-start(bf16[256,256]{1,0:T(8,128)(2,1)S(1)} %get-tuple-element.31), channel_id=1, source_target_pairs={{0,8},{1,9},{2,10},{3,11},{4,12},{5,13},{6,14},{7,15},{8,0},{9,1},... | collective-permute-start | bytes 393224 | tf_op jit(solution)/shard_map/ppermute | solution.py:294
  27.2 11.6 %collective-permute-start.3 = (bf16[256,256]{1,0:T(8,128)(2,1)S(1)}, bf16[256,256]{1,0:T(8,128)(2,1)S(1)}, u32[]{:S(2)}, u32[]{:S(2)}) collective-permute-start(bf16[256,256]{1,0:T(8,128)(2,1)S(1)} %get-tuple-element.32), channel_id=1, source_target_pairs={{8,16},{9,17},{10,18},{11,19},{12,20},{13,21},{14,22},{15,23},{16,... | collective-permute-start | bytes 393224 | tf_op jit(solution)/shard_map/ppermute | solution.py:294
  29.2 14.5 %collective-permute-start.10 = (bf16[256,256]{1,0:T(8,128)(2,1)S(1)}, bf16[256,256]{1,0:T(8,128)(2,1)S(1)}, u32[]{:S(2)}, u32[]{:S(2)}) collective-permute-start(bf16[256,256]{1,0:T(8,128)(2,1)S(1)} %add_add_fusion.tile1_ref), channel_id=1, source_target_pairs={{0,8},{1,9},{2,10},{3,11},{4,12},{5,13},{6,14},{7,15},{8,0},{9,1},... | collective-permute-start | bytes 393224 | tf_op jit(solution)/shard_map/ppermute | solution.py:294
  39.0 6.9 %collective-permute-start.4 = (bf16[256,256]{1,0:T(8,128)(2,1)S(1)}, bf16[256,256]{1,0:T(8,128)(2,1)S(1)}, u32[]{:S(2)}, u32[]{:S(2)}) collective-permute-start(bf16[256,256]{1,0:T(8,128)(2,1)S(1)} %get-tuple-element.36), channel_id=1, source_target_pairs={{0,1},{1,0},{2,3},{3,2},{4,5},{5,4},{6,7},{7,6},{8,9},{9,8},{10,11... | collective-permute-start | bytes 393224 | tf_op jit(solution)/shard_map/ppermute | solution.py:294
  41.7 8.1 %collective-permute-start.5 = (bf16[256,256]{1,0:T(8,128)(2,1)S(1)}, bf16[256,256]{1,0:T(8,128)(2,1)S(1)}, u32[]{:S(2)}, u32[]{:S(2)}) collective-permute-start(bf16[256,256]{1,0:T(8,128)(2,1)S(1)} %get-tuple-element.37), channel_id=1, source_target_pairs={{1,2},{2,1},{3,4},{4,3},{5,6},{6,5},{9,10},{10,9},{11,12},{12,11},... | collective-permute-start | bytes 393224 | tf_op jit(solution)/shard_map/ppermute | solution.py:294

commit v5 on v4

--- a/solution.py
+++ b/solution.py
@@ -94,7 +94,7 @@
 def round_pairs(shape):
     nx, ny, nz = shape
     up, down1, down2 = [], [], []
-    stops = ((3, 15, 1, 1), (2, 12, 3, 3))
+    stops = ((3, 11, 1, 1), (2, 8, 3, 3))
     for z in range(nz):
         for y in (0, 2):
             up.append((at_place(shape, nx - 1, (y + 2) % ny, z), at_place(shape, 0, y, z)))
@@ -141,7 +141,7 @@
     zside_ref[i] = r[cells + sent :]
 
 
-def inner_kernel(count_ref, c_ref, text_ref, x_ref, mid_ref, yside_ref, z_ref, zside_ref):
+def inner_kernel(count_ref, c_ref, text_ref, mid_ref, yside_ref, z_ref, zside_ref):
     planes, rows = c_ref.shape[1], c_ref.shape[2]
     mask = lane_mask(count_ref, rows, c_ref.shape[3])
     for m in range(1, planes):
@@ -155,11 +155,38 @@
             even.append(jnp.where(mask, e, 0.0).astype(BF16))
         for i, parts in ((2 * m - 2, odd), (2 * m - 1, even)):
             x = jnp.concatenate(parts, axis=0)
-            x_ref[i] = x
             split_cells(jnp.dot(text_ref[...], x, preferred_element_type=F32), i, mid_ref, yside_ref, z_ref, zside_ref)
 
 
-def edge_kernel(count_ref, planes_ref, near_ref, far_ref, x_ref, edge_ref, ynear_ref, yfar_ref, *, cy, cz):
+def rim_kernel(count_ref, c_ref, ynear_ref, yfar_ref, *, cz):
+    planes, rows = c_ref.shape[1], c_ref.shape[2]
+    mask = lane_mask(count_ref, cz, c_ref.shape[3])
+    even_y = parity("gy") == 0
+    ends = []
+    for tap, low in ((3, rows - cz), (0, 0)):
+        end = [[None] * planes for _ in range(4)]
+        for xb in range(2):
+            for zb in range(2):
+                for k in range(planes):
+                    s0 = c_ref[4 * xb + zb, k, low : low + cz].astype(F32)
+                    w0 = c_ref[4 * xb + 2 + zb, k, low : low + cz].astype(F32)
+                    end[2 * xb + zb][k] = jnp.where(mask, FILT[tap] * s0 + WAVE[tap] * w0, 0.0)
+        ends.append(end)
+    for m in range(1, planes):
+        for n, old, new in ((2 * m - 1, 2, 0), (2 * m, 3, 1)):
+            sides = []
+            for end in ends:
+                parts = []
+                for zb in range(2):
+                    s, w = end[zb], end[2 + zb]
+                    parts.append(FILT[old] * s[m - 1] + WAVE[old] * w[m - 1] + FILT[new] * s[m] + WAVE[new] * w[m])
+                sides.append(jnp.concatenate(parts, axis=0))
+            last, first = sides
+            ynear_ref[n * 2 * cz : (n + 1) * 2 * cz] = jnp.where(even_y, last, first).astype(BF16)
+            yfar_ref[n * 2 * cz : (n + 1) * 2 * cz] = jnp.where(even_y, first, last).astype(BF16)
+
+
+def edge_kernel(count_ref, planes_ref, near_ref, far_ref, nearrim_ref, farrim_ref, edge_ref, ynear_ref, yfar_ref, *, cy, cz):
     rows = planes_ref.shape[2]
     mask = lane_mask(count_ref, rows, planes_ref.shape[3])
     even = parity("gx") == 0
@@ -173,19 +200,20 @@
         edge_ref[0, b * rows : (b + 1) * rows] = lo.astype(BF16)
         edge_ref[1, b * rows : (b + 1) * rows] = hi.astype(BF16)
     even_y = parity("gy") == 0
-    fine = x_ref.shape[0] + 2
-    for n in range(fine):
-        ref, i = (edge_ref, 0) if n == 0 else (edge_ref, 1) if n == fine - 1 else (x_ref, n - 1)
+    step, size = 2 * cz, ynear_ref.shape[0]
+    ynear_ref[step : size - step] = nearrim_ref[step : size - step]
+    yfar_ref[step : size - step] = farrim_ref[step : size - step]
+    for i, start in ((0, 0), (1, size - step)):
         near_rows, far_rows = [], []
         for zb in range(2):
             low, high = zb * rows, (2 + zb) * rows
             end = (cy - 1) * cz
-            first = FILT[0] * ref[i, low : low + cz].astype(F32) + WAVE[0] * ref[i, high : high + cz].astype(F32)
-            last = FILT[3] * ref[i, low + end : low + end + cz].astype(F32) + WAVE[3] * ref[i, high + end : high + end + cz].astype(F32)
+            face = lambda tap, at: FILT[tap] * edge_ref[i, low + at : low + at + cz].astype(F32) + WAVE[tap] * edge_ref[i, high + at : high + at + cz].astype(F32)
+            first, last = face(0, 0), face(3, end)
             near_rows.append(jnp.where(even_y, last, first))
             far_rows.append(jnp.where(even_y, first, last))
-        ynear_ref[n * 2 * cz : (n + 1) * 2 * cz] = jnp.concatenate(near_rows, axis=0).astype(BF16)
-        yfar_ref[n * 2 * cz : (n + 1) * 2 * cz] = jnp.concatenate(far_rows, axis=0).astype(BF16)
+        ynear_ref[start : start + step] = jnp.concatenate(near_rows, axis=0).astype(BF16)
+        yfar_ref[start : start + step] = jnp.concatenate(far_rows, axis=0).astype(BF16)
 
 
 def edge_cells_kernel(edge_ref, text_ref, *out_refs):
@@ -327,14 +355,12 @@
             vmem((n, 4 * cy, slots), F32), vmem((n, 4 * cy, slots), F32),
         ]
 
-    x, mid, yside, z, zside = call(
-        inner_kernel, [vmem((fx - 2, 4 * rows, slots), BF16)] + cell_outs(fx - 2), [count, c, text], 1,
-        flops=2e9,
-    )
     yshape = vmem((fx * 2 * cz, slots), BF16)
+    nearrim, farrim = call(functools.partial(rim_kernel, cz=cz), [yshape, yshape], [count, c], 1)
+    mid, yside, z, zside = call(inner_kernel, cell_outs(fx - 2), [count, c, text], 1, flops=2e9)
     edge, ynear, yfar = call(
         functools.partial(edge_kernel, cy=cy, cz=cz),
-        [vmem((2, 4 * rows, slots), BF16), yshape, yshape], [count, planes, xnear, xfar, x], 1,
+        [vmem((2, 4 * rows, slots), BF16), yshape, yshape], [count, planes, xnear, xfar, nearrim, farrim], 1,
     )
     yfar = send(yfar, far[1])
     ynear = send(ynear, near[1])

time: 51.2 us -> 52.9 us (1.033)
  the two profiles are of different devices: /device:TPU:76 before, /device:TPU:320 now
where the time goes in v5:
time: 52.9 us; the launch traced here: 52.5 us
  starting transfers between devices  38.5 us (73%)
  Pallas kernels  6.34 us (12%)
  waiting for transfers between devices  6.08 us (11%)
  between operations  1.54 us (3%)
    ppermute x11, starting transfers between devices, send(): return lax.ppermute(value, AXES, pairs)  38.5 us
    pallas_call x8, Pallas kernels, call(): pl.pallas_call(body, out_shape=tuple(outs), in_specs=specs, out_specs=tup...  6.34 us
    ppermute x11, waiting for transfers between devices, send(): return lax.ppermute(value, AXES, pairs)  6.08 us
  transfers between devices with their start and end apart: 11, of which 3 were waited for; matrix products, arithmetic and copies ran while one was open for 0% of the time, Pallas kernels for 10%

profile of v5, /device:TPU:320, one launch (start us, length us, event | category | flops | bytes accessed | tf_op | source)
XLA Modules:
  0.0 52.5 jit_solution(1053863903771131204)
XLA Ops:
  0.0 0.0 copy-start.2
  0.0 0.0 copy-start
  0.0 0.8 %collective-permute-start.8 = (bf16[256,256]{1,0:T(8,128)(2,1)}, bf16[256,256]{1,0:T(8,128)(2,1)S(1)}, u32[]{:S(2)}, u32[]{:S(2)}) collective-permute-start(bf16[256,256]{1,0:T(8,128)(2,1)} %bitcast.13), channel_id=1, source_target_pairs={{24,360},{16,280},{25,361},{17,281},{26,362},{18,282},{27,363},{19... | collective-permute-start | bytes 393224 | tf_op jit(solution)/shard_map/ppermute | solution.py:322
  1.4 1.2 %shard_map.73 = (bf16[256,256]{1,0:T(8,128)(2,1)S(1)}, bf16[256,256]{1,0:T(8,128)(2,1)S(1)}, bf16[2,8,64,256]{3,2,1,0:T(8,128)(2,1)S(1)}, bf16[320,256]{1,0:T(8,128)(2,1)S(1)}) custom-call(s32[1]{0:T(128)} %bitcast.5.count_ref, bf16[8,8,64,256]{3,2,1,0:T(8,128)(2,1)} %bitcast.10, bf16[2,320,256]{2,1,0:T(8,128)(2,1)} %constant.6.clone.text_hbm), custom_call_target="tpu_custom_call" | custom-call | flops 1000000 | bytes 950272 | tf_op jit(solution)/shard_map/pallas_call | solution.py:310
  2.6 3.4 %collective-permute-start = (bf16[256,256]{1,0:T(8,128)(2,1)S(1)}, bf16[256,256]{1,0:T(8,128)(2,1)S(1)}, u32[]{:S(2)}, u32[]{:S(2)}) collective-permute-start(bf16[256,256]{1,0:T(8,128)(2,1)S(1)} %get-tuple-element.28), channel_id=1, source_target_pairs={{0,32},{1,33},{2,34},{3,35},{4,36},{5,37},{6,38},{7,39},{8,40},{9,... | collective-permute-start | bytes 393224 | tf_op jit(solution)/shard_map/ppermute | solution.py:322
  6.1 2.5 %collective-permute-start.1 = (bf16[256,256]{1,0:T(8,128)(2,1)S(1)}, bf16[256,256]{1,0:T(8,128)(2,1)S(1)}, u32[]{:S(2)}, u32[]{:S(2)}) collective-permute-start(bf16[256,256]{1,0:T(8,128)(2,1)S(1)} %get-tuple-element.29), channel_id=1, source_target_pairs={{32,64},{33,65},{34,66},{35,67},{36,68},{37,69},{38,70},{39,71},{4... | collective-permute-start | bytes 393224 | tf_op jit(solution)/shard_map/ppermute | solution.py:322
  8.5 0.0 copy-done.2
  8.5 4.3 %collective-permute-start.6 = (bf16[256,256]{1,0:T(8,128)(2,1)S(1)}, bf16[256,256]{1,0:T(8,128)(2,1)S(1)}, u32[]{:S(2)}, u32[]{:S(2)}) collective-permute-start(bf16[256,256]{1,0:T(8,128)(2,1)S(1)} %bitcast.14), channel_id=1, source_target_pairs={{40,8},{41,9},{42,10},{43,11},{44,12},{45,13},{46,14},{47,15},{56,... | collective-permute-start | bytes 393224 | tf_op jit(solution)/shard_map/ppermute | solution.py:322
  12.9 0.7 %collective-permute-start.7 = (bf16[256,256]{1,0:T(8,128)(2,1)S(1)}, bf16[256,256]{1,0:T(8,128)(2,1)S(1)}, u32[]{:S(2)}, u32[]{:S(2)}) collective-permute-start(bf16[256,256]{1,0:T(8,128)(2,1)S(1)} %bitcast.15), channel_id=1, source_target_pairs={{1008,0},{992,16},{1009,1},{993,17},{1010,2},{994,18},{1011,3},{99... | collective-permute-start | bytes 393224 | tf_op jit(solution)/shard_map/ppermute | solution.py:322
  13.6 0.0 collective-permute-done.8
  13.6 0.7 %collective-permute-start.9 = (bf16[256,256]{1,0:T(8,128)(2,1)S(1)}, bf16[256,256]{1,0:T(8,128)(2,1)S(1)}, u32[]{:S(2)}, u32[]{:S(2)}) collective-permute-start(bf16[256,256]{1,0:T(8,128)(2,1)S(1)} %collective-permute-done.8), channel_id=1, source_target_pairs={{360,1000},{280,1016},{361,1001},{281,1017},{362,1002},{282,1018},... | collective-permute-start | bytes 393224 | tf_op jit(solution)/shard_map/ppermute | solution.py:322
  14.9 0.0 copy-done
  14.9 0.2 shard_map.74
  15.1 0.0 collective-permute-done.near_ref
  15.2 1.4 %collective-permute-done.1.far_ref = bf16[256,256]{1,0:T(8,128)(2,1)S(1)} collective-permute-done((bf16[256,256]{1,0:T(8,128)(2,1)S(1)}, bf16[256,256]{1,0:T(8,128)(2,1)S(1)}, u32[]{:S(2)}, u32[]{:S(2)}) %collective-permute-start.1) | collective-permute-done | bytes 131104 | tf_op jit(solution)/shard_map/ppermute | solution.py:322
  16.6 0.2 shard_map.75
  16.8 2.9 %collective-permute-start.2 = (bf16[256,256]{1,0:T(8,128)(2,1)S(1)}, bf16[256,256]{1,0:T(8,128)(2,1)S(1)}, u32[]{:S(2)}, u32[]{:S(2)}) collective-permute-start(bf16[256,256]{1,0:T(8,128)(2,1)S(1)} %get-tuple-element.32), channel_id=1, source_target_pairs={{0,8},{1,9},{2,10},{3,11},{4,12},{5,13},{6,14},{7,15},{8,0},{9,1},... | collective-permute-start | bytes 393224 | tf_op jit(solution)/shard_map/ppermute | solution.py:322
  19.7 0.7 %collective-permute-start.3 = (bf16[256,256]{1,0:T(8,128)(2,1)S(1)}, bf16[256,256]{1,0:T(8,128)(2,1)S(1)}, u32[]{:S(2)}, u32[]{:S(2)}) collective-permute-start(bf16[256,256]{1,0:T(8,128)(2,1)S(1)} %get-tuple-element.33), channel_id=1, source_target_pairs={{8,16},{9,17},{10,18},{11,19},{12,20},{13,21},{14,22},{15,23},{16,... | collective-permute-start | bytes 393224 | tf_op jit(solution)/shard_map/ppermute | solution.py:322
  20.4 0.0 collective-permute-done.6
  20.4 0.0 collective-permute-done.7
  20.4 0.0 collective-permute-done.9
  20.4 18.0 %collective-permute-start.10 = (bf16[256,256]{1,0:T(8,128)(2,1)S(1)}, bf16[256,256]{1,0:T(8,128)(2,1)S(1)}, u32[]{:S(2)}, u32[]{:S(2)}) collective-permute-start(bf16[256,256]{1,0:T(8,128)(2,1)S(1)} %add_add_fusion.tile1_ref), channel_id=1, source_target_pairs={{0,8},{1,9},{2,10},{3,11},{4,12},{5,13},{6,14},{7,15},{8,0},{9,1},... | collective-permute-start | bytes 393224 | tf_op jit(solution)/shard_map/ppermute | solution.py:322
  38.4 0.0 copy-start.1
  38.4 0.0 copy-start.3
  38.5 1.6 %shard_map.76 = (bf16[14,224,256]{2,1,0:T(8,128)(2,1)S(1)}, f32[14,32,256]{2,1,0:T(8,128)S(1)}, f32[14,32,256]{2,1,0:T(8,128)S(1)}, f32[14,32,256]{2,1,0:T(8,128)S(1)}) custom-call(s32[1]{0:T(128)} %bitcast.8.count_ref, bf16[8,8,64,256]{3,2,1,0:T(8,128)(2,1)S(1)} %bitcast.12, bf16[320,256]{1,0:T(8,128)(2,1)S(1)} %get-tuple-element.34.text_ref), custom_call_target="tpu_custom_call" | custom-call | flops 2000000000 | bytes 2981888 | tf_op jit(solution)/shard_map/pallas_call | solution.py:310
  40.1 0.2 shard_map.77
  40.3 0.0 collective-permute-done.2.ynear_ref
  40.3 0.0 collective-permute-done.3.yfar_ref
  40.3 0.0 copy-done.1
  40.3 0.2 shard_map.78
  40.5 2.7 %collective-permute-start.4 = (bf16[256,256]{1,0:T(8,128)(2,1)S(1)}, bf16[256,256]{1,0:T(8,128)(2,1)S(1)}, u32[]{:S(2)}, u32[]{:S(2)}) collective-permute-start(bf16[256,256]{1,0:T(8,128)(2,1)S(1)} %get-tuple-element.38), channel_id=1, source_target_pairs={{0,1},{1,0},{2,3},{3,2},{4,5},{5,4},{6,7},{7,6},{8,9},{9,8},{10,11... | collective-permute-start | bytes 393224 | tf_op jit(solution)/shard_map/ppermute | solution.py:322
  43.3 1.9 %collective-permute-start.5 = (bf16[256,256]{1,0:T(8,128)(2,1)S(1)}, bf16[256,256]{1,0:T(8,128)(2,1)S(1)}, u32[]{:S(2)}, u32[]{:S(2)}) collective-permute-start(bf16[256,256]{1,0:T(8,128)(2,1)S(1)} %get-tuple-element.39), channel_id=1, source_target_pairs={{1,2},{2,1},{3,4},{4,3},{5,6},{6,5},{9,10},{10,9},{11,12},{12,11},... | collective-permute-start | bytes 393224 | tf_op jit(solution)/shard_map/ppermute | solution.py:322
  45.2 0.0 collective-permute-done.10.tile2_ref
  45.2 0.0 copy-done.3
  45.2 1.6 %shard_map.79 = (f32[16,32,256]{2,1,0:T(8,128)S(1)}, f32[16,256]{1,0:T(8,128)S(1)}, bf16[256,256]{1,0:T(8,128)(2,1)S(1)}) custom-call(s32[1]{0:T(128)} %bitcast.9.offset_ref, bf16[256,256]{1,0:T(8,128)(2,1)S(1)} %bitcast.16, bf16[256,256]{1,0:T(8,128)(2,1)S(1)} %add_add_fusion.tile1_ref, bf16[256,256]{1,0:T(8,128)(2,1)S(1)} %collective-permute-done.10.tile2_ref, ...), custom_call_target="tpu_custom_call" | custom-call | flops 2000000000 | bytes 671744 | tf_op jit(solution)/shard_map/pallas_call | solution.py:310
  46.9 1.0 %collective-permute-done.4.near_ref = bf16[256,256]{1,0:T(8,128)(2,1)S(1)} collective-permute-done((bf16[256,256]{1,0:T(8,128)(2,1)S(1)}, bf16[256,256]{1,0:T(8,128)(2,1)S(1)}, u32[]{:S(2)}, u32[]{:S(2)}) %collective-permute-start.4) | collective-permute-done | bytes 131104 | tf_op jit(solution)/shard_map/ppermute | solution.py:322
  47.9 3.6 %collective-permute-done.5.far_ref = bf16[256,256]{1,0:T(8,128)(2,1)S(1)} collective-permute-done((bf16[256,256]{1,0:T(8,128)(2,1)S(1)}, bf16[256,256]{1,0:T(8,128)(2,1)S(1)}, u32[]{:S(2)}, u32[]{:S(2)}) %collective-permute-start.5) | collective-permute-done | bytes 131104 | tf_op jit(solution)/shard_map/ppermute | solution.py:322
  51.5 1.0 %shard_map.80 = f32[32,128]{1,0:T(8,128)} custom-call(bf16[256,256]{1,0:T(8,128)(2,1)S(1)} %collective-permute-done.4.near_ref, bf16[256,256]{1,0:T(8,128)(2,1)S(1)} %collective-permute-done.5.far_ref, f32[16,32,256]{2,1,0:T(8,128)S(1)} %get-tuple-element.46.side_ref, f32[16,256]{1,0:T(8,128)S(1)} %get-tuple-element.47.d_ref, ...), custom_call_target="tpu_custom_call" | custom-call | flops 1000000 | bytes 16384 | tf_op jit(solution)/shard_map/pallas_call | solution.py:310
  (1 shorter events, 0.0 us)
Async XLA Ops:
  0.0 8.5 %copy-start.2 = (bf16[1,256,256]{2,1,0:T(8,128)(2,1)S(1)}, bf16[1,256,256]{2,1,0:T(8,128)(2,1)}, u32[]{:S(2)}) copy-start(bf16[1,256,256]{2,1,0:T(8,128)(2,1)} %param.10) | copy-start | bytes 393220
  0.0 14.9 %copy-start = (bf16[8,8,8,8,256]{4,3,2,1,0:T(8,128)(2,1)S(1)}, bf16[8,8,8,8,256]{4,3,2,1,0:T(8,128)(2,1)}, u32[]{:S(2)}) copy-start(bf16[8,8,8,8,256]{4,3,2,1,0:T(8,128)(2,1)} %param.7) | copy-start | bytes 6291460
  0.0 13.6 %collective-permute-start.8 = (bf16[256,256]{1,0:T(8,128)(2,1)}, bf16[256,256]{1,0:T(8,128)(2,1)S(1)}, u32[]{:S(2)}, u32[]{:S(2)}) collective-permute-start(bf16[256,256]{1,0:T(8,128)(2,1)} %bitcast.13), channel_id=1, source_target_pairs={{24,360},{16,280},{25,361},{17,281},{26,362},{18,282},{27,363},{19... | collective-permute-start | bytes 393224 | tf_op jit(solution)/shard_map/ppermute | solution.py:322
  2.6 12.5 %collective-permute-start = (bf16[256,256]{1,0:T(8,128)(2,1)S(1)}, bf16[256,256]{1,0:T(8,128)(2,1)S(1)}, u32[]{:S(2)}, u32[]{:S(2)}) collective-permute-start(bf16[256,256]{1,0:T(8,128)(2,1)S(1)} %get-tuple-element.28), channel_id=1, source_target_pairs={{0,32},{1,33},{2,34},{3,35},{4,36},{5,37},{6,38},{7,39},{8,40},{9,... | collective-permute-start | bytes 393224 | tf_op jit(solution)/shard_map/ppermute | solution.py:322
  6.1 10.5 %collective-permute-start.1 = (bf16[256,256]{1,0:T(8,128)(2,1)S(1)}, bf16[256,256]{1,0:T(8,128)(2,1)S(1)}, u32[]{:S(2)}, u32[]{:S(2)}) collective-permute-start(bf16[256,256]{1,0:T(8,128)(2,1)S(1)} %get-tuple-element.29), channel_id=1, source_target_pairs={{32,64},{33,65},{34,66},{35,67},{36,68},{37,69},{38,70},{39,71},{4... | collective-permute-start | bytes 393224 | tf_op jit(solution)/shard_map/ppermute | solution.py:322
  8.5 11.8 %collective-permute-start.6 = (bf16[256,256]{1,0:T(8,128)(2,1)S(1)}, bf16[256,256]{1,0:T(8,128)(2,1)S(1)}, u32[]{:S(2)}, u32[]{:S(2)}) collective-permute-start(bf16[256,256]{1,0:T(8,128)(2,1)S(1)} %bitcast.14), channel_id=1, source_target_pairs={{40,8},{41,9},{42,10},{43,11},{44,12},{45,13},{46,14},{47,15},{56,... | collective-permute-start | bytes 393224 | tf_op jit(solution)/shard_map/ppermute | solution.py:322
  12.9 7.5 %collective-permute-start.7 = (bf16[256,256]{1,0:T(8,128)(2,1)S(1)}, bf16[256,256]{1,0:T(8,128)(2,1)S(1)}, u32[]{:S(2)}, u32[]{:S(2)}) collective-permute-start(bf16[256,256]{1,0:T(8,128)(2,1)S(1)} %bitcast.15), channel_id=1, source_target_pairs={{1008,0},{992,16},{1009,1},{993,17},{1010,2},{994,18},{1011,3},{99... | collective-permute-start | bytes 393224 | tf_op jit(solution)/shard_map/ppermute | solution.py:322
  13.6 6.8 %collective-permute-start.9 = (bf16[256,256]{1,0:T(8,128)(2,1)S(1)}, bf16[256,256]{1,0:T(8,128)(2,1)S(1)}, u32[]{:S(2)}, u32[]{:S(2)}) collective-permute-start(bf16[256,256]{1,0:T(8,128)(2,1)S(1)} %collective-permute-done.8), channel_id=1, source_target_pairs={{360,1000},{280,1016},{361,1001},{281,1017},{362,1002},{282,1018},... | collective-permute-start | bytes 393224 | tf_op jit(solution)/shard_map/ppermute | solution.py:322
  16.8 23.5 %collective-permute-start.2 = (bf16[256,256]{1,0:T(8,128)(2,1)S(1)}, bf16[256,256]{1,0:T(8,128)(2,1)S(1)}, u32[]{:S(2)}, u32[]{:S(2)}) collective-permute-start(bf16[256,256]{1,0:T(8,128)(2,1)S(1)} %get-tuple-element.32), channel_id=1, source_target_pairs={{0,8},{1,9},{2,10},{3,11},{4,12},{5,13},{6,14},{7,15},{8,0},{9,1},... | collective-permute-start | bytes 393224 | tf_op jit(solution)/shard_map/ppermute | solution.py:322
  19.7 20.6 %collective-permute-start.3 = (bf16[256,256]{1,0:T(8,128)(2,1)S(1)}, bf16[256,256]{1,0:T(8,128)(2,1)S(1)}, u32[]{:S(2)}, u32[]{:S(2)}) collective-permute-start(bf16[256,256]{1,0:T(8,128)(2,1)S(1)} %get-tuple-element.33), channel_id=1, source_target_pairs={{8,16},{9,17},{10,18},{11,19},{12,20},{13,21},{14,22},{15,23},{16,... | collective-permute-start | bytes 393224 | tf_op jit(solution)/shard_map/ppermute | solution.py:322
  20.4 24.8 %collective-permute-start.10 = (bf16[256,256]{1,0:T(8,128)(2,1)S(1)}, bf16[256,256]{1,0:T(8,128)(2,1)S(1)}, u32[]{:S(2)}, u32[]{:S(2)}) collective-permute-start(bf16[256,256]{1,0:T(8,128)(2,1)S(1)} %add_add_fusion.tile1_ref), channel_id=1, source_target_pairs={{0,8},{1,9},{2,10},{3,11},{4,12},{5,13},{6,14},{7,15},{8,0},{9,1},... | collective-permute-start | bytes 393224 | tf_op jit(solution)/shard_map/ppermute | solution.py:322
  38.4 1.9 %copy-start.1 = (bf16[4,32,32]{2,1,0:T(8,128)(2,1)S(1)}, bf16[4,32,32]{2,1,0:T(8,128)(2,1)}, u32[]{:S(2)}) copy-start(bf16[4,32,32]{2,1,0:T(8,128)(2,1)} %constant.7.clone.mzh_ref) | copy-start | bytes 24580
  38.4 6.8 %copy-start.3 = (bf16[2,64,32]{2,1,0:T(8,128)(2,1)S(1)}, bf16[2,64,32]{2,1,0:T(8,128)(2,1)}, u32[]{:S(2)}) copy-start(bf16[2,64,32]{2,1,0:T(8,128)(2,1)} %constant.8.clone.add_ref) | copy-start | bytes 24580
  40.5 7.3 %collective-permute-start.4 = (bf16[256,256]{1,0:T(8,128)(2,1)S(1)}, bf16[256,256]{1,0:T(8,128)(2,1)S(1)}, u32[]{:S(2)}, u32[]{:S(2)}) collective-permute-start(bf16[256,256]{1,0:T(8,128)(2,1)S(1)} %get-tuple-element.38), channel_id=1, source_target_pairs={{0,1},{1,0},{2,3},{3,2},{4,5},{5,4},{6,7},{7,6},{8,9},{9,8},{10,11... | collective-permute-start | bytes 393224 | tf_op jit(solution)/shard_map/ppermute | solution.py:322
  43.3 8.2 %collective-permute-start.5 = (bf16[256,256]{1,0:T(8,128)(2,1)S(1)}, bf16[256,256]{1,0:T(8,128)(2,1)S(1)}, u32[]{:S(2)}, u32[]{:S(2)}) collective-permute-start(bf16[256,256]{1,0:T(8,128)(2,1)S(1)} %get-tuple-element.39), channel_id=1, source_target_pairs={{1,2},{2,1},{3,4},{4,3},{5,6},{6,5},{9,10},{10,9},{11,12},{12,11},... | collective-permute-start | bytes 393224 | tf_op jit(solution)/shard_map/ppermute | solution.py:322

commit v6 on v5

--- a/solution.py
+++ b/solution.py
@@ -346,7 +346,6 @@
     xfar = send(xfar, far[0])
     xnear = send(xnear, near[0])
     up_pairs, down1_pairs, down2_pairs = round_pairs(shape)
-    up = send(own, up_pairs)
     down = send(own, down1_pairs)
 
     def cell_outs(n):
@@ -365,13 +364,13 @@
     yfar = send(yfar, far[1])
     ynear = send(ynear, near[1])
     down = send(down, down2_pairs)
-    tile1 = send(own, tile_pairs(shape))
+    tile1 = send(own, tile_pairs(shape) + up_pairs)
     mide, ysidee, ze, zsidee = call(edge_cells_kernel, cell_outs(2), [edge, text], flops=3e8)
     zshape = vmem((fx * 2 * cy, slots), BF16)
     znear, zfar = call(zfaces_kernel, [zshape, zshape], [ynear, yfar, z, ze, mzh])
     znear = send(znear, near[2])
     zfar = send(zfar, far[2])
-    tile1 = tile1 + up + down
+    tile1 = tile1 + down
     tile2 = send(tile1, near[1])
     side, d, tile = call(
         density_kernel, [vmem((fx, 4 * cy, slots), F32), vmem((fx, cells), F32), vmem((slots, slots), BF16)],

time: 52.9 us -> 52.2 us (0.987)
  starting transfers between devices: 38.5 us -> 37.2 us
  waiting for transfers between devices: 6.08 us -> 6.74 us
    ppermute x11 -> x10, starting transfers between devices: 38.5 us -> 37.2 us  [send(): return lax.ppermute(value, AXES, pairs)]
    ppermute x11 -> x10, waiting for transfers between devices: 6.08 us -> 6.74 us  [send(): return lax.ppermute(value, AXES, pairs)]
  transfers between devices with their start and end apart: 11 -> 10, of which waited for: 3 -> 3; matrix products, arithmetic and copies ran while one was open for 0% -> 0% of each run, Pallas kernels for 10% -> 10%
where the time goes in v6:
time: 52.2 us; the launch traced here: 51.8 us
  starting transfers between devices  37.2 us (71%)
  waiting for transfers between devices  6.74 us (13%)
  Pallas kernels  6.34 us (12%)
  between operations  1.52 us (3%)
    ppermute x10, starting transfers between devices, send(): return lax.ppermute(value, AXES, pairs)  37.2 us
    ppermute x10, waiting for transfers between devices, send(): return lax.ppermute(value, AXES, pairs)  6.74 us
    pallas_call x8, Pallas kernels, call(): pl.pallas_call(body, out_shape=tuple(outs), in_specs=specs, out_specs=tup...  6.34 us
  transfers between devices with their start and end apart: 10, of which 3 were waited for; matrix products, arithmetic and copies ran while one was open for 0% of the time, Pallas kernels for 10%

profile of v6, /device:TPU:320, one launch (start us, length us, event | category | flops | bytes accessed | tf_op | source)
XLA Modules:
  0.0 51.8 jit_solution(14851389550620386826)
XLA Ops:
  0.0 0.0 copy-start.2
  0.0 0.0 copy-start
  0.0 0.8 %collective-permute-start.7 = (bf16[256,256]{1,0:T(8,128)(2,1)}, bf16[256,256]{1,0:T(8,128)(2,1)S(1)}, u32[]{:S(2)}, u32[]{:S(2)}) collective-permute-start(bf16[256,256]{1,0:T(8,128)(2,1)} %bitcast.13), channel_id=1, source_target_pairs={{24,360},{16,280},{25,361},{17,281},{26,362},{18,282},{27,363},{19... | collective-permute-start | bytes 393224 | tf_op jit(solution)/shard_map/ppermute | solution.py:322
  1.4 1.2 %shard_map.73 = (bf16[256,256]{1,0:T(8,128)(2,1)S(1)}, bf16[256,256]{1,0:T(8,128)(2,1)S(1)}, bf16[2,8,64,256]{3,2,1,0:T(8,128)(2,1)S(1)}, bf16[320,256]{1,0:T(8,128)(2,1)S(1)}) custom-call(s32[1]{0:T(128)} %bitcast.5.count_ref, bf16[8,8,64,256]{3,2,1,0:T(8,128)(2,1)} %bitcast.10, bf16[2,320,256]{2,1,0:T(8,128)(2,1)} %constant.6.clone.text_hbm), custom_call_target="tpu_custom_call" | custom-call | flops 1000000 | bytes 950272 | tf_op jit(solution)/shard_map/pallas_call | solution.py:310
  2.6 3.4 %collective-permute-start = (bf16[256,256]{1,0:T(8,128)(2,1)S(1)}, bf16[256,256]{1,0:T(8,128)(2,1)S(1)}, u32[]{:S(2)}, u32[]{:S(2)}) collective-permute-start(bf16[256,256]{1,0:T(8,128)(2,1)S(1)} %get-tuple-element.28), channel_id=1, source_target_pairs={{0,32},{1,33},{2,34},{3,35},{4,36},{5,37},{6,38},{7,39},{8,40},{9,... | collective-permute-start | bytes 393224 | tf_op jit(solution)/shard_map/ppermute | solution.py:322
  6.1 2.5 %collective-permute-start.1 = (bf16[256,256]{1,0:T(8,128)(2,1)S(1)}, bf16[256,256]{1,0:T(8,128)(2,1)S(1)}, u32[]{:S(2)}, u32[]{:S(2)}) collective-permute-start(bf16[256,256]{1,0:T(8,128)(2,1)S(1)} %get-tuple-element.29), channel_id=1, source_target_pairs={{32,64},{33,65},{34,66},{35,67},{36,68},{37,69},{38,70},{39,71},{4... | collective-permute-start | bytes 393224 | tf_op jit(solution)/shard_map/ppermute | solution.py:322
  8.5 0.0 copy-done.2
  8.5 4.3 %collective-permute-start.6 = (bf16[256,256]{1,0:T(8,128)(2,1)S(1)}, bf16[256,256]{1,0:T(8,128)(2,1)S(1)}, u32[]{:S(2)}, u32[]{:S(2)}) collective-permute-start(bf16[256,256]{1,0:T(8,128)(2,1)S(1)} %bitcast.14), channel_id=1, source_target_pairs={{40,8},{41,9},{42,10},{43,11},{44,12},{45,13},{46,14},{47,15},{56,... | collective-permute-start | bytes 393224 | tf_op jit(solution)/shard_map/ppermute | solution.py:322
  12.9 0.0 collective-permute-done.7
  12.9 0.7 %collective-permute-start.8 = (bf16[256,256]{1,0:T(8,128)(2,1)S(1)}, bf16[256,256]{1,0:T(8,128)(2,1)S(1)}, u32[]{:S(2)}, u32[]{:S(2)}) collective-permute-start(bf16[256,256]{1,0:T(8,128)(2,1)S(1)} %collective-permute-done.7), channel_id=1, source_target_pairs={{360,1000},{280,1016},{361,1001},{281,1017},{362,1002},{282,1018},... | collective-permute-start | bytes 393224 | tf_op jit(solution)/shard_map/ppermute | solution.py:322
  14.2 0.0 copy-done
  14.2 0.2 shard_map.74
  14.5 0.0 collective-permute-done.near_ref
  14.5 2.1 %collective-permute-done.1.far_ref = bf16[256,256]{1,0:T(8,128)(2,1)S(1)} collective-permute-done((bf16[256,256]{1,0:T(8,128)(2,1)S(1)}, bf16[256,256]{1,0:T(8,128)(2,1)S(1)}, u32[]{:S(2)}, u32[]{:S(2)}) %collective-permute-start.1) | collective-permute-done | bytes 131104 | tf_op jit(solution)/shard_map/ppermute | solution.py:322
  16.6 0.2 shard_map.75
  16.8 2.2 %collective-permute-start.2 = (bf16[256,256]{1,0:T(8,128)(2,1)S(1)}, bf16[256,256]{1,0:T(8,128)(2,1)S(1)}, u32[]{:S(2)}, u32[]{:S(2)}) collective-permute-start(bf16[256,256]{1,0:T(8,128)(2,1)S(1)} %get-tuple-element.32), channel_id=1, source_target_pairs={{0,8},{1,9},{2,10},{3,11},{4,12},{5,13},{6,14},{7,15},{8,0},{9,1},... | collective-permute-start | bytes 393224 | tf_op jit(solution)/shard_map/ppermute | solution.py:322
  19.0 0.7 %collective-permute-start.3 = (bf16[256,256]{1,0:T(8,128)(2,1)S(1)}, bf16[256,256]{1,0:T(8,128)(2,1)S(1)}, u32[]{:S(2)}, u32[]{:S(2)}) collective-permute-start(bf16[256,256]{1,0:T(8,128)(2,1)S(1)} %get-tuple-element.33), channel_id=1, source_target_pairs={{8,16},{9,17},{10,18},{11,19},{12,20},{13,21},{14,22},{15,23},{16,... | collective-permute-start | bytes 393224 | tf_op jit(solution)/shard_map/ppermute | solution.py:322
  19.7 0.0 collective-permute-done.6
  19.7 0.0 collective-permute-done.8
  19.7 18.0 %collective-permute-start.9 = (bf16[256,256]{1,0:T(8,128)(2,1)S(1)}, bf16[256,256]{1,0:T(8,128)(2,1)S(1)}, u32[]{:S(2)}, u32[]{:S(2)}) collective-permute-start(bf16[256,256]{1,0:T(8,128)(2,1)S(1)} %add.3.tile1_ref), channel_id=1, source_target_pairs={{0,8},{1,9},{2,10},{3,11},{4,12},{5,13},{6,14},{7,15},{8,0},{9,1},... | collective-permute-start | bytes 393224 | tf_op jit(solution)/shard_map/ppermute | solution.py:322
  37.8 0.0 copy-start.1
  37.8 0.0 copy-start.3
  37.8 1.6 %shard_map.76 = (bf16[14,224,256]{2,1,0:T(8,128)(2,1)S(1)}, f32[14,32,256]{2,1,0:T(8,128)S(1)}, f32[14,32,256]{2,1,0:T(8,128)S(1)}, f32[14,32,256]{2,1,0:T(8,128)S(1)}) custom-call(s32[1]{0:T(128)} %bitcast.8.count_ref, bf16[8,8,64,256]{3,2,1,0:T(8,128)(2,1)S(1)} %bitcast.12, bf16[320,256]{1,0:T(8,128)(2,1)S(1)} %get-tuple-element.34.text_ref), custom_call_target="tpu_custom_call" | custom-call | flops 2000000000 | bytes 2981888 | tf_op jit(solution)/shard_map/pallas_call | solution.py:310
  39.4 0.2 shard_map.77
  39.6 0.0 collective-permute-done.2.ynear_ref
  39.6 0.0 collective-permute-done.3.yfar_ref
  39.6 0.0 copy-done.1
  39.7 0.2 shard_map.78
  39.9 2.7 %collective-permute-start.4 = (bf16[256,256]{1,0:T(8,128)(2,1)S(1)}, bf16[256,256]{1,0:T(8,128)(2,1)S(1)}, u32[]{:S(2)}, u32[]{:S(2)}) collective-permute-start(bf16[256,256]{1,0:T(8,128)(2,1)S(1)} %get-tuple-element.38), channel_id=1, source_target_pairs={{0,1},{1,0},{2,3},{3,2},{4,5},{5,4},{6,7},{7,6},{8,9},{9,8},{10,11... | collective-permute-start | bytes 393224 | tf_op jit(solution)/shard_map/ppermute | solution.py:322
  42.6 1.9 %collective-permute-start.5 = (bf16[256,256]{1,0:T(8,128)(2,1)S(1)}, bf16[256,256]{1,0:T(8,128)(2,1)S(1)}, u32[]{:S(2)}, u32[]{:S(2)}) collective-permute-start(bf16[256,256]{1,0:T(8,128)(2,1)S(1)} %get-tuple-element.39), channel_id=1, source_target_pairs={{1,2},{2,1},{3,4},{4,3},{5,6},{6,5},{9,10},{10,9},{11,12},{12,11},... | collective-permute-start | bytes 393224 | tf_op jit(solution)/shard_map/ppermute | solution.py:322
  44.5 0.0 collective-permute-done.9.tile2_ref
  44.5 0.0 copy-done.3
  44.5 1.6 %shard_map.79 = (f32[16,32,256]{2,1,0:T(8,128)S(1)}, f32[16,256]{1,0:T(8,128)S(1)}, bf16[256,256]{1,0:T(8,128)(2,1)S(1)}) custom-call(s32[1]{0:T(128)} %bitcast.9.offset_ref, bf16[256,256]{1,0:T(8,128)(2,1)S(1)} %bitcast.15, bf16[256,256]{1,0:T(8,128)(2,1)S(1)} %add.3.tile1_ref, bf16[256,256]{1,0:T(8,128)(2,1)S(1)} %collective-permute-done.9.tile2_ref, ...), custom_call_target="tpu_custom_call" | custom-call | flops 2000000000 | bytes 671744 | tf_op jit(solution)/shard_map/pallas_call | solution.py:310
  46.2 1.0 %collective-permute-done.4.near_ref = bf16[256,256]{1,0:T(8,128)(2,1)S(1)} collective-permute-done((bf16[256,256]{1,0:T(8,128)(2,1)S(1)}, bf16[256,256]{1,0:T(8,128)(2,1)S(1)}, u32[]{:S(2)}, u32[]{:S(2)}) %collective-permute-start.4) | collective-permute-done | bytes 131104 | tf_op jit(solution)/shard_map/ppermute | solution.py:322
  47.2 3.6 %collective-permute-done.5.far_ref = bf16[256,256]{1,0:T(8,128)(2,1)S(1)} collective-permute-done((bf16[256,256]{1,0:T(8,128)(2,1)S(1)}, bf16[256,256]{1,0:T(8,128)(2,1)S(1)}, u32[]{:S(2)}, u32[]{:S(2)}) %collective-permute-start.5) | collective-permute-done | bytes 131104 | tf_op jit(solution)/shard_map/ppermute | solution.py:322
  50.8 1.0 %shard_map.80 = f32[32,128]{1,0:T(8,128)} custom-call(bf16[256,256]{1,0:T(8,128)(2,1)S(1)} %collective-permute-done.4.near_ref, bf16[256,256]{1,0:T(8,128)(2,1)S(1)} %collective-permute-done.5.far_ref, f32[16,32,256]{2,1,0:T(8,128)S(1)} %get-tuple-element.46.side_ref, f32[16,256]{1,0:T(8,128)S(1)} %get-tuple-element.47.d_ref, ...), custom_call_target="tpu_custom_call" | custom-call | flops 1000000 | bytes 16384 | tf_op jit(solution)/shard_map/pallas_call | solution.py:310
  (1 shorter events, 0.0 us)
Async XLA Ops:
  0.0 8.5 %copy-start.2 = (bf16[1,256,256]{2,1,0:T(8,128)(2,1)S(1)}, bf16[1,256,256]{2,1,0:T(8,128)(2,1)}, u32[]{:S(2)}) copy-start(bf16[1,256,256]{2,1,0:T(8,128)(2,1)} %param.10) | copy-start | bytes 393220
  0.0 14.2 %copy-start = (bf16[8,8,8,8,256]{4,3,2,1,0:T(8,128)(2,1)S(1)}, bf16[8,8,8,8,256]{4,3,2,1,0:T(8,128)(2,1)}, u32[]{:S(2)}) copy-start(bf16[8,8,8,8,256]{4,3,2,1,0:T(8,128)(2,1)} %param.7) | copy-start | bytes 6291460
  0.0 12.9 %collective-permute-start.7 = (bf16[256,256]{1,0:T(8,128)(2,1)}, bf16[256,256]{1,0:T(8,128)(2,1)S(1)}, u32[]{:S(2)}, u32[]{:S(2)}) collective-permute-start(bf16[256,256]{1,0:T(8,128)(2,1)} %bitcast.13), channel_id=1, source_target_pairs={{24,360},{16,280},{25,361},{17,281},{26,362},{18,282},{27,363},{19... | collective-permute-start | bytes 393224 | tf_op jit(solution)/shard_map/ppermute | solution.py:322
  2.6 11.8 %collective-permute-start = (bf16[256,256]{1,0:T(8,128)(2,1)S(1)}, bf16[256,256]{1,0:T(8,128)(2,1)S(1)}, u32[]{:S(2)}, u32[]{:S(2)}) collective-permute-start(bf16[256,256]{1,0:T(8,128)(2,1)S(1)} %get-tuple-element.28), channel_id=1, source_target_pairs={{0,32},{1,33},{2,34},{3,35},{4,36},{5,37},{6,38},{7,39},{8,40},{9,... | collective-permute-start | bytes 393224 | tf_op jit(solution)/shard_map/ppermute | solution.py:322
  6.1 10.5 %collective-permute-start.1 = (bf16[256,256]{1,0:T(8,128)(2,1)S(1)}, bf16[256,256]{1,0:T(8,128)(2,1)S(1)}, u32[]{:S(2)}, u32[]{:S(2)}) collective-permute-start(bf16[256,256]{1,0:T(8,128)(2,1)S(1)} %get-tuple-element.29), channel_id=1, source_target_pairs={{32,64},{33,65},{34,66},{35,67},{36,68},{37,69},{38,70},{39,71},{4... | collective-permute-start | bytes 393224 | tf_op jit(solution)/shard_map/ppermute | solution.py:322
  8.5 11.1 %collective-permute-start.6 = (bf16[256,256]{1,0:T(8,128)(2,1)S(1)}, bf16[256,256]{1,0:T(8,128)(2,1)S(1)}, u32[]{:S(2)}, u32[]{:S(2)}) collective-permute-start(bf16[256,256]{1,0:T(8,128)(2,1)S(1)} %bitcast.14), channel_id=1, source_target_pairs={{40,8},{41,9},{42,10},{43,11},{44,12},{45,13},{46,14},{47,15},{56,... | collective-permute-start | bytes 393224 | tf_op jit(solution)/shard_map/ppermute | solution.py:322
  12.9 6.8 %collective-permute-start.8 = (bf16[256,256]{1,0:T(8,128)(2,1)S(1)}, bf16[256,256]{1,0:T(8,128)(2,1)S(1)}, u32[]{:S(2)}, u32[]{:S(2)}) collective-permute-start(bf16[256,256]{1,0:T(8,128)(2,1)S(1)} %collective-permute-done.7), channel_id=1, source_target_pairs={{360,1000},{280,1016},{361,1001},{281,1017},{362,1002},{282,1018},... | collective-permute-start | bytes 393224 | tf_op jit(solution)/shard_map/ppermute | solution.py:322
  16.8 22.9 %collective-permute-start.2 = (bf16[256,256]{1,0:T(8,128)(2,1)S(1)}, bf16[256,256]{1,0:T(8,128)(2,1)S(1)}, u32[]{:S(2)}, u32[]{:S(2)}) collective-permute-start(bf16[256,256]{1,0:T(8,128)(2,1)S(1)} %get-tuple-element.32), channel_id=1, source_target_pairs={{0,8},{1,9},{2,10},{3,11},{4,12},{5,13},{6,14},{7,15},{8,0},{9,1},... | collective-permute-start | bytes 393224 | tf_op jit(solution)/shard_map/ppermute | solution.py:322
  19.0 20.6 %collective-permute-start.3 = (bf16[256,256]{1,0:T(8,128)(2,1)S(1)}, bf16[256,256]{1,0:T(8,128)(2,1)S(1)}, u32[]{:S(2)}, u32[]{:S(2)}) collective-permute-start(bf16[256,256]{1,0:T(8,128)(2,1)S(1)} %get-tuple-element.33), channel_id=1, source_target_pairs={{8,16},{9,17},{10,18},{11,19},{12,20},{13,21},{14,22},{15,23},{16,... | collective-permute-start | bytes 393224 | tf_op jit(solution)/shard_map/ppermute | solution.py:322
  19.7 24.8 %collective-permute-start.9 = (bf16[256,256]{1,0:T(8,128)(2,1)S(1)}, bf16[256,256]{1,0:T(8,128)(2,1)S(1)}, u32[]{:S(2)}, u32[]{:S(2)}) collective-permute-start(bf16[256,256]{1,0:T(8,128)(2,1)S(1)} %add.3.tile1_ref), channel_id=1, source_target_pairs={{0,8},{1,9},{2,10},{3,11},{4,12},{5,13},{6,14},{7,15},{8,0},{9,1},... | collective-permute-start | bytes 393224 | tf_op jit(solution)/shard_map/ppermute | solution.py:322
  37.8 1.9 %copy-start.1 = (bf16[4,32,32]{2,1,0:T(8,128)(2,1)S(1)}, bf16[4,32,32]{2,1,0:T(8,128)(2,1)}, u32[]{:S(2)}) copy-start(bf16[4,32,32]{2,1,0:T(8,128)(2,1)} %constant.7.clone.mzh_ref) | copy-start | bytes 24580
  37.8 6.8 %copy-start.3 = (bf16[2,64,32]{2,1,0:T(8,128)(2,1)S(1)}, bf16[2,64,32]{2,1,0:T(8,128)(2,1)}, u32[]{:S(2)}) copy-start(bf16[2,64,32]{2,1,0:T(8,128)(2,1)} %constant.8.clone.add_ref) | copy-start | bytes 24580
  39.9 7.3 %collective-permute-start.4 = (bf16[256,256]{1,0:T(8,128)(2,1)S(1)}, bf16[256,256]{1,0:T(8,128)(2,1)S(1)}, u32[]{:S(2)}, u32[]{:S(2)}) collective-permute-start(bf16[256,256]{1,0:T(8,128)(2,1)S(1)} %get-tuple-element.38), channel_id=1, source_target_pairs={{0,1},{1,0},{2,3},{3,2},{4,5},{5,4},{6,7},{7,6},{8,9},{9,8},{10,11... | collective-permute-start | bytes 393224 | tf_op jit(solution)/shard_map/ppermute | solution.py:322
  42.6 8.2 %collective-permute-start.5 = (bf16[256,256]{1,0:T(8,128)(2,1)S(1)}, bf16[256,256]{1,0:T(8,128)(2,1)S(1)}, u32[]{:S(2)}, u32[]{:S(2)}) collective-permute-start(bf16[256,256]{1,0:T(8,128)(2,1)S(1)} %get-tuple-element.39), channel_id=1, source_target_pairs={{1,2},{2,1},{3,4},{4,3},{5,6},{6,5},{9,10},{10,9},{11,12},{12,11},... | collective-permute-start | bytes 393224 | tf_op jit(solution)/shard_map/ppermute | solution.py:322

commit v7 on v6

--- a/solution.py
+++ b/solution.py
@@ -276,30 +276,29 @@
         d_ref[n : n + 1] = row_of(slot_sums(phi_ref[n], k_ref[...], 128))
 
 
-def finish_kernel(near_ref, far_ref, side_ref, d_ref, tile_ref, out_ref):
+def side_kernel(got_ref, side_ref, d_ref, tile_ref, out_ref, *, near):
     fine, cells = d_ref.shape
-    even = parity("gz") == 0
-    fy = near_ref.shape[0] // fine
+    last = parity("gz") == (0 if near else 1)
+    fy = got_ref.shape[0] // fine
     fz = cells // fy
-    shape = (2 * fy, cells)
-    row, lane = lax.broadcasted_iota(jnp.int32, shape, 0), lax.broadcasted_iota(jnp.int32, shape, 1)
-    mine = lane == jnp.where(row < fy, row * fz, (row - fy) * fz + fz - 1)
-    lane = lax.broadcasted_iota(jnp.int32, (1, cells), 1) % fz
-    side = (lane == 0) | (lane == fz - 1)
-    some = fine // 4
-    for part in range(4):
+    edge = jnp.where(last, fz - 1, 0)
+    row, lane = (lax.broadcasted_iota(jnp.int32, (fy, cells), axis) for axis in range(2))
+    mine = lane == row * fz + edge
+    at_edge = lax.broadcasted_iota(jnp.int32, (1, cells), 1) % fz == edge
+    some = fine // 2
+    for part in range(2):
         phi = []
         for n in range(part * some, (part + 1) * some):
-            near, far = near_ref[n * fy : (n + 1) * fy].astype(F32), far_ref[n * fy : (n + 1) * fy].astype(F32)
-            before, after = jnp.where(even, far, near), jnp.where(even, near, far)
-            phi.append((side_ref[n] + jnp.concatenate([before, after], axis=0)).astype(BF16))
+            own = jnp.where(last, side_ref[n, fy:], side_ref[n, :fy])
+            phi.append((own + got_ref[n * fy : (n + 1) * fy].astype(F32)).astype(BF16))
         sums = slot_sums(jnp.concatenate(phi, axis=0), tile_ref[...], cells)
         for i in range(some):
             n = part * some + i
-            new = jnp.sum(jnp.where(mine, sums[i * 2 * fy : (i + 1) * 2 * fy], 0.0), axis=0, keepdims=True)
-            new = jnp.where(side, new, d_ref[n : n + 1])
-            for j in range(cells // 128):
-                out_ref[n * (cells // 128) + j : n * (cells // 128) + j + 1] = new[:, j * 128 : (j + 1) * 128]
+            new = jnp.sum(jnp.where(mine, sums[i * fy : (i + 1) * fy], 0.0), axis=0, keepdims=True)
+            new = jnp.where(at_edge, new, d_ref[n : n + 1])
+            width = out_ref.shape[1]
+            for j in range(cells // width):
+                out_ref[n * (cells // width) + j : n * (cells // width) + j + 1] = new[:, j * width : (j + 1) * width]
 
 
 def call(body, outs, args, scalars=0, scratch=(), flops=1e6, hbm=()):
@@ -377,7 +376,10 @@
         [offset, own, tile1, tile2, ynear, yfar, add, mid, yside, zside, mide, ysidee, zsidee], 1, flops=2e9,
         scratch=[vmem((fx, cells, slots), BF16)],
     )
-    (out,) = call(finish_kernel, [jax.ShapeDtypeStruct((fx * cells // 128, 128), F32)], [znear, zfar, side, d, tile])
+    (d,) = call(functools.partial(side_kernel, near=True), [vmem((fx, cells), F32)], [znear, side, d, tile])
+    (out,) = call(
+        functools.partial(side_kernel, near=False), [jax.ShapeDtypeStruct((fx * cells // 128, 128), F32)], [zfar, side, d, tile]
+    )
     return out.reshape(1, 1, 1, -1)
 
 

time: 52.2 us -> 53.4 us (1.023)
  the two profiles are of different devices: /device:TPU:320 before, /device:TPU:304 now
where the time goes in v7:
time: 53.4 us; the launch traced here: 53 us
  starting transfers between devices  39.3 us (74%)
  Pallas kernels  6.63 us (12%)
  waiting for transfers between devices  5.55 us (10%)
  between operations  1.54 us (3%)
    ppermute x10, starting transfers between devices, send(): return lax.ppermute(value, AXES, pairs)  39.3 us
    pallas_call x9, Pallas kernels, call(): pl.pallas_call(body, out_shape=tuple(outs), in_specs=specs, out_specs=tup...  6.63 us
    ppermute x10, waiting for transfers between devices, send(): return lax.ppermute(value, AXES, pairs)  5.55 us
  transfers between devices with their start and end apart: 10, of which 2 were waited for; matrix products, arithmetic and copies ran while one was open for 0% of the time, Pallas kernels for 11%

profile of v7, /device:TPU:304, one launch (start us, length us, event | category | flops | bytes accessed | tf_op | source)
XLA Modules:
  0.0 53.0 jit_solution(15224360030181229378)
XLA Ops:
  0.0 0.0 copy-start.2
  0.0 0.0 copy-start
  0.0 0.8 %collective-permute-start.6 = (bf16[256,256]{1,0:T(8,128)(2,1)}, bf16[256,256]{1,0:T(8,128)(2,1)S(1)}, u32[]{:S(2)}, u32[]{:S(2)}) collective-permute-start(bf16[256,256]{1,0:T(8,128)(2,1)} %bitcast.13), channel_id=1, source_target_pairs={{24,360},{16,280},{25,361},{17,281},{26,362},{18,282},{27,363},{19... | collective-permute-start | bytes 393224 | tf_op jit(solution)/shard_map/ppermute | solution.py:321
  1.4 1.2 %shard_map.73 = (bf16[256,256]{1,0:T(8,128)(2,1)S(1)}, bf16[256,256]{1,0:T(8,128)(2,1)S(1)}, bf16[2,8,64,256]{3,2,1,0:T(8,128)(2,1)S(1)}, bf16[320,256]{1,0:T(8,128)(2,1)S(1)}) custom-call(s32[1]{0:T(128)} %bitcast.5.count_ref, bf16[8,8,64,256]{3,2,1,0:T(8,128)(2,1)} %bitcast.10, bf16[2,320,256]{2,1,0:T(8,128)(2,1)} %constant.6.clone.text_hbm), custom_call_target="tpu_custom_call" | custom-call | flops 1000000 | bytes 950272 | tf_op jit(solution)/shard_map/pallas_call | solution.py:309
  2.6 3.4 %collective-permute-start = (bf16[256,256]{1,0:T(8,128)(2,1)S(1)}, bf16[256,256]{1,0:T(8,128)(2,1)S(1)}, u32[]{:S(2)}, u32[]{:S(2)}) collective-permute-start(bf16[256,256]{1,0:T(8,128)(2,1)S(1)} %get-tuple-element.28), channel_id=1, source_target_pairs={{0,32},{1,33},{2,34},{3,35},{4,36},{5,37},{6,38},{7,39},{8,40},{9,... | collective-permute-start | bytes 393224 | tf_op jit(solution)/shard_map/ppermute | solution.py:321
  6.1 2.5 %collective-permute-start.1 = (bf16[256,256]{1,0:T(8,128)(2,1)S(1)}, bf16[256,256]{1,0:T(8,128)(2,1)S(1)}, u32[]{:S(2)}, u32[]{:S(2)}) collective-permute-start(bf16[256,256]{1,0:T(8,128)(2,1)S(1)} %get-tuple-element.29), channel_id=1, source_target_pairs={{32,64},{33,65},{34,66},{35,67},{36,68},{37,69},{38,70},{39,71},{4... | collective-permute-start | bytes 393224 | tf_op jit(solution)/shard_map/ppermute | solution.py:321
  8.5 0.0 copy-done.2
  8.5 4.3 %collective-permute-start.5 = (bf16[256,256]{1,0:T(8,128)(2,1)S(1)}, bf16[256,256]{1,0:T(8,128)(2,1)S(1)}, u32[]{:S(2)}, u32[]{:S(2)}) collective-permute-start(bf16[256,256]{1,0:T(8,128)(2,1)S(1)} %bitcast.14), channel_id=1, source_target_pairs={{40,8},{41,9},{42,10},{43,11},{44,12},{45,13},{46,14},{47,15},{56,... | collective-permute-start | bytes 393224 | tf_op jit(solution)/shard_map/ppermute | solution.py:321
  12.9 0.0 collective-permute-done.6
  12.9 0.7 %collective-permute-start.7 = (bf16[256,256]{1,0:T(8,128)(2,1)S(1)}, bf16[256,256]{1,0:T(8,128)(2,1)S(1)}, u32[]{:S(2)}, u32[]{:S(2)}) collective-permute-start(bf16[256,256]{1,0:T(8,128)(2,1)S(1)} %collective-permute-done.6), channel_id=1, source_target_pairs={{360,1000},{280,1016},{361,1001},{281,1017},{362,1002},{282,1018},... | collective-permute-start | bytes 393224 | tf_op jit(solution)/shard_map/ppermute | solution.py:321
  14.2 0.0 copy-done
  14.2 0.2 shard_map.74
  14.5 0.0 collective-permute-done.near_ref
  14.5 2.1 %collective-permute-done.1.far_ref = bf16[256,256]{1,0:T(8,128)(2,1)S(1)} collective-permute-done((bf16[256,256]{1,0:T(8,128)(2,1)S(1)}, bf16[256,256]{1,0:T(8,128)(2,1)S(1)}, u32[]{:S(2)}, u32[]{:S(2)}) %collective-permute-start.1) | collective-permute-done | bytes 131104 | tf_op jit(solution)/shard_map/ppermute | solution.py:321
  16.6 0.2 shard_map.75
  16.8 2.2 %collective-permute-start.2 = (bf16[256,256]{1,0:T(8,128)(2,1)S(1)}, bf16[256,256]{1,0:T(8,128)(2,1)S(1)}, u32[]{:S(2)}, u32[]{:S(2)}) collective-permute-start(bf16[256,256]{1,0:T(8,128)(2,1)S(1)} %get-tuple-element.32), channel_id=1, source_target_pairs={{0,8},{1,9},{2,10},{3,11},{4,12},{5,13},{6,14},{7,15},{8,0},{9,1},... | collective-permute-start | bytes 393224 | tf_op jit(solution)/shard_map/ppermute | solution.py:321
  19.0 0.7 %collective-permute-start.3 = (bf16[256,256]{1,0:T(8,128)(2,1)S(1)}, bf16[256,256]{1,0:T(8,128)(2,1)S(1)}, u32[]{:S(2)}, u32[]{:S(2)}) collective-permute-start(bf16[256,256]{1,0:T(8,128)(2,1)S(1)} %get-tuple-element.33), channel_id=1, source_target_pairs={{8,16},{9,17},{10,18},{11,19},{12,20},{13,21},{14,22},{15,23},{16,... | collective-permute-start | bytes 393224 | tf_op jit(solution)/shard_map/ppermute | solution.py:321
  19.7 0.0 collective-permute-done.5
  19.7 0.0 collective-permute-done.7
  19.7 18.0 %collective-permute-start.8 = (bf16[256,256]{1,0:T(8,128)(2,1)S(1)}, bf16[256,256]{1,0:T(8,128)(2,1)S(1)}, u32[]{:S(2)}, u32[]{:S(2)}) collective-permute-start(bf16[256,256]{1,0:T(8,128)(2,1)S(1)} %add.3.tile1_ref), channel_id=1, source_target_pairs={{0,8},{1,9},{2,10},{3,11},{4,12},{5,13},{6,14},{7,15},{8,0},{9,1},... | collective-permute-start | bytes 393224 | tf_op jit(solution)/shard_map/ppermute | solution.py:321
  37.8 0.0 copy-start.1
  37.8 0.0 copy-start.3
  37.8 1.6 %shard_map.76 = (bf16[14,224,256]{2,1,0:T(8,128)(2,1)S(1)}, f32[14,32,256]{2,1,0:T(8,128)S(1)}, f32[14,32,256]{2,1,0:T(8,128)S(1)}, f32[14,32,256]{2,1,0:T(8,128)S(1)}) custom-call(s32[1]{0:T(128)} %bitcast.8.count_ref, bf16[8,8,64,256]{3,2,1,0:T(8,128)(2,1)S(1)} %bitcast.12, bf16[320,256]{1,0:T(8,128)(2,1)S(1)} %get-tuple-element.34.text_ref), custom_call_target="tpu_custom_call" | custom-call | flops 2000000000 | bytes 2981888 | tf_op jit(solution)/shard_map/pallas_call | solution.py:309
  39.4 0.2 shard_map.77
  39.6 0.0 collective-permute-done.2.ynear_ref
  39.6 0.0 collective-permute-done.3.yfar_ref
  39.7 0.0 copy-done.1
  39.7 0.2 shard_map.78
  39.9 4.8 %collective-permute-start.4 = (bf16[256,256]{1,0:T(8,128)(2,1)S(1)}, bf16[256,256]{1,0:T(8,128)(2,1)S(1)}, u32[]{:S(2)}, u32[]{:S(2)}) collective-permute-start(bf16[256,256]{1,0:T(8,128)(2,1)S(1)} %get-tuple-element.38), channel_id=1, source_target_pairs={{1,2},{2,1},{3,4},{4,3},{5,6},{6,5},{9,10},{10,9},{11,12},{12,11},... | collective-permute-start | bytes 393224 | tf_op jit(solution)/shard_map/ppermute | solution.py:321
  44.7 1.9 %collective-permute-start.9 = (bf16[256,256]{1,0:T(8,128)(2,1)S(1)}, bf16[256,256]{1,0:T(8,128)(2,1)S(1)}, u32[]{:S(2)}, u32[]{:S(2)}) collective-permute-start(bf16[256,256]{1,0:T(8,128)(2,1)S(1)} %get-tuple-element.46), channel_id=1, source_target_pairs={{0,1},{1,0},{2,3},{3,2},{4,5},{5,4},{6,7},{7,6},{8,9},{9,8},{10,11... | collective-permute-start | bytes 393224 | tf_op jit(solution)/shard_map/ppermute | solution.py:321
  46.6 0.0 collective-permute-done.8.tile2_ref
  46.6 0.0 copy-done.3
  46.6 1.6 %shard_map.79 = (f32[16,32,256]{2,1,0:T(8,128)S(1)}, f32[16,256]{1,0:T(8,128)S(1)}, bf16[256,256]{1,0:T(8,128)(2,1)S(1)}) custom-call(s32[1]{0:T(128)} %bitcast.9.offset_ref, bf16[256,256]{1,0:T(8,128)(2,1)S(1)} %bitcast.15, bf16[256,256]{1,0:T(8,128)(2,1)S(1)} %add.3.tile1_ref, bf16[256,256]{1,0:T(8,128)(2,1)S(1)} %collective-permute-done.8.tile2_ref, ...), custom_call_target="tpu_custom_call" | custom-call | flops 2000000000 | bytes 671744 | tf_op jit(solution)/shard_map/pallas_call | solution.py:309
  48.3 3.4 %collective-permute-done.9.got_ref = bf16[256,256]{1,0:T(8,128)(2,1)S(1)} collective-permute-done((bf16[256,256]{1,0:T(8,128)(2,1)S(1)}, bf16[256,256]{1,0:T(8,128)(2,1)S(1)}, u32[]{:S(2)}, u32[]{:S(2)}) %collective-permute-start.9) | collective-permute-done | bytes 131104 | tf_op jit(solution)/shard_map/ppermute | solution.py:321
  51.7 0.3 shard_map.80.d_ref
  52.1 0.0 collective-permute-done.4.got_ref
  52.1 1.0 %shard_map.81 = f32[32,128]{1,0:T(8,128)} custom-call(bf16[256,256]{1,0:T(8,128)(2,1)S(1)} %collective-permute-done.4.got_ref, f32[16,32,256]{2,1,0:T(8,128)S(1)} %get-tuple-element.45.side_ref, f32[16,256]{1,0:T(8,128)S(1)} %shard_map.80.d_ref, bf16[256,256]{1,0:T(8,128)(2,1)S(1)} %get-tuple-element.48.tile_ref), custom_call_target="tpu_custom_call" | custom-call | flops 1000000 | bytes 16384 | tf_op jit(solution)/shard_map/pallas_call | solution.py:309
  (1 shorter events, 0.0 us)
Async XLA Ops:
  0.0 8.5 %copy-start.2 = (bf16[1,256,256]{2,1,0:T(8,128)(2,1)S(1)}, bf16[1,256,256]{2,1,0:T(8,128)(2,1)}, u32[]{:S(2)}) copy-start(bf16[1,256,256]{2,1,0:T(8,128)(2,1)} %param.10) | copy-start | bytes 393220
  0.0 14.2 %copy-start = (bf16[8,8,8,8,256]{4,3,2,1,0:T(8,128)(2,1)S(1)}, bf16[8,8,8,8,256]{4,3,2,1,0:T(8,128)(2,1)}, u32[]{:S(2)}) copy-start(bf16[8,8,8,8,256]{4,3,2,1,0:T(8,128)(2,1)} %param.7) | copy-start | bytes 6291460
  0.0 12.9 %collective-permute-start.6 = (bf16[256,256]{1,0:T(8,128)(2,1)}, bf16[256,256]{1,0:T(8,128)(2,1)S(1)}, u32[]{:S(2)}, u32[]{:S(2)}) collective-permute-start(bf16[256,256]{1,0:T(8,128)(2,1)} %bitcast.13), channel_id=1, source_target_pairs={{24,360},{16,280},{25,361},{17,281},{26,362},{18,282},{27,363},{19... | collective-permute-start | bytes 393224 | tf_op jit(solution)/shard_map/ppermute | solution.py:321
  2.6 11.8 %collective-permute-start = (bf16[256,256]{1,0:T(8,128)(2,1)S(1)}, bf16[256,256]{1,0:T(8,128)(2,1)S(1)}, u32[]{:S(2)}, u32[]{:S(2)}) collective-permute-start(bf16[256,256]{1,0:T(8,128)(2,1)S(1)} %get-tuple-element.28), channel_id=1, source_target_pairs={{0,32},{1,33},{2,34},{3,35},{4,36},{5,37},{6,38},{7,39},{8,40},{9,... | collective-permute-start | bytes 393224 | tf_op jit(solution)/shard_map/ppermute | solution.py:321
  6.1 10.5 %collective-permute-start.1 = (bf16[256,256]{1,0:T(8,128)(2,1)S(1)}, bf16[256,256]{1,0:T(8,128)(2,1)S(1)}, u32[]{:S(2)}, u32[]{:S(2)}) collective-permute-start(bf16[256,256]{1,0:T(8,128)(2,1)S(1)} %get-tuple-element.29), channel_id=1, source_target_pairs={{32,64},{33,65},{34,66},{35,67},{36,68},{37,69},{38,70},{39,71},{4... | collective-permute-start | bytes 393224 | tf_op jit(solution)/shard_map/ppermute | solution.py:321
  8.5 11.1 %collective-permute-start.5 = (bf16[256,256]{1,0:T(8,128)(2,1)S(1)}, bf16[256,256]{1,0:T(8,128)(2,1)S(1)}, u32[]{:S(2)}, u32[]{:S(2)}) collective-permute-start(bf16[256,256]{1,0:T(8,128)(2,1)S(1)} %bitcast.14), channel_id=1, source_target_pairs={{40,8},{41,9},{42,10},{43,11},{44,12},{45,13},{46,14},{47,15},{56,... | collective-permute-start | bytes 393224 | tf_op jit(solution)/shard_map/ppermute | solution.py:321
  12.9 6.8 %collective-permute-start.7 = (bf16[256,256]{1,0:T(8,128)(2,1)S(1)}, bf16[256,256]{1,0:T(8,128)(2,1)S(1)}, u32[]{:S(2)}, u32[]{:S(2)}) collective-permute-start(bf16[256,256]{1,0:T(8,128)(2,1)S(1)} %collective-permute-done.6), channel_id=1, source_target_pairs={{360,1000},{280,1016},{361,1001},{281,1017},{362,1002},{282,1018},... | collective-permute-start | bytes 393224 | tf_op jit(solution)/shard_map/ppermute | solution.py:321
  16.8 22.9 %collective-permute-start.2 = (bf16[256,256]{1,0:T(8,128)(2,1)S(1)}, bf16[256,256]{1,0:T(8,128)(2,1)S(1)}, u32[]{:S(2)}, u32[]{:S(2)}) collective-permute-start(bf16[256,256]{1,0:T(8,128)(2,1)S(1)} %get-tuple-element.32), channel_id=1, source_target_pairs={{0,8},{1,9},{2,10},{3,11},{4,12},{5,13},{6,14},{7,15},{8,0},{9,1},... | collective-permute-start | bytes 393224 | tf_op jit(solution)/shard_map/ppermute | solution.py:321
  19.0 20.7 %collective-permute-start.3 = (bf16[256,256]{1,0:T(8,128)(2,1)S(1)}, bf16[256,256]{1,0:T(8,128)(2,1)S(1)}, u32[]{:S(2)}, u32[]{:S(2)}) collective-permute-start(bf16[256,256]{1,0:T(8,128)(2,1)S(1)} %get-tuple-element.33), channel_id=1, source_target_pairs={{8,16},{9,17},{10,18},{11,19},{12,20},{13,21},{14,22},{15,23},{16,... | collective-permute-start | bytes 393224 | tf_op jit(solution)/shard_map/ppermute | solution.py:321
  19.7 26.9 %collective-permute-start.8 = (bf16[256,256]{1,0:T(8,128)(2,1)S(1)}, bf16[256,256]{1,0:T(8,128)(2,1)S(1)}, u32[]{:S(2)}, u32[]{:S(2)}) collective-permute-start(bf16[256,256]{1,0:T(8,128)(2,1)S(1)} %add.3.tile1_ref), channel_id=1, source_target_pairs={{0,8},{1,9},{2,10},{3,11},{4,12},{5,13},{6,14},{7,15},{8,0},{9,1},... | collective-permute-start | bytes 393224 | tf_op jit(solution)/shard_map/ppermute | solution.py:321
  37.8 1.9 %copy-start.1 = (bf16[4,32,32]{2,1,0:T(8,128)(2,1)S(1)}, bf16[4,32,32]{2,1,0:T(8,128)(2,1)}, u32[]{:S(2)}) copy-start(bf16[4,32,32]{2,1,0:T(8,128)(2,1)} %constant.7.clone.mzh_ref) | copy-start | bytes 24580
  37.8 8.9 %copy-start.3 = (bf16[2,64,32]{2,1,0:T(8,128)(2,1)S(1)}, bf16[2,64,32]{2,1,0:T(8,128)(2,1)}, u32[]{:S(2)}) copy-start(bf16[2,64,32]{2,1,0:T(8,128)(2,1)} %constant.8.clone.add_ref) | copy-start | bytes 24580
  39.9 12.2 %collective-permute-start.4 = (bf16[256,256]{1,0:T(8,128)(2,1)S(1)}, bf16[256,256]{1,0:T(8,128)(2,1)S(1)}, u32[]{:S(2)}, u32[]{:S(2)}) collective-permute-start(bf16[256,256]{1,0:T(8,128)(2,1)S(1)} %get-tuple-element.38), channel_id=1, source_target_pairs={{1,2},{2,1},{3,4},{4,3},{5,6},{6,5},{9,10},{10,9},{11,12},{12,11},... | collective-permute-start | bytes 393224 | tf_op jit(solution)/shard_map/ppermute | solution.py:321
  44.7 7.0 %collective-permute-start.9 = (bf16[256,256]{1,0:T(8,128)(2,1)S(1)}, bf16[256,256]{1,0:T(8,128)(2,1)S(1)}, u32[]{:S(2)}, u32[]{:S(2)}) collective-permute-start(bf16[256,256]{1,0:T(8,128)(2,1)S(1)} %get-tuple-element.46), channel_id=1, source_target_pairs={{0,1},{1,0},{2,3},{3,2},{4,5},{5,4},{6,7},{7,6},{8,9},{9,8},{10,11... | collective-permute-start | bytes 393224 | tf_op jit(solution)/shard_map/ppermute | solution.py:321
